TPU v7x, 32 devices: a whole 2x2x4 slice. The times are simulated.
32 devices in a mesh: gx: 2 (over x), gy: 4 (over z), gz: 4 (over y, core).
Axes of the slice: x: 2, y: 2, z: 4, core: 2. Of those that a mesh axis runs over, the one named last changes fastest.
Arguments:
- source_field: float32 [3, 16, 32, 512], P(None, 'gx', 'gy', 'gz'), may hold values from -6 to 6
- cell_contrast: bfloat16 [4096, 1536], P(('gx', 'gy', 'gz')), may hold values from 0.19921875 to 2
- point_field: bfloat16 [3, 4096], P(None, ('gx', 'gy', 'gz')), may hold values from -3 to 3
- point_class: int32 [4096, 1], P(('gx', 'gy', 'gz')), may hold values from 0 to 1; in each aligned block of 128 rows (0 to 127, 128 to 255, ...) at most 128 rows name the same one
- cell_kind: int32 [4096], P(('gx', 'gy', 'gz')), may hold values from 0 to 3
- inverse_blocks: float32 [2, 4, 3, 3, 512], P('gx'), may hold values from -0.3 to 0.3
Outputs:
- newton_step: float32 [3, 16, 32, 512], P(None, 'gx', 'gy', 'gz')
- krylov_residual: float32 [3, 16, 32, 512], P(None, 'gx', 'gy', 'gz')
Inputs may be any that keep to these rules, and one draw needn't show every extreme that they name: `point_class`: among the 128 points of one device's block no class is named more than 128 times, a bound that some block reaches there.
All inputs are finite; a program needn't handle non-finite values.
Results may differ from a plain program's by a relative error of at most 0.0076.
Values may be sent and summed in bfloat16 or wider, within the bound.
No kernel may reach another device: no remote copies, remote signals or barrier semaphores. Data moves between devices by JAX's collectives and lax.ppermute only.
A program may use at most 64 MiB of HBM per device.

v0:
```python
import math

import jax
import jax.numpy as jnp
from jax import lax
from jax.sharding import PartitionSpec as P

CELL = 8
VOX = 512
TYPES = 4
ZP = 8
ITERS = 3


kerr_scale = 0.1


def with_halo(block, sides, width):
    for axis, dim in sides:
        count = lax.axis_size(axis)
        forward = [(i, i + 1) for i in range(count - 1)]
        backward = [(target, source) for source, target in forward]
        low = lax.ppermute(
            lax.slice_in_dim(block, block.shape[dim] - width, None, axis=dim), axis, forward
        )
        high = lax.ppermute(lax.slice_in_dim(block, 0, width, axis=dim), axis, backward)
        block = jnp.concatenate([low, block, high], axis=dim)
    return block


def hartley_table():
    voxel_index = jnp.arange(VOX, dtype=jnp.int32)
    along_one = voxel_index // (CELL * CELL)
    along_two = voxel_index // CELL % CELL
    along_three = voxel_index % CELL
    phase_index = (
        along_one[:, None] * along_one[None, :]
        + along_two[:, None] * along_two[None, :]
        + along_three[:, None] * along_three[None, :]
    ) % CELL
    phase_angle = 2.0 * math.pi / CELL * phase_index.astype(jnp.float32)
    return ((jnp.cos(phase_angle) + jnp.sin(phase_angle)) / math.sqrt(VOX)).astype(jnp.bfloat16)


def cell_solve(contrast, point_values, blocks, hartley):
    row_count = contrast.shape[0]
    weights = contrast.reshape(row_count, 3, VOX).astype(jnp.float32)
    base_field = point_values.astype(jnp.float32)[:, :, None]

    def correction(polarization):
        spectrum = jnp.dot(
            polarization.reshape(row_count * 3, VOX), hartley, preferred_element_type=jnp.float32
        ).reshape(row_count, 3, VOX)
        mixed_spectrum = jnp.sum(blocks * spectrum[:, None, :, :], axis=2).astype(jnp.bfloat16)
        return jnp.dot(
            mixed_spectrum.reshape(row_count * 3, VOX), hartley, preferred_element_type=jnp.float32
        ).reshape(row_count, 3, VOX)

    local_field = base_field - correction((weights * base_field).astype(jnp.bfloat16))
    kerr_polar = (weights * local_field * (1.0 + kerr_scale * local_field * local_field)).astype(
        jnp.bfloat16
    )
    final_field = base_field - correction(kerr_polar)
    flux_mean = jnp.mean((1.0 + weights) * final_field, axis=2)
    stiffness = 0.5 + jnp.mean(weights * final_field * final_field, axis=(1, 2))
    return jnp.concatenate([flux_mean, stiffness[:, None]], axis=1)


def solve_batched(contrast, point_values, keys, library, hartley):
    return cell_solve(contrast, point_values, library[keys], hartley)


def operate(field, diagonal):
    padded = with_halo(field, (("gx", 1), ("gy", 2), ("gz", 3)), 1)
    beside = padded[:, 2:, 1:-1, 1:-1] + padded[:, :-2, 1:-1, 1:-1]
    beside = beside + padded[:, 1:-1, 2:, 1:-1] + padded[:, 1:-1, :-2, 1:-1]
    beside = beside + padded[:, 1:-1, 1:-1, 2:] + padded[:, 1:-1, 1:-1, :-2]
    return (6.0 + diagonal)[None] * field - beside


def two_products(residual, image):
    return lax.psum((jnp.sum(residual * residual), jnp.sum(residual * image)), ("gx", "gy", "gz"))


def per_device(source_field, cell_contrast, point_field, point_class, cell_kind, inverse_blocks):
    hartley = hartley_table()
    point_values = point_field.T
    library = lax.all_gather(inverse_blocks, "gx", axis=0, tiled=True)
    library = library.reshape(library.shape[0] * library.shape[1], 3, 3, VOX)
    chosen = point_class[:, 0] * TYPES + cell_kind
    summary = solve_batched(cell_contrast, point_values, chosen, library, hartley)
    extent_x = source_field.shape[1]
    extent_y = source_field.shape[2]
    extent_z = source_field.shape[3]
    blocks_z = extent_z // ZP
    stiffness_grid = jnp.broadcast_to(
        summary[:, 3].reshape(1, extent_y, blocks_z, 1), (extent_x, extent_y, blocks_z, ZP)
    ).reshape(extent_x, extent_y, extent_z)
    flux_grid = jnp.broadcast_to(
        summary[:, :3].T.reshape(3, 1, extent_y, blocks_z, 1), (3, extent_x, extent_y, blocks_z, ZP)
    ).reshape(3, extent_x, extent_y, extent_z)
    right = source_field - flux_grid
    newton_step = jnp.zeros_like(right)
    residual = right
    image = operate(residual, stiffness_grid)
    norm_now, product = two_products(residual, image)
    alpha = norm_now / product
    direction, along = (residual, image)
    for iteration in range(ITERS):
        newton_step = newton_step + alpha * direction
        residual = residual - alpha * along
        if iteration + 1 < ITERS:
            image = operate(residual, stiffness_grid)
            norm_next, product = two_products(residual, image)
            ratio = norm_next / norm_now
            alpha = norm_next / (product - ratio * norm_next / alpha)
            direction = residual + ratio * direction
            along = image + ratio * along
            norm_now = norm_next
    return (newton_step, residual)


def solution(mesh):
    placed = (
        P(None, "gx", "gy", "gz"),
        P(("gx", "gy", "gz"), None),
        P(None, ("gx", "gy", "gz")),
        P(("gx", "gy", "gz"), None),
        P(("gx", "gy", "gz")),
        P("gx", None, None, None, None),
    )
    return jax.shard_map(
        per_device,
        mesh=mesh,
        in_specs=placed,
        out_specs=(P(None, "gx", "gy", "gz"), P(None, "gx", "gy", "gz")),
        check_vma=False,
    )
```

profile of v0, /device:TPU:0, one launch (start us, length us, event | category | flops | bytes accessed | tf_op | source)
XLA Modules:
  0.0 260.3 jit_solution(5146362177927208598)
XLA Ops:
  0.7 0.7 convert_bitcast_fusion
  1.3 0.7 compare_select_fusion
  2.0 6.2 %all_gather.3 = f32[2,4,3,3,512]{4,1,3,2,0:T(4,128)S(1)} all-gather(f32[1,4,3,3,512]{4,1,3,2,0:T(4,128)} %param.11), channel_id=1, replica_groups=mesh['gx'=2,'gy'=4,'gz'=4] {'gx'}, dimensions={0}, use_global_device_ids=true | all-gather | bytes 221184 | tf_op jit(solution)/shard_map/all_gather | solution.py:88
  8.2 0.1 copy.45
  8.3 1.2 copy.34
  9.6 0.2 copy.35
  9.8 4.7 %fusion.12 = f32[128,3,512]{2,0,1:T(8,128)S(1)} fusion(s32[512]{0:T(512)S(1)} %get-tuple-element.39, s32[512]{0:T(512)S(1)} %get-tuple-element.40, s32[512]{0:T(512)S(1)} %add_select_fusion.4, f32[128,3,512]{2,0,1:T(8,128)S(1)} %copy.35, f32[128,3]{0,1:T(4,128)S(1)} %convert_bitcast_fusion), kind=kOutput, calls=%fused_computation.24 | convolution fusion | flops 207224832 | bytes 1580544 | tf_op jit(solution)/shard_map/dot_general | solution.py:51
  14.5 1.5 copy.39
  16.0 2.4 gather_fusion
  18.5 4.6 %multiply_reduce_fusion.1 = bf16[128,3,512]{2,1,0:T(4,128)(2,1)} fusion(f32[128,3,3,512]{3,2,1,0:T(4,128)S(1)} %gather_fusion, f32[128,3,512]{2,1,0:T(4,128)} %copy.39), kind=kLoop, calls=%fused_computation.2 | loop fusion | flops 983040 | bytes 3538944 | tf_op jit(solution)/shard_map/reduce_sum | solution.py:54
  23.1 11.6 %fusion.7 = f32[128,3,512]{2,0,1:T(8,128)} fusion(f32[128,3,512]{2,0,1:T(8,128)} %copy-done.1, s32[512]{0:T(512)S(1)} %get-tuple-element.39, s32[512]{0:T(512)S(1)} %get-tuple-element.40, s32[512]{0:T(512)S(1)} %add_select_fusion.4, bf16[128,3,512]{2,1,0:T(4,128)(2,1)} %multiply_reduce_fusion.1, f32[128,3]{0,1:T(4,128)S(1)} %convert_bitcast_fusion), kind=kOutput, calls=%fused_computation.21 | convolution fusion | flops 415039488 | bytes 1973760 | tf_op jit(solution)/shard_map/dot_general | solution.py:51
  34.7 1.7 copy.42
  36.5 3.5 %multiply_reduce_fusion = bf16[128,3,512]{2,1,0:T(4,128)(2,1)S(1)} fusion(f32[128,3,3,512]{3,2,1,0:T(4,128)S(1)} %gather_fusion, f32[128,3,512]{2,1,0:T(4,128)S(1)} %copy.42), kind=kLoop, calls=%fused_computation.1 | loop fusion | flops 983040 | bytes 3538944 | tf_op jit(solution)/shard_map/reduce_sum | solution.py:54
  39.9 5.2 %fusion.6 = (f32[128]{0:T(128)S(1)}, f32[128,3]{0,1:T(4,128)S(1)}) fusion(f32[128,3,512]{2,0,1:T(8,128)S(1)} %copy-done.2, s32[512]{0:T(512)S(1)} %get-tuple-element.39, s32[512]{0:T(512)S(1)} %get-tuple-element.40, s32[512]{0:T(512)S(1)} %add_select_fusion.4, bf16[128,3,512]{2,1,0:T(4,128)(2,1)S(1)} %multiply_reduce_fusion, ...), kind=kOutput, calls=%fused_computation.17 | convolution fusion | flops 208207360 | bytes 1189376 | tf_op jit(solution)/shard_map/dot_general | solution.py:55
  45.1 0.1 broadcast_in_dim.13
  45.2 0.1 broadcast_in_dim.14
  45.3 0.1 broadcast_in_dim.15
  45.5 3.9 %collective-permute-start.1 = (f32[3,1,8,128]{3,2,1,0:T(8,128)S(1)}, f32[3,1,8,128]{3,2,1,0:T(8,128)S(1)}, u32[]{:S(2)}, u32[]{:S(2)}) collective-permute-start(f32[3,1,8,128]{3,2,1,0:T(8,128)S(1)} %get-tuple-element.37), channel_id=1, source_target_pairs={{0,16},{1,17},{2,18},{3,19},{4,20},{5,21},{6,22},{7,23},{8,24},{9,... | collective-permute-start | bytes 36872 | tf_op jit(solution)/shard_map/ppermute | solution.py:23
  49.4 1.3 collective-permute-start
  50.7 0.1 collective-permute-done.1
  50.8 4.2 %collective-permute-done = f32[3,1,8,128]{3,2,1,0:T(8,128)S(1)} collective-permute-done((f32[3,1,8,128]{3,2,1,0:T(8,128)S(1)}, f32[3,1,8,128]{3,2,1,0:T(8,128)S(1)}, u32[]{:S(2)}, u32[]{:S(2)}) %collective-permute-start) | collective-permute-done | bytes 12320 | tf_op jit(solution)/shard_map/ppermute | solution.py:26
  55.0 3.5 %collective-permute-start.3 = (f32[3,10,1,128]{3,2,1,0:T(1,128)S(1)}, f32[3,10,1,128]{3,2,1,0:T(1,128)S(1)}, u32[]{:S(2)}, u32[]{:S(2)}) collective-permute-start(f32[3,10,1,128]{3,2,1,0:T(1,128)S(1)} %get-tuple-element.29), channel_id=1, source_target_pairs={{0,4},{4,8},{8,12},{1,5},{5,9},{9,13},{2,6},{6,10},{10,14},{3,7},{... | collective-permute-start | bytes 46088 | tf_op jit(solution)/shard_map/ppermute | solution.py:23
  58.5 1.3 collective-permute-start.2
  59.8 0.1 collective-permute-done.3
  59.9 4.2 %collective-permute-done.2 = f32[3,10,1,128]{3,2,1,0:T(1,128)S(1)} collective-permute-done((f32[3,10,1,128]{3,2,1,0:T(1,128)S(1)}, f32[3,10,1,128]{3,2,1,0:T(1,128)S(1)}, u32[]{:S(2)}, u32[]{:S(2)}) %collective-permute-start.2) | collective-permute-done | bytes 15392 | tf_op jit(solution)/shard_map/ppermute | solution.py:26
  64.1 0.1 pad_maximum_fusion
  64.1 0.1 fusion.70
  64.3 1.3 collective-permute-start.4
  65.6 3.0 %collective-permute-start.5 = (f32[3,10,10,1]{3,2,1,0:T(8,128)S(1)}, f32[3,10,10,1]{3,2,1,0:T(8,128)S(1)}, u32[]{:S(2)}, u32[]{:S(2)}) collective-permute-start(f32[3,10,10,1]{3,2,1,0:T(8,128)S(1)} %get-tuple-element.24), channel_id=1, source_target_pairs={{0,1},{1,2},{2,3},{4,5},{5,6},{6,7},{8,9},{9,10},{10,11},{12,13},{... | collective-permute-start | bytes 3608 | tf_op jit(solution)/shard_map/ppermute | solution.py:23
  68.6 0.1 add.222
  68.7 0.1 broadcast_in_dim.34
  68.8 0.1 add.223
  68.9 0.8 collective-permute-done.5
  69.7 0.8 multiply_reduce_fusion.7
  70.5 43.3 %all-reduce.2 = (f32[]{:T(128)}, f32[]{:T(128)}) all-reduce(f32[]{:T(128)} %get-tuple-element.9, f32[]{:T(128)} %get-tuple-element.8), channel_id=1, replica_groups=mesh['gx'=2,'gy'=4,'gz'=4] {'gx','gy','gz'}, use_global_device_ids=true, to_apply=%region_4.5 | all-reduce | flops 2 | bytes 16 | tf_op jit(solution)/shard_map/psum | solution.py:82
  115.2 4.2 %collective-permute-start.7 = (f32[3,1,8,128]{3,2,1,0:T(8,128)S(1)}, f32[3,1,8,128]{3,2,1,0:T(8,128)S(1)}, u32[]{:S(2)}, u32[]{:S(2)}) collective-permute-start(f32[3,1,8,128]{3,2,1,0:T(8,128)S(1)} %get-tuple-element.35), channel_id=1, source_target_pairs={{0,16},{1,17},{2,18},{3,19},{4,20},{5,21},{6,22},{7,23},{8,24},{9,... | collective-permute-start | bytes 36872 | tf_op jit(solution)/shard_map/ppermute | solution.py:23
  119.4 1.3 collective-permute-start.6
  120.7 0.1 collective-permute-done.7
  120.7 4.2 %collective-permute-done.6 = f32[3,1,8,128]{3,2,1,0:T(8,128)S(1)} collective-permute-done((f32[3,1,8,128]{3,2,1,0:T(8,128)S(1)}, f32[3,1,8,128]{3,2,1,0:T(8,128)S(1)}, u32[]{:S(2)}, u32[]{:S(2)}) %collective-permute-start.6) | collective-permute-done | bytes 12320 | tf_op jit(solution)/shard_map/ppermute | solution.py:26
  125.0 2.1 collective-permute-start.9
  127.1 1.3 collective-permute-start.8
  128.4 0.1 collective-permute-done.9
  128.5 4.2 %collective-permute-done.8 = f32[3,10,1,128]{3,2,1,0:T(1,128)S(1)} collective-permute-done((f32[3,10,1,128]{3,2,1,0:T(1,128)S(1)}, f32[3,10,1,128]{3,2,1,0:T(1,128)S(1)}, u32[]{:S(2)}, u32[]{:S(2)}) %collective-permute-start.8) | collective-permute-done | bytes 15392 | tf_op jit(solution)/shard_map/ppermute | solution.py:26
  132.7 0.1 fusion.69
  132.9 1.3 collective-permute-start.10
  134.2 3.0 %collective-permute-start.11 = (f32[3,10,10,1]{3,2,1,0:T(8,128)S(1)}, f32[3,10,10,1]{3,2,1,0:T(8,128)S(1)}, u32[]{:S(2)}, u32[]{:S(2)}) collective-permute-start(f32[3,10,10,1]{3,2,1,0:T(8,128)S(1)} %get-tuple-element.22), channel_id=1, source_target_pairs={{0,1},{1,2},{2,3},{4,5},{5,6},{6,7},{8,9},{9,10},{10,11},{12,13},{... | collective-permute-start | bytes 3608 | tf_op jit(solution)/shard_map/ppermute | solution.py:23
  137.2 1.1 collective-permute-done.11
  138.3 0.8 multiply_reduce_fusion.5
  139.2 43.9 %all-reduce.1 = (f32[]{:T(128)}, f32[]{:T(128)}) all-reduce(f32[]{:T(128)} %get-tuple-element.7, f32[]{:T(128)} %get-tuple-element.6), channel_id=1, replica_groups=mesh['gx'=2,'gy'=4,'gz'=4] {'gx','gy','gz'}, use_global_device_ids=true, to_apply=%region_9.10 | all-reduce | flops 2 | bytes 16 | tf_op jit(solution)/shard_map/psum | solution.py:82
  187.6 4.2 %collective-permute-start.13 = (f32[3,1,8,128]{3,2,1,0:T(8,128)S(1)}, f32[3,1,8,128]{3,2,1,0:T(8,128)S(1)}, u32[]{:S(2)}, u32[]{:S(2)}) collective-permute-start(f32[3,1,8,128]{3,2,1,0:T(8,128)S(1)} %get-tuple-element.33), channel_id=1, source_target_pairs={{0,16},{1,17},{2,18},{3,19},{4,20},{5,21},{6,22},{7,23},{8,24},{9,... | collective-permute-start | bytes 36872 | tf_op jit(solution)/shard_map/ppermute | solution.py:23
  191.8 1.3 collective-permute-start.12
  193.1 0.1 collective-permute-done.13
  193.2 4.2 %collective-permute-done.12 = f32[3,1,8,128]{3,2,1,0:T(8,128)S(1)} collective-permute-done((f32[3,1,8,128]{3,2,1,0:T(8,128)S(1)}, f32[3,1,8,128]{3,2,1,0:T(8,128)S(1)}, u32[]{:S(2)}, u32[]{:S(2)}) %collective-permute-start.12) | collective-permute-done | bytes 12320 | tf_op jit(solution)/shard_map/ppermute | solution.py:26
  197.4 2.1 collective-permute-start.15
  199.5 1.3 collective-permute-start.14
  200.8 0.1 collective-permute-done.15
  200.9 4.2 %collective-permute-done.14 = f32[3,10,1,128]{3,2,1,0:T(1,128)S(1)} collective-permute-done((f32[3,10,1,128]{3,2,1,0:T(1,128)S(1)}, f32[3,10,1,128]{3,2,1,0:T(1,128)S(1)}, u32[]{:S(2)}, u32[]{:S(2)}) %collective-permute-start.14) | collective-permute-done | bytes 15392 | tf_op jit(solution)/shard_map/ppermute | solution.py:26
  205.2 0.1 fusion.68
  205.3 1.3 collective-permute-start.16
  206.6 3.0 %collective-permute-start.17 = (f32[3,10,10,1]{3,2,1,0:T(8,128)S(1)}, f32[3,10,10,1]{3,2,1,0:T(8,128)S(1)}, u32[]{:S(2)}, u32[]{:S(2)}) collective-permute-start(f32[3,10,10,1]{3,2,1,0:T(8,128)S(1)} %get-tuple-element.20), channel_id=1, source_target_pairs={{0,1},{1,2},{2,3},{4,5},{5,6},{6,7},{8,9},{9,10},{10,11},{12,13},{... | collective-permute-start | bytes 3608 | tf_op jit(solution)/shard_map/ppermute | solution.py:23
  209.7 1.1 collective-permute-done.17
  210.8 0.8 multiply_reduce_fusion.3
  211.6 44.0 %all-reduce = (f32[]{:T(128)}, f32[]{:T(128)}) all-reduce(f32[]{:T(128)} %get-tuple-element.5, f32[]{:T(128)} %get-tuple-element.4), channel_id=1, replica_groups=mesh['gx'=2,'gy'=4,'gz'=4] {'gx','gy','gz'}, use_global_device_ids=true, to_apply=%region_13.14 | all-reduce | flops 2 | bytes 16 | tf_op jit(solution)/shard_map/psum | solution.py:82
  259.5 0.7 multiply_subtract_fusion
  (25 shorter events, 0.3 us)
Async XLA Ops:
  9.7 4.8 %copy-start.1 = (f32[128,3,512]{2,0,1:T(8,128)}, f32[128,3,512]{2,0,1:T(8,128)S(1)}, u32[]{:S(2)}) copy-start(f32[128,3,512]{2,0,1:T(8,128)S(1)} %copy.35) | copy-start | bytes 2359300
  34.7 5.2 %copy-start.2 = (f32[128,3,512]{2,0,1:T(8,128)S(1)}, f32[128,3,512]{2,0,1:T(8,128)}, u32[]{:S(2)}) copy-start(f32[128,3,512]{2,0,1:T(8,128)} %copy-done.1) | copy-start | bytes 2359300
  39.9 5.5 %copy-start = (f32[3,8,8,128]{3,2,1,0:T(8,128)S(1)}, f32[3,8,8,128]{3,2,1,0:T(8,128)}, u32[]{:S(2)}) copy-start(f32[3,8,8,128]{3,2,1,0:T(8,128)} %param.6) | copy-start | bytes 294916
  45.5 5.3 %collective-permute-start.1 = (f32[3,1,8,128]{3,2,1,0:T(8,128)S(1)}, f32[3,1,8,128]{3,2,1,0:T(8,128)S(1)}, u32[]{:S(2)}, u32[]{:S(2)}) collective-permute-start(f32[3,1,8,128]{3,2,1,0:T(8,128)S(1)} %get-tuple-element.37), channel_id=1, source_target_pairs={{0,16},{1,17},{2,18},{3,19},{4,20},{5,21},{6,22},{7,23},{8,24},{9,... | collective-permute-start | bytes 36872 | tf_op jit(solution)/shard_map/ppermute | solution.py:23
  49.4 5.6 %collective-permute-start = (f32[3,1,8,128]{3,2,1,0:T(8,128)S(1)}, f32[3,1,8,128]{3,2,1,0:T(8,128)S(1)}, u32[]{:S(2)}, u32[]{:S(2)}) collective-permute-start(f32[3,1,8,128]{3,2,1,0:T(8,128)S(1)} %get-tuple-element.38), channel_id=1, source_target_pairs={{16,0},{17,1},{18,2},{19,3},{20,4},{21,5},{22,6},{23,7},{24,8},{25... | collective-permute-start | bytes 36872 | tf_op jit(solution)/shard_map/ppermute | solution.py:26
  55.0 4.9 %collective-permute-start.3 = (f32[3,10,1,128]{3,2,1,0:T(1,128)S(1)}, f32[3,10,1,128]{3,2,1,0:T(1,128)S(1)}, u32[]{:S(2)}, u32[]{:S(2)}) collective-permute-start(f32[3,10,1,128]{3,2,1,0:T(1,128)S(1)} %get-tuple-element.29), channel_id=1, source_target_pairs={{0,4},{4,8},{8,12},{1,5},{5,9},{9,13},{2,6},{6,10},{10,14},{3,7},{... | collective-permute-start | bytes 46088 | tf_op jit(solution)/shard_map/ppermute | solution.py:23
  58.5 5.6 %collective-permute-start.2 = (f32[3,10,1,128]{3,2,1,0:T(1,128)S(1)}, f32[3,10,1,128]{3,2,1,0:T(1,128)S(1)}, u32[]{:S(2)}, u32[]{:S(2)}) collective-permute-start(f32[3,10,1,128]{3,2,1,0:T(1,128)S(1)} %get-tuple-element.30), channel_id=1, source_target_pairs={{4,0},{8,4},{12,8},{5,1},{9,5},{13,9},{6,2},{10,6},{14,10},{7,3},{... | collective-permute-start | bytes 46088 | tf_op jit(solution)/shard_map/ppermute | solution.py:26
  64.3 4.6 %collective-permute-start.4 = (f32[3,10,10,1]{3,2,1,0:T(8,128)S(1)}, f32[3,10,10,1]{3,2,1,0:T(8,128)S(1)}, u32[]{:S(2)}, u32[]{:S(2)}) collective-permute-start(f32[3,10,10,1]{3,2,1,0:T(8,128)S(1)} %get-tuple-element.23), channel_id=1, source_target_pairs={{1,0},{2,1},{3,2},{5,4},{6,5},{7,6},{9,8},{10,9},{11,10},{13,12},{... | collective-permute-start | bytes 3608 | tf_op jit(solution)/shard_map/ppermute | solution.py:26
  65.6 4.2 %collective-permute-start.5 = (f32[3,10,10,1]{3,2,1,0:T(8,128)S(1)}, f32[3,10,10,1]{3,2,1,0:T(8,128)S(1)}, u32[]{:S(2)}, u32[]{:S(2)}) collective-permute-start(f32[3,10,10,1]{3,2,1,0:T(8,128)S(1)} %get-tuple-element.24), channel_id=1, source_target_pairs={{0,1},{1,2},{2,3},{4,5},{5,6},{6,7},{8,9},{9,10},{10,11},{12,13},{... | collective-permute-start | bytes 3608 | tf_op jit(solution)/shard_map/ppermute | solution.py:23
  115.2 5.6 %collective-permute-start.7 = (f32[3,1,8,128]{3,2,1,0:T(8,128)S(1)}, f32[3,1,8,128]{3,2,1,0:T(8,128)S(1)}, u32[]{:S(2)}, u32[]{:S(2)}) collective-permute-start(f32[3,1,8,128]{3,2,1,0:T(8,128)S(1)} %get-tuple-element.35), channel_id=1, source_target_pairs={{0,16},{1,17},{2,18},{3,19},{4,20},{5,21},{6,22},{7,23},{8,24},{9,... | collective-permute-start | bytes 36872 | tf_op jit(solution)/shard_map/ppermute | solution.py:23
  119.4 5.6 %collective-permute-start.6 = (f32[3,1,8,128]{3,2,1,0:T(8,128)S(1)}, f32[3,1,8,128]{3,2,1,0:T(8,128)S(1)}, u32[]{:S(2)}, u32[]{:S(2)}) collective-permute-start(f32[3,1,8,128]{3,2,1,0:T(8,128)S(1)} %get-tuple-element.36), channel_id=1, source_target_pairs={{16,0},{17,1},{18,2},{19,3},{20,4},{21,5},{22,6},{23,7},{24,8},{25... | collective-permute-start | bytes 36872 | tf_op jit(solution)/shard_map/ppermute | solution.py:26
  125.0 3.5 %collective-permute-start.9 = (f32[3,10,1,128]{3,2,1,0:T(1,128)S(1)}, f32[3,10,1,128]{3,2,1,0:T(1,128)S(1)}, u32[]{:S(2)}, u32[]{:S(2)}) collective-permute-start(f32[3,10,1,128]{3,2,1,0:T(1,128)S(1)} %get-tuple-element.27), channel_id=1, source_target_pairs={{0,4},{4,8},{8,12},{1,5},{5,9},{9,13},{2,6},{6,10},{10,14},{3,7},{... | collective-permute-start | bytes 46088 | tf_op jit(solution)/shard_map/ppermute | solution.py:23
  127.1 5.6 %collective-permute-start.8 = (f32[3,10,1,128]{3,2,1,0:T(1,128)S(1)}, f32[3,10,1,128]{3,2,1,0:T(1,128)S(1)}, u32[]{:S(2)}, u32[]{:S(2)}) collective-permute-start(f32[3,10,1,128]{3,2,1,0:T(1,128)S(1)} %get-tuple-element.28), channel_id=1, source_target_pairs={{4,0},{8,4},{12,8},{5,1},{9,5},{13,9},{6,2},{10,6},{14,10},{7,3},{... | collective-permute-start | bytes 46088 | tf_op jit(solution)/shard_map/ppermute | solution.py:26
  132.9 4.4 %collective-permute-start.10 = (f32[3,10,10,1]{3,2,1,0:T(8,128)S(1)}, f32[3,10,10,1]{3,2,1,0:T(8,128)S(1)}, u32[]{:S(2)}, u32[]{:S(2)}) collective-permute-start(f32[3,10,10,1]{3,2,1,0:T(8,128)S(1)} %get-tuple-element.21), channel_id=1, source_target_pairs={{1,0},{2,1},{3,2},{5,4},{6,5},{7,6},{9,8},{10,9},{11,10},{13,12},{... | collective-permute-start | bytes 3608 | tf_op jit(solution)/shard_map/ppermute | solution.py:26
  134.2 4.2 %collective-permute-start.11 = (f32[3,10,10,1]{3,2,1,0:T(8,128)S(1)}, f32[3,10,10,1]{3,2,1,0:T(8,128)S(1)}, u32[]{:S(2)}, u32[]{:S(2)}) collective-permute-start(f32[3,10,10,1]{3,2,1,0:T(8,128)S(1)} %get-tuple-element.22), channel_id=1, source_target_pairs={{0,1},{1,2},{2,3},{4,5},{5,6},{6,7},{8,9},{9,10},{10,11},{12,13},{... | collective-permute-start | bytes 3608 | tf_op jit(solution)/shard_map/ppermute | solution.py:23
  187.6 5.6 %collective-permute-start.13 = (f32[3,1,8,128]{3,2,1,0:T(8,128)S(1)}, f32[3,1,8,128]{3,2,1,0:T(8,128)S(1)}, u32[]{:S(2)}, u32[]{:S(2)}) collective-permute-start(f32[3,1,8,128]{3,2,1,0:T(8,128)S(1)} %get-tuple-element.33), channel_id=1, source_target_pairs={{0,16},{1,17},{2,18},{3,19},{4,20},{5,21},{6,22},{7,23},{8,24},{9,... | collective-permute-start | bytes 36872 | tf_op jit(solution)/shard_map/ppermute | solution.py:23
  191.8 5.6 %collective-permute-start.12 = (f32[3,1,8,128]{3,2,1,0:T(8,128)S(1)}, f32[3,1,8,128]{3,2,1,0:T(8,128)S(1)}, u32[]{:S(2)}, u32[]{:S(2)}) collective-permute-start(f32[3,1,8,128]{3,2,1,0:T(8,128)S(1)} %get-tuple-element.34), channel_id=1, source_target_pairs={{16,0},{17,1},{18,2},{19,3},{20,4},{21,5},{22,6},{23,7},{24,8},{25... | collective-permute-start | bytes 36872 | tf_op jit(solution)/shard_map/ppermute | solution.py:26
  197.4 3.5 %collective-permute-start.15 = (f32[3,10,1,128]{3,2,1,0:T(1,128)S(1)}, f32[3,10,1,128]{3,2,1,0:T(1,128)S(1)}, u32[]{:S(2)}, u32[]{:S(2)}) collective-permute-start(f32[3,10,1,128]{3,2,1,0:T(1,128)S(1)} %get-tuple-element.25), channel_id=1, source_target_pairs={{0,4},{4,8},{8,12},{1,5},{5,9},{9,13},{2,6},{6,10},{10,14},{3,7},{... | collective-permute-start | bytes 46088 | tf_op jit(solution)/shard_map/ppermute | solution.py:23
  199.5 5.6 %collective-permute-start.14 = (f32[3,10,1,128]{3,2,1,0:T(1,128)S(1)}, f32[3,10,1,128]{3,2,1,0:T(1,128)S(1)}, u32[]{:S(2)}, u32[]{:S(2)}) collective-permute-start(f32[3,10,1,128]{3,2,1,0:T(1,128)S(1)} %get-tuple-element.26), channel_id=1, source_target_pairs={{4,0},{8,4},{12,8},{5,1},{9,5},{13,9},{6,2},{10,6},{14,10},{7,3},{... | collective-permute-start | bytes 46088 | tf_op jit(solution)/shard_map/ppermute | solution.py:26
  205.3 4.4 %collective-permute-start.16 = (f32[3,10,10,1]{3,2,1,0:T(8,128)S(1)}, f32[3,10,10,1]{3,2,1,0:T(8,128)S(1)}, u32[]{:S(2)}, u32[]{:S(2)}) collective-permute-start(f32[3,10,10,1]{3,2,1,0:T(8,128)S(1)} %get-tuple-element.19), channel_id=1, source_target_pairs={{1,0},{2,1},{3,2},{5,4},{6,5},{7,6},{9,8},{10,9},{11,10},{13,12},{... | collective-permute-start | bytes 3608 | tf_op jit(solution)/shard_map/ppermute | solution.py:26
  206.6 4.2 %collective-permute-start.17 = (f32[3,10,10,1]{3,2,1,0:T(8,128)S(1)}, f32[3,10,10,1]{3,2,1,0:T(8,128)S(1)}, u32[]{:S(2)}, u32[]{:S(2)}) collective-permute-start(f32[3,10,10,1]{3,2,1,0:T(8,128)S(1)} %get-tuple-element.20), channel_id=1, source_target_pairs={{0,1},{1,2},{2,3},{4,5},{5,6},{6,7},{8,9},{9,10},{10,11},{12,13},{... | collective-permute-start | bytes 3608 | tf_op jit(solution)/shard_map/ppermute | solution.py:23
where the time goes:
time: 261 us; the launch traced here: 260 us
  blocking collectives  137 us (52%)
  starting transfers between devices  40.7 us (16%)
  waiting for transfers between devices  28.8 us (11%)
  matrix products  21.5 us (8%)
  other arithmetic  12.9 us (5%)
  between operations  10.8 us (4%)
  local copies, waits for them, and re-layouts  8.15 us (3%)
    psum x3, blocking collectives, two_products(): lax.psum((jnp.sum(residual * residual), jnp.sum(residual * image)), ('gx'...  131 us
    ppermute x9, starting transfers between devices, with_halo(): lax.ppermute(lax.slice_in_dim(block, block.shape[dim] - width, None, axis...  29 us
    ppermute x9, waiting for transfers between devices, with_halo(): lax.ppermute(lax.slice_in_dim(block, 0, width, axis=dim), axis, backward)  25.2 us
    dot_general x2, matrix products, correction(): jnp.dot(polarization.reshape(row_count * 3, VOX), hartley, preferred_elem...  16.4 us
    ppermute x9, starting transfers between devices, with_halo(): lax.ppermute(lax.slice_in_dim(block, 0, width, axis=dim), axis, backward)  11.6 us
    reduce_sum x2, other arithmetic, correction(): jnp.sum(blocks * spectrum[:, None, :, :], axis=2).astype(jnp.bfloat16)  8.07 us
    all_gather x1, blocking collectives, per_device(): library = lax.all_gather(inverse_blocks, 'gx', axis=0, tiled=True)  6.23 us
  transfers between devices with their start and end apart: 18, of which 15 were waited for; matrix products, arithmetic and copies ran while one was open for 0% of the time, Pallas kernels for 0%

commit v1 on v0

v1 whole, which is shorter than its diff:
```python
import functools
import math

import jax
import jax.numpy as jnp
from jax import lax
from jax.experimental import pallas as pl
from jax.experimental.pallas import tpu as pltpu
from jax.sharding import PartitionSpec as P

CELL = 8
VOX = 512
TYPES = 4
ZP = 8
ITERS = 3
AXES = ("gx", "gy", "gz")
DENSE = 64
SHIFT = 8.0

kerr_scale = 0.1


def where_am_i():
    return tuple(lax.axis_index(a) for a in AXES)


def spectrum_kernel(contrast, point_field, hartley, spectrum, columns, polar):
    rows = contrast.shape[0]
    step = CELL * CELL
    inner = lax.broadcasted_iota(jnp.int32, (step, VOX), 0)
    voxel = lax.broadcasted_iota(jnp.int32, (step, VOX), 1)
    phase = (inner // CELL) * (voxel // CELL % CELL) + (inner % CELL) * (voxel % CELL)
    outer = voxel // step
    plain = 1.0 / math.sqrt(VOX)
    peak = math.sqrt(2.0) / math.sqrt(VOX)
    for block in range(VOX // step):
        turn = (phase + block * outer) & (CELL - 1)
        quarter = turn & 3
        size = jnp.where(quarter == 1, peak, jnp.where(quarter == 3, 0.0, plain))
        value = jnp.where(turn >= 4, -size, size)
        hartley[block * step : (block + 1) * step, :] = value.astype(jnp.bfloat16)
    fields = point_field[...].astype(jnp.float32)
    fields = jnp.concatenate([fields, jnp.zeros((5, rows), jnp.float32)], axis=0)
    columns[...] = fields.T
    for j in range(3):
        e = columns[:, j : j + 1]
        m = contrast[:, j * VOX : (j + 1) * VOX].astype(jnp.float32)
        polar[j * rows : (j + 1) * rows, :] = (m * e).astype(jnp.bfloat16)
    spectrum[...] = jnp.dot(polar[...], hartley[...], preferred_element_type=jnp.float32)


def solve_kernel(keep_class, contrast, columns, spectrum, hartley, point_class, cell_kind, library, other,
                 source, tiles, bundle, mixing, stacked, product):
    rows = contrast.shape[0]
    zb = rows // 8
    gx, _, gz = where_am_i()
    keys = point_class[...] if keep_class else jnp.where(point_class[...] == gx, 0, 1)
    keys = keys * TYPES + cell_kind[...]
    count = library.shape[0] * TYPES * (1 if keep_class else 2)
    pick = (lax.broadcasted_iota(jnp.int32, (count, rows), 0) == keys).astype(jnp.float32)
    pick = jnp.concatenate([pick, pick], axis=0)
    pick = pick.T.astype(jnp.bfloat16)
    for ij in range(9):
        i, j = ij // 3, ij % 3
        parts = [library[c, i, j] for c in range(library.shape[0])]
        if not keep_class:
            parts = parts + [other[c, i, j] for c in range(library.shape[0])]
        table = jnp.concatenate(parts, axis=0)
        high = table.astype(jnp.bfloat16).astype(jnp.float32)
        both = jnp.concatenate([high, table - high], axis=0).astype(jnp.bfloat16)
        mixing[ij] = jnp.dot(pick, both, preferred_element_type=jnp.float32)

    def mix(from_ref):
        for c in range(rows // 16):
            at = slice(c * 16, (c + 1) * 16)
            held = [from_ref[j * rows + c * 16 : j * rows + (c + 1) * 16, :] for j in range(3)]
            for i in range(3):
                total = mixing[3 * i, at, :] * held[0]
                total = total + mixing[3 * i + 1, at, :] * held[1]
                total = total + mixing[3 * i + 2, at, :] * held[2]
                stacked[i * rows + c * 16 : i * rows + (c + 1) * 16, :] = total.astype(jnp.bfloat16)

    mix(spectrum)
    product[...] = jnp.dot(stacked[...], hartley[...], preferred_element_type=jnp.float32)
    for c in range(rows // 16):
        for j in range(3):
            at = slice(j * rows + c * 16, j * rows + (c + 1) * 16)
            m = contrast[c * 16 : (c + 1) * 16, j * VOX : (j + 1) * VOX].astype(jnp.float32)
            local = columns[c * 16 : (c + 1) * 16, j : j + 1] - product[at, :]
            stacked[at, :] = (m * local * (1.0 + kerr_scale * local * local)).astype(jnp.bfloat16)
    product[...] = jnp.dot(stacked[...], hartley[...], preferred_element_type=jnp.float32)
    mix(product)
    product[...] = jnp.dot(stacked[...], hartley[...], preferred_element_type=jnp.float32)

    depth = lax.broadcasted_iota(jnp.int32, (zb, 128), 0)
    lane = lax.broadcasted_iota(jnp.int32, (zb, 128), 1)
    spread = lane // ZP == depth
    packed = lane % zb == depth
    group = lane // zb
    for c in range(rows // 16):
        means = []
        stiff = jnp.zeros((16, VOX), jnp.float32)
        for j in range(3):
            at = slice(j * rows + c * 16, j * rows + (c + 1) * 16)
            m = contrast[c * 16 : (c + 1) * 16, j * VOX : (j + 1) * VOX].astype(jnp.float32)
            final = columns[c * 16 : (c + 1) * 16, j : j + 1] - product[at, :]
            means.append(jnp.sum((1.0 + m) * final, axis=1, keepdims=True) * (1.0 / VOX))
            stiff = stiff + m * final * final
        means.append(0.5 + jnp.sum(stiff, axis=1, keepdims=True) * (1.0 / (3 * VOX)))
        compact = jnp.zeros((zb, 128), jnp.float32)
        for t in range(4):
            wide = jnp.broadcast_to(means[t], (zb, 128))
            tiles[t, c : c + 1, :] = jnp.sum(jnp.where(spread, wide, 0.0), axis=0, keepdims=True)
            compact = compact + jnp.where(packed & (group == t), wide, 0.0)
        product[c : c + 1, 0:128] = jnp.sum(compact, axis=0, keepdims=True)
    compact = product[0:8, 0:128]

    place = lax.broadcasted_iota(jnp.int32, (8, 128), 1)
    low = jnp.zeros((8, 128), jnp.float32)
    high = jnp.zeros((8, 128), jnp.float32)
    slabs = source.shape[1]
    for s in range(3 * slabs + 1):
        if s < 3 * slabs:
            value = source[s // slabs, s % slabs] - tiles[s // slabs]
        else:
            value = tiles[3]
        here = (place >= 3 * s) & (place < 3 * s + 3)
        low = jnp.where(here, pltpu.roll(value, (3 * s) % 128, 1) if s else value, low)
        high = jnp.where(here, pltpu.roll(value, (3 * s + 3) % 128, 1), high)
    for d in range(bundle.shape[1]):
        zero = jnp.zeros((8, 128), jnp.float32)
        tile = jnp.where(gz == d, compact, jnp.where(gz + 1 == d, high, jnp.where(gz - 1 == d, low, zero)))
        for x in range(bundle.shape[0]):
            bundle[x, d] = tile


def moment_kernel(dense, counts, tiles, got, source, xlow, xhigh, ylow, yhigh, v0, v1, v2, v3, moments, w0, w1, w2):
    slabs = source.shape[1]
    gx, gy, gz = where_am_i()
    nx, ny, nz = counts
    row = lax.broadcasted_iota(jnp.int32, (8, 128), 0)
    lane = lax.broadcasted_iota(jnp.int32, (8, 128), 1)
    has_xl, has_xh = gx > 0, gx < nx - 1
    has_yl, has_yh = gy > 0, gy < ny - 1
    has_zl, has_zh = gz > 0, gz < nz - 1
    one = lambda flag: jnp.where(flag, 1.0, 0.0)
    mask_y = jnp.where(row < 4, one(has_yh), one(has_yl))
    mask_z = jnp.where(lane < 64, one(has_zh), one(has_zl))
    masks = (None, mask_y, mask_z, mask_y * mask_z)
    yl, yh = jnp.maximum(gy - 1, 0), jnp.minimum(gy + 1, ny - 1)
    zl, zh = jnp.maximum(gz - 1, 0), jnp.minimum(gz + 1, nz - 1)
    if dense:
        regions = (jnp.maximum(gx - 1, 0), gx, jnp.minimum(gx + 1, nx - 1))
    else:
        regions = (0, 1, 2)
    upper = row < 4
    spread = lane // ZP
    zb = 128 // ZP

    def unfold(tile, t):
        return jnp.take_along_axis(tile, spread + t * zb, axis=1)

    def pull(low_tile, high_tile, s):
        a = pltpu.roll(high_tile, (-3 * s) % 128, 1) if s else high_tile
        b = pltpu.roll(low_tile, (125 - 3 * s) % 128, 1)
        return jnp.where(lane < 64, a, b)

    diag = {}
    flux = {}
    for r in range(3):
        x = regions[r]
        rowtile = jnp.where(upper, got[x, yh, gz], got[x, yl, gz])
        flux[r, 1] = [unfold(rowtile, t) for t in range(3)]
        diag[r, 1] = unfold(rowtile, 3)
        if r == 1:
            flux[r, 0] = [tiles[t] for t in range(3)]
            diag[r, 0] = tiles[3]
        else:
            flux[r, 0] = [unfold(got[x, gy, gz], t) for t in range(3)]
            diag[r, 0] = unfold(got[x, gy, gz], 3)
        side_low, side_high = got[x, gy, zl], got[x, gy, zh]
        corner_low = jnp.where(upper, got[x, yh, zl], got[x, yl, zl])
        corner_high = jnp.where(upper, got[x, yh, zh], got[x, yl, zh])
        diag[r, 2] = pull(side_low, side_high, 3 * slabs)
        diag[r, 3] = pull(corner_low, corner_high, 3 * slabs)
        edge_x = None if r == 1 else one(has_xl if r == 0 else has_xh)
        for c in range(3):
            for k in range(3 if r != 1 else slabs):
                at = k if r == 0 else (3 + k if r == 1 else 3 + slabs + k)
                out = (3 - k) if r == 0 else (0 if r == 1 else k + 1)
                s = c * slabs + (slabs - 3 + k if r == 0 else k)
                value = (source if r == 1 else (xlow if r == 0 else xhigh))[c, k] - flux[r, 0][c]
                w0[c, at, 0] = value if edge_x is None else value * edge_x
                if r == 1:
                    v0[c, k] = value
                if out <= 2:
                    halo = jnp.concatenate([yhigh[c, at], ylow[c, at]], axis=0) - flux[r, 1][c]
                    w0[c, at, 1] = halo * (mask_y if edge_x is None else mask_y * edge_x)
                    value = pull(side_low, side_high, s)
                    w0[c, at, 2] = value * (mask_z if edge_x is None else mask_z * edge_x)
                if out <= 1:
                    value = pull(corner_low, corner_high, s)
                    w0[c, at, 3] = value * (masks[3] if edge_x is None else masks[3] * edge_x)
    for key in diag:
        diag[key] = diag[key] + (6.0 - SHIFT)

    first_row, last_row = row == 0, row == 7
    first_lane, last_lane = lane == 0, lane == 127
    acc = [jnp.zeros((8, 128), jnp.float32) for _ in range(6)]
    levels = (w0, w1, w2, None)
    results = (v0, v1, v2, v3)
    for level in (1, 2, 3):
        src, dst = levels[level - 1], levels[level]
        reach = 3 - level
        for c in range(3):
            for at in range(3 - reach, 3 + slabs + reach):
                out = max(3 - at, at - slabs - 2, 0)
                r = 0 if at < 3 else (1 if at < 3 + slabs else 2)
                depth = reach - out
                want = (0,) if depth == 0 else ((0, 1, 2) if depth == 1 else (0, 1, 2, 3))
                have = (0, 1, 2) if depth == 0 else (0, 1, 2, 3)
                v = {t: src[c, at, t] for t in have}
                left = {t: pltpu.roll(v[t], 127, 1) for t in have if t in (0, 2) or depth > 0}
                right = {t: pltpu.roll(v[t], 1, 1) for t in have if t in (0, 2) or depth > 0}
                down = {t: pltpu.roll(v[t], 7, 0) for t in have if t in (0, 1) or depth > 0}
                over = {t: pltpu.roll(v[t], 1, 0) for t in have if t in (0, 1) or depth > 0}
                edge_x = None if r == 1 else one(has_xl if r == 0 else has_xh)
                for t in want:
                    zp = jnp.where(last_lane, left[t ^ 2], left[t])
                    zm = jnp.where(first_lane, right[t ^ 2], right[t])
                    yp = jnp.where(last_row, down[t ^ 1], down[t])
                    ym = jnp.where(first_row, over[t ^ 1], over[t])
                    beside = (src[c, at - 1, t] + src[c, at + 1, t]) + (zp + zm) + (yp + ym)
                    value = diag[r, t] * v[t] - beside
                    if masks[t] is not None:
                        value = value * masks[t]
                    if edge_x is not None:
                        value = value * edge_x
                    if dst is not None:
                        dst[c, at, t] = value
                    if t == 0 and r == 1:
                        results[level][c, at - 3] = value
                        acc[2 * level - 1] = acc[2 * level - 1] + v[0] * value
                        if level < 3:
                            acc[2 * level] = acc[2 * level] + value * value
                        if level == 1:
                            acc[0] = acc[0] + v[0] * v[0]
    for k in range(6):
        moments[k : k + 1, :] = jnp.sum(acc[k], axis=0, keepdims=True)
    moments[6:8, :] = jnp.zeros((2, 128), jnp.float32)


def combine_kernel(parts, v0, v1, v2, v3, step_out, residual_out):
    total = parts[0]
    for k in range(1, parts.shape[0]):
        total = total + parts[k]
    sums = jnp.sum(total, axis=1, keepdims=True)
    nu = [sums[k : k + 1, :] for k in range(6)]

    def gram(a, b):
        result = None
        for i, ai in enumerate(a):
            for j, bj in enumerate(b):
                term = ai * bj * nu[i + j]
                result = term if result is None else result + term
        return result

    def added(a, b):
        size = max(len(a), len(b))
        return [a[k] if k >= len(b) else (b[k] if k >= len(a) else a[k] + b[k]) for k in range(size)]

    unit = jnp.ones((1, 1), jnp.float32)
    direction, residual, newton = [unit], [unit], []
    norm = nu[0]
    for iteration in range(ITERS):
        image = added([SHIFT * d for d in direction], [0.0 * unit] + direction)
        alpha = norm / gram(direction, image)
        newton = added(newton, [alpha * d for d in direction])
        residual = added(residual, [-alpha * g for g in image])
        if iteration + 1 < ITERS:
            following = gram(residual, residual)
            ratio = following / norm
            direction = added(residual, [ratio * d for d in direction])
            norm = following
    wide = lambda a: jnp.broadcast_to(a, (8, 128))
    newton = [wide(a) for a in newton]
    residual = [wide(a) for a in residual]
    for c in range(v0.shape[0]):
        for x in range(v0.shape[1]):
            a, b, d = v0[c, x], v1[c, x], v2[c, x]
            step_out[c, x] = newton[0] * a + newton[1] * b + newton[2] * d
            residual_out[c, x] = residual[0] * a + residual[1] * b + residual[2] * d + residual[3] * v3[c, x]


def call(body, outs, ins, scratch=(), name=None):
    vmem = pl.BlockSpec(memory_space=pltpu.VMEM)
    return pl.pallas_call(
        body,
        name=name,
        out_shape=tuple(jax.ShapeDtypeStruct(s, d) for s, d in outs),
        in_specs=[vmem] * len(ins),
        out_specs=tuple(vmem for _ in outs),
        scratch_shapes=list(scratch),
    )(*ins)


def ladder(axis):
    count = lax.axis_size(axis)
    forward = [(i, i + 1) for i in range(count - 1)]
    return forward, [(b, a) for a, b in forward]


def from_both(low_face, high_face, axis):
    forward, backward = ladder(axis)
    return lax.ppermute(high_face, axis, forward), lax.ppermute(low_face, axis, backward)


def per_device(source, contrast, point_field, point_class, cell_kind, inverse_blocks):
    f32, bf16 = jnp.float32, jnp.bfloat16
    rows = contrast.shape[0]
    counts = tuple(lax.axis_size(a) for a in AXES)
    nx, ny, nz = counts
    slabs = source.shape[1]
    gx = lax.axis_index("gx")
    dense = nx * ny * nz <= DENSE
    pair = nx == 2
    library = inverse_blocks.transpose(0, 2, 3, 1, 4)
    if pair:
        swap = [(0, 1), (1, 0)]
        other = lax.ppermute(library, "gx", swap)
        face = jnp.where(gx == 0, source[:, slabs - 3 :], source[:, :3])
        face = lax.ppermute(face, "gx", swap)
        xlow = jnp.where(gx == 1, face, 0.0)
        xhigh = jnp.where(gx == 0, face, 0.0)
    else:
        library = lax.all_gather(library, "gx", axis=0, tiled=True)
        other = library
        xlow, xhigh = from_both(source[:, :3], source[:, slabs - 3 :], "gx")
    hartley, spectrum, columns = call(
        spectrum_kernel,
        [((VOX, VOX), bf16), ((3 * rows, VOX), f32), ((rows, 8), f32)],
        (contrast, point_field),
        [pltpu.VMEM((3 * rows, VOX), bf16)],
        name="spectrum",
    )
    longer = jnp.concatenate([xlow, source, xhigh], axis=1)
    ylow, yhigh = from_both(longer[:, :, :4], longer[:, :, 4:], "gy")
    tiles, bundle = call(
        functools.partial(solve_kernel, not pair),
        [((4, 8, 128), f32), ((nx * ny if dense else 1, nz, 8, 128), f32)],
        (contrast, columns, spectrum, hartley, point_class.reshape(1, rows), cell_kind.reshape(1, rows),
         library, other, source),
        [pltpu.VMEM((9, rows, VOX), f32), pltpu.VMEM((3 * rows, VOX), bf16), pltpu.VMEM((3 * rows, VOX), f32)],
        name="solve",
    )
    if dense:
        got = lax.all_to_all(bundle.reshape(nx * ny * nz, 8, 128), AXES, 0, 0).reshape(nx, ny, nz, 8, 128)
    else:
        below, above = from_both(bundle[0], bundle[0], "gx")
        trio = jnp.stack([below, bundle[0], above], axis=1)
        trio = jnp.broadcast_to(trio[None], (ny,) + trio.shape).reshape(ny * nz, 3, 8, 128)
        got = lax.all_to_all(trio, ("gy", "gz"), 0, 0).reshape(ny, nz, 3, 8, 128).transpose(2, 0, 1, 3, 4)
    field = (source.shape, f32)
    v0, v1, v2, v3, moments = call(
        functools.partial(moment_kernel, dense, counts),
        [field, field, field, field, ((8, 128), f32)],
        (tiles, got, source, xlow, xhigh, ylow, yhigh),
        [pltpu.VMEM((3, slabs + 6, 4, 8, 128), f32) for _ in range(3)],
        name="moments",
    )
    if dense:
        parts = jnp.broadcast_to(moments[None], (nx * ny * nz, 8, 128))
        parts = lax.all_to_all(parts, AXES, 0, 0)
    else:
        parts = lax.psum(moments, AXES)[None]
    return call(combine_kernel, [field, field], (parts, v0, v1, v2, v3), name="combine")


def solution(mesh):
    placed = (
        P(None, "gx", "gy", "gz"),
        P(("gx", "gy", "gz"), None),
        P(None, ("gx", "gy", "gz")),
        P(("gx", "gy", "gz"), None),
        P(("gx", "gy", "gz")),
        P("gx", None, None, None, None),
    )
    return jax.shard_map(
        per_device,
        mesh=mesh,
        in_specs=placed,
        out_specs=(P(None, "gx", "gy", "gz"), P(None, "gx", "gy", "gz")),
        check_vma=False,
    )
```

time: 261 us -> 48.3 us (0.19)
  blocking collectives: 137 us -> 12.7 us
  starting transfers between devices: 40.7 us -> 13.6 us
  waiting for transfers between devices: 28.8 us -> 5.78 us
  matrix products: 21.5 us -> 0 us
  other arithmetic: 12.9 us -> 0.85 us
  Pallas kernels: 0 us -> 11.2 us
  between operations: 10.8 us -> 0.73 us
  local copies, waits for them, and re-layouts: 8.15 us -> 2.93 us
    psum x3 -> x0, blocking collectives: 131 us -> none  [two_products(): lax.psum((jnp.sum(residual * residual), jnp.sum(residual * image)), ('gx'...]
    ppermute x18 -> x4, starting transfers between devices: 40.7 us -> 8.01 us  [the longest x1 3.68 us: from_both(): lax.ppermute(high_face, axis, forward)]
    ppermute x18 -> x4, waiting for transfers between devices: 28.8 us -> 5.77 us  [the longest x1 4.3 us: from_both(): lax.ppermute(low_face, axis, backward)]
    dot_general x3 -> x0, matrix products: 21.5 us -> none  [the longest x2 16.4 us: correction(): jnp.dot(polarization.reshape(row_count * 3, VOX), hartley, preferred_elem...]
    all_to_all x0 -> x1, blocking collectives: none -> 12.7 us  [per_device(): parts = lax.all_to_all(parts, AXES, 0, 0)]
    pallas_call x0 -> x4, Pallas kernels: none -> 11.2 us  [call(): pl.pallas_call(body, name=name, out_shape=tuple((jax.ShapeDtypeStruct(s,...]
    reduce_sum x5 -> x0, other arithmetic: 10.5 us -> none  [the longest x2 8.07 us: correction(): jnp.sum(blocks * spectrum[:, None, :, :], axis=2).astype(jnp.bfloat16)]
    all_gather x1 -> x0, blocking collectives: 6.23 us -> none  [per_device(): library = lax.all_gather(inverse_blocks, 'gx', axis=0, tiled=True)]
  transfers between devices with their start and end apart: 18 -> 5, of which waited for: 15 -> 3; matrix products, arithmetic and copies ran while one was open for 0% -> 0% of each run, Pallas kernels for 0% -> 5%
where the time goes in v1:
time: 48.3 us; the launch traced here: 47.9 us
  starting transfers between devices  13.6 us (28%)
  blocking collectives  12.7 us (26%)
  Pallas kernels  11.2 us (23%)
  waiting for transfers between devices  5.78 us (12%)
  local copies, waits for them, and re-layouts  2.93 us (6%)
  other arithmetic  0.85 us (2%)
  between operations  0.73 us (2%)
    all_to_all x1, blocking collectives, per_device(): parts = lax.all_to_all(parts, AXES, 0, 0)  12.7 us
    pallas_call x4, Pallas kernels, call(): pl.pallas_call(body, name=name, out_shape=tuple((jax.ShapeDtypeStruct(s,...  11.2 us
    all_to_all x1, starting transfers between devices, per_device(): lax.all_to_all(bundle.reshape(nx * ny * nz, 8, 128), AXES, 0, 0)  5.63 us
    ppermute x1, waiting for transfers between devices, from_both(): lax.ppermute(low_face, axis, backward)  4.3 us
    ppermute x1, starting transfers between devices, from_both(): lax.ppermute(high_face, axis, forward)  3.68 us
    ppermute x1, starting transfers between devices, per_device(): face = lax.ppermute(face, 'gx', swap)  2.97 us
    unnamed x16, local copies, waits for them, and re-layouts  2.22 us
    ppermute x1, starting transfers between devices, from_both(): lax.ppermute(low_face, axis, backward)  1.29 us
  transfers between devices with their start and end apart: 5, of which 3 were waited for; matrix products, arithmetic and copies ran while one was open for 0% of the time, Pallas kernels for 5%

profile of v1, /device:TPU:0, one launch (start us, length us, event | category | flops | bytes accessed | tf_op | source)
XLA Modules:
  0.0 47.9 jit_solution(12053139075151241904)
XLA Ops:
  0.6 0.0 copy-start.6
  0.6 0.8 %slice_select_fusion = f32[3,3,8,128]{3,2,1,0:T(8,128)S(1)} fusion(f32[3,8,8,128]{3,2,1,0:T(8,128)} %source.3, pred[]{:T(512)S(6)} %eq.8), kind=kLoop, calls=%fused_computation.1 | loop fusion | flops 9216 | bytes 110593 | tf_op jit(solution)/shard_map/jit(_where)/select_n | solution.py:331
  1.5 3.0 %collective-permute-start.1 = (f32[3,3,8,128]{3,2,1,0:T(8,128)S(1)}, f32[3,3,8,128]{3,2,1,0:T(8,128)S(1)}, u32[]{:S(2)}, u32[]{:S(2)}) collective-permute-start(f32[3,3,8,128]{3,2,1,0:T(8,128)S(1)} %slice_select_fusion), channel_id=1, source_target_pairs={{0,16},{16,0},{1,17},{17,1},{2,18},{18,2},{3,19},{19,3},{4,20},{20... | collective-permute-start | bytes 110600 | tf_op jit(solution)/shard_map/ppermute | solution.py:332
  4.4 0.0 copy-done.6
  4.4 0.1 collective-permute-start
  4.5 2.6 %spectrum.1 = (bf16[512,512]{1,0:T(8,128)(2,1)}, f32[384,512]{1,0:T(8,128)}, f32[128,8]{1,0:T(8,128)}) custom-call(bf16[128,1536]{1,0:T(8,128)(2,1)} %contrast.3, bf16[3,128]{1,0:T(4,128)(2,1)} %point_field.1), custom_call_target="tpu_custom_call" | custom-call | tf_op jit(solution)/shard_map/spectrum/pallas_call | solution.py:297
  7.2 0.0 copy-start
  7.2 0.0 collective-permute-done.1
  7.2 0.0 copy-start.2
  7.2 0.0 copy-start.3
  7.2 0.9 %copy-done = f32[3,8,8,128]{3,2,1,0:T(8,128)S(1)} copy-done((f32[3,8,8,128]{3,2,1,0:T(8,128)S(1)}, f32[3,8,8,128]{3,2,1,0:T(8,128)}, u32[]{:S(2)}) %copy-start) | copy-done | bytes 98328
  8.1 0.0 copy-done.2
  8.1 0.0 copy-done.3
  8.1 0.7 %collective-permute-done.other = f32[1,3,3,4,512]{4,3,2,1,0:T(4,128)S(1)} collective-permute-done((f32[1,3,3,4,512]{4,3,2,1,0:T(4,128)S(1)}, f32[1,3,3,4,512]{4,3,2,1,0:T(4,128)S(1)}, u32[]{:S(2)}, u32[]{:S(2)}) %collective-permute-start) | collective-permute-done | bytes 73760 | tf_op jit(solution)/shard_map/ppermute | solution.py:330
  8.8 0.0 copy-start.7
  8.8 0.6 %copy-done.7 = f32[1,3,3,4,512]{4,3,2,1,0:T(4,128)} copy-done((f32[1,3,3,4,512]{4,3,2,1,0:T(4,128)}, f32[1,3,3,4,512]{4,3,2,1,0:T(4,128)S(1)}, u32[]{:S(2)}) %copy-start.7) | copy-done | bytes 73752
  9.4 3.9 %solve.1 = (f32[4,8,128]{2,1,0:T(8,128)}, f32[8,4,8,128]{3,2,1,0:T(8,128)}) custom-call(bf16[128,1536]{1,0:T(8,128)(2,1)} %contrast.3, f32[128,8]{1,0:T(8,128)} %get-tuple-element.12.columns, f32[384,512]{1,0:T(8,128)} %get-tuple-element.13.spectrum, bf16[512,512]{1,0:T(8,128)(2,1)} %get-tuple-element.14.hartley, s32[1,128]{1,0:T(1,128)} %bitcast.9, ...), custom_call_target="tpu_custom_call" | custom-call | tf_op jit(solution)/shard_map/solve/pallas_call | solution.py:297
  13.4 5.6 %all-to-all-start = ((f32[32,8,128]{2,1,0:T(8,128)}), f32[32,8,128]{2,1,0:T(8,128)S(1)}, u32[]{:S(2)}, u32[]{:S(2)}) async-start(f32[32,8,128]{2,1,0:T(8,128)} %bitcast.6), calls=%async_computation | async-start | bytes 262144 | tf_op jit(solution)/shard_map/all_to_all | solution.py:357
  19.0 3.7 %collective-permute-start.2 = (f32[3,14,4,128]{3,2,1,0:T(4,128)S(1)}, f32[3,14,4,128]{3,2,1,0:T(4,128)S(1)}, u32[]{:S(2)}, u32[]{:S(2)}) collective-permute-start(f32[3,14,4,128]{3,2,1,0:T(4,128)S(1)} %get-tuple-element.23), channel_id=1, source_target_pairs={{0,4},{4,8},{8,12},{1,5},{5,9},{9,13},{2,6},{6,10},{10,14},{3,7},{... | collective-permute-start | bytes 258056 | tf_op jit(solution)/shard_map/ppermute | solution.py:315
  22.7 1.3 %collective-permute-start.3 = (f32[3,14,4,128]{3,2,1,0:T(4,128)S(1)}, f32[3,14,4,128]{3,2,1,0:T(4,128)S(1)}, u32[]{:S(2)}, u32[]{:S(2)}) collective-permute-start(f32[3,14,4,128]{3,2,1,0:T(4,128)S(1)} %get-tuple-element.22), channel_id=1, source_target_pairs={{4,0},{8,4},{12,8},{5,1},{9,5},{13,9},{6,2},{10,6},{14,10},{7,3},{... | collective-permute-start | bytes 258056 | tf_op jit(solution)/shard_map/ppermute | solution.py:315
  24.0 0.8 %collective-permute-done.2.ylow = f32[3,14,4,128]{3,2,1,0:T(4,128)S(1)} collective-permute-done((f32[3,14,4,128]{3,2,1,0:T(4,128)S(1)}, f32[3,14,4,128]{3,2,1,0:T(4,128)S(1)}, u32[]{:S(2)}, u32[]{:S(2)}) %collective-permute-start.2) | collective-permute-done | bytes 86048 | tf_op jit(solution)/shard_map/ppermute | solution.py:315
  24.8 0.0 copy-start.4
  24.8 4.3 %collective-permute-done.3.yhigh = f32[3,14,4,128]{3,2,1,0:T(4,128)S(1)} collective-permute-done((f32[3,14,4,128]{3,2,1,0:T(4,128)S(1)}, f32[3,14,4,128]{3,2,1,0:T(4,128)S(1)}, u32[]{:S(2)}, u32[]{:S(2)}) %collective-permute-start.3) | collective-permute-done | bytes 86048 | tf_op jit(solution)/shard_map/ppermute | solution.py:315
  29.1 0.0 copy-start.5
  29.1 0.0 all-to-all-done
  29.1 0.0 copy-start.1
  29.1 0.0 copy-done.4
  29.1 0.6 %copy-done.5 = f32[3,14,4,128]{3,2,1,0:T(4,128)} copy-done((f32[3,14,4,128]{3,2,1,0:T(4,128)}, f32[3,14,4,128]{3,2,1,0:T(4,128)S(1)}, u32[]{:S(2)}) %copy-start.5) | copy-done | bytes 86040
  29.7 0.1 copy-done.1
  29.8 2.7 %moments.1 = (f32[3,8,8,128]{3,2,1,0:T(8,128)}, f32[3,8,8,128]{3,2,1,0:T(8,128)}, f32[3,8,8,128]{3,2,1,0:T(8,128)}, f32[3,8,8,128]{3,2,1,0:T(8,128)}, f32[8,128]{1,0:T(8,128)}) custom-call(f32[4,8,128]{2,1,0:T(8,128)} %get-tuple-element.15.tiles, f32[2,4,4,8,128]{4,3,2,1,0:T(8,128)} %bitcast.5, f32[3,8,8,128]{3,2,1,0:T(8,128)} %source.3, ...), custom_call_target="tpu_custom_call" | custom-call | tf_op jit(solution)/shard_map/moments/pallas_call | solution.py:297
  32.5 0.7 %broadcast_in_dim.12 = f32[32,8,128]{2,1,0:T(8,128)S(1)} broadcast(f32[8,128]{1,0:T(8,128)} %get-tuple-element.17), dimensions={1,2} | broadcast | bytes 135168 | tf_op jit(solution)/shard_map/broadcast_in_dim | solution.py:372
  33.1 12.7 %all_to_all.10.parts = f32[32,8,128]{2,1,0:T(8,128)} all-to-all(f32[32,8,128]{2,1,0:T(8,128)S(1)} %broadcast_in_dim.12), channel_id=1, replica_groups=mesh['gx'=2,'gy'=4,'gz'=4] {'gx','gy','gz'}, dimensions={0} | all-to-all | bytes 262144 | tf_op jit(solution)/shard_map/all_to_all | solution.py:373
  45.9 2.0 %combine.1 = (f32[3,8,8,128]{3,2,1,0:T(8,128)}, f32[3,8,8,128]{3,2,1,0:T(8,128)}) custom-call(f32[32,8,128]{2,1,0:T(8,128)} %all_to_all.10.parts, f32[3,8,8,128]{3,2,1,0:T(8,128)} %get-tuple-element.18.v0, f32[3,8,8,128]{3,2,1,0:T(8,128)} %get-tuple-element.19.v1, f32[3,8,8,128]{3,2,1,0:T(8,128)} %get-tuple-element.20.v2, f32[3,8,8,128]{3,2,1,0:T(8,128)} %get-tuple-element.21.v3), custom_call_target="tpu_custom_call" | custom-call | tf_op jit(solution)/shard_map/combine/pallas_call | solution.py:297
  (3 shorter events, 0.0 us)
Async XLA Ops:
  0.6 3.8 %copy-start.6 = (f32[1,4,3,3,512]{4,1,3,2,0:T(4,128)S(1)}, f32[1,4,3,3,512]{4,1,3,2,0:T(4,128)}, u32[]{:S(2)}) copy-start(f32[1,4,3,3,512]{4,1,3,2,0:T(4,128)} %param.11) | copy-start | bytes 221188
  1.5 5.7 %collective-permute-start.1 = (f32[3,3,8,128]{3,2,1,0:T(8,128)S(1)}, f32[3,3,8,128]{3,2,1,0:T(8,128)S(1)}, u32[]{:S(2)}, u32[]{:S(2)}) collective-permute-start(f32[3,3,8,128]{3,2,1,0:T(8,128)S(1)} %slice_select_fusion), channel_id=1, source_target_pairs={{0,16},{16,0},{1,17},{17,1},{2,18},{18,2},{3,19},{19,3},{4,20},{20... | collective-permute-start | bytes 110600 | tf_op jit(solution)/shard_map/ppermute | solution.py:332
  4.4 4.4 %collective-permute-start = (f32[1,3,3,4,512]{4,3,2,1,0:T(4,128)S(1)}, f32[1,3,3,4,512]{4,3,2,1,0:T(4,128)S(1)}, u32[]{:S(2)}, u32[]{:S(2)}) collective-permute-start(f32[1,3,3,4,512]{4,3,2,1,0:T(4,128)S(1)} %bitcast.8), channel_id=1, source_target_pairs={{0,16},{16,0},{1,17},{17,1},{2,18},{18,2},{3,19},{19,3},{4,20},{20... | collective-permute-start | bytes 221192 | tf_op jit(solution)/shard_map/ppermute | solution.py:330
  7.2 0.9 %copy-start = (f32[3,8,8,128]{3,2,1,0:T(8,128)S(1)}, f32[3,8,8,128]{3,2,1,0:T(8,128)}, u32[]{:S(2)}) copy-start(f32[3,8,8,128]{3,2,1,0:T(8,128)} %source.3) | copy-start | bytes 294916
  7.2 0.9 %copy-start.2 = (f32[3,3,8,128]{3,2,1,0:T(8,128)}, f32[3,3,8,128]{3,2,1,0:T(8,128)S(1)}, u32[]{:S(2)}) copy-start(f32[3,3,8,128]{3,2,1,0:T(8,128)S(1)} %get-tuple-element.24.xhigh) | copy-start | bytes 110596
  7.2 0.9 %copy-start.3 = (f32[3,3,8,128]{3,2,1,0:T(8,128)}, f32[3,3,8,128]{3,2,1,0:T(8,128)S(1)}, u32[]{:S(2)}) copy-start(f32[3,3,8,128]{3,2,1,0:T(8,128)S(1)} %get-tuple-element.25.xlow) | copy-start | bytes 110596
  8.8 0.6 %copy-start.7 = (f32[1,3,3,4,512]{4,3,2,1,0:T(4,128)}, f32[1,3,3,4,512]{4,3,2,1,0:T(4,128)S(1)}, u32[]{:S(2)}) copy-start(f32[1,3,3,4,512]{4,3,2,1,0:T(4,128)S(1)} %collective-permute-done.other) | copy-start | bytes 221188
  13.4 15.7 %all-to-all-start = ((f32[32,8,128]{2,1,0:T(8,128)}), f32[32,8,128]{2,1,0:T(8,128)S(1)}, u32[]{:S(2)}, u32[]{:S(2)}) async-start(f32[32,8,128]{2,1,0:T(8,128)} %bitcast.6), calls=%async_computation | async-start | bytes 262144 | tf_op jit(solution)/shard_map/all_to_all | solution.py:357
  19.0 5.8 %collective-permute-start.2 = (f32[3,14,4,128]{3,2,1,0:T(4,128)S(1)}, f32[3,14,4,128]{3,2,1,0:T(4,128)S(1)}, u32[]{:S(2)}, u32[]{:S(2)}) collective-permute-start(f32[3,14,4,128]{3,2,1,0:T(4,128)S(1)} %get-tuple-element.23), channel_id=1, source_target_pairs={{0,4},{4,8},{8,12},{1,5},{5,9},{9,13},{2,6},{6,10},{10,14},{3,7},{... | collective-permute-start | bytes 258056 | tf_op jit(solution)/shard_map/ppermute | solution.py:315
  22.7 6.4 %collective-permute-start.3 = (f32[3,14,4,128]{3,2,1,0:T(4,128)S(1)}, f32[3,14,4,128]{3,2,1,0:T(4,128)S(1)}, u32[]{:S(2)}, u32[]{:S(2)}) collective-permute-start(f32[3,14,4,128]{3,2,1,0:T(4,128)S(1)} %get-tuple-element.22), channel_id=1, source_target_pairs={{4,0},{8,4},{12,8},{5,1},{9,5},{13,9},{6,2},{10,6},{14,10},{7,3},{... | collective-permute-start | bytes 258056 | tf_op jit(solution)/shard_map/ppermute | solution.py:315
  24.8 4.3 %copy-start.4 = (f32[3,14,4,128]{3,2,1,0:T(4,128)}, f32[3,14,4,128]{3,2,1,0:T(4,128)S(1)}, u32[]{:S(2)}) copy-start(f32[3,14,4,128]{3,2,1,0:T(4,128)S(1)} %collective-permute-done.2.ylow) | copy-start | bytes 258052
  29.1 0.6 %copy-start.5 = (f32[3,14,4,128]{3,2,1,0:T(4,128)}, f32[3,14,4,128]{3,2,1,0:T(4,128)S(1)}, u32[]{:S(2)}) copy-start(f32[3,14,4,128]{3,2,1,0:T(4,128)S(1)} %collective-permute-done.3.yhigh) | copy-start | bytes 258052
  29.1 0.7 %copy-start.1 = (f32[32,8,128]{2,1,0:T(8,128)}, f32[32,8,128]{2,1,0:T(8,128)S(1)}, u32[]{:S(2)}) copy-start(f32[32,8,128]{2,1,0:T(8,128)S(1)} %all-to-all-done) | copy-start | bytes 393220

commit v2 on v1

--- a/solution.py
+++ b/solution.py
@@ -7,6 +7,7 @@
 from jax.experimental import pallas as pl
 from jax.experimental.pallas import tpu as pltpu
 from jax.sharding import PartitionSpec as P
+
 
 CELL = 8
 VOX = 512
@@ -16,6 +17,7 @@
 AXES = ("gx", "gy", "gz")
 DENSE = 64
 SHIFT = 8.0
+GRANT = 16 * 1024 * 1024
 
 kerr_scale = 0.1
 
@@ -24,8 +26,15 @@
     return tuple(lax.axis_index(a) for a in AXES)
 
 
-def spectrum_kernel(contrast, point_field, hartley, spectrum, columns, polar):
+def spectrum_kernel(pair, count, contrast_in, field_in, class_in, kind_in, source_in, library_in,
+                    hartley, spectrum, columns, pick, contrast, source, library, polar, field, classes, kinds, sems):
     rows = contrast.shape[0]
+    moves = [(field_in, field), (class_in, classes), (kind_in, kinds), (contrast_in, contrast), (source_in, source)]
+    if pair:
+        moves.append((library_in, library))
+    moves = [pltpu.make_async_copy(a, b, sems.at[k]) for k, (a, b) in enumerate(moves)]
+    for move in moves:
+        move.start()
     step = CELL * CELL
     inner = lax.broadcasted_iota(jnp.int32, (step, VOX), 0)
     voxel = lax.broadcasted_iota(jnp.int32, (step, VOX), 1)
@@ -39,36 +48,40 @@
         size = jnp.where(quarter == 1, peak, jnp.where(quarter == 3, 0.0, plain))
         value = jnp.where(turn >= 4, -size, size)
         hartley[block * step : (block + 1) * step, :] = value.astype(jnp.bfloat16)
-    fields = point_field[...].astype(jnp.float32)
+    for move in moves[:3]:
+        move.wait()
+    fields = field[...].astype(jnp.float32)
     fields = jnp.concatenate([fields, jnp.zeros((5, rows), jnp.float32)], axis=0)
     columns[...] = fields.T
+    keys = jnp.where(classes[...] == lax.axis_index("gx"), 0, 1) if pair else classes[...]
+    keys = keys * TYPES + kinds[...]
+    named = (lax.broadcasted_iota(jnp.int32, (count, rows), 0) == keys).astype(jnp.float32)
+    named = jnp.concatenate([named, named], axis=0)
+    pick[...] = named.T.astype(jnp.bfloat16)
+    moves[3].wait()
     for j in range(3):
         e = columns[:, j : j + 1]
         m = contrast[:, j * VOX : (j + 1) * VOX].astype(jnp.float32)
         polar[j * rows : (j + 1) * rows, :] = (m * e).astype(jnp.bfloat16)
     spectrum[...] = jnp.dot(polar[...], hartley[...], preferred_element_type=jnp.float32)
-
-
-def solve_kernel(keep_class, contrast, columns, spectrum, hartley, point_class, cell_kind, library, other,
-                 source, tiles, bundle, mixing, stacked, product):
+    for move in moves[4:]:
+        move.wait()
+
+
+def solve_kernel(contrast, columns, spectrum, hartley, pick, library, other, source, tiles, bundle,
+                 mixing, stacked, product):
     rows = contrast.shape[0]
     zb = rows // 8
-    gx, _, gz = where_am_i()
-    keys = point_class[...] if keep_class else jnp.where(point_class[...] == gx, 0, 1)
-    keys = keys * TYPES + cell_kind[...]
-    count = library.shape[0] * TYPES * (1 if keep_class else 2)
-    pick = (lax.broadcasted_iota(jnp.int32, (count, rows), 0) == keys).astype(jnp.float32)
-    pick = jnp.concatenate([pick, pick], axis=0)
-    pick = pick.T.astype(jnp.bfloat16)
+    _, _, gz = where_am_i()
     for ij in range(9):
         i, j = ij // 3, ij % 3
         parts = [library[c, i, j] for c in range(library.shape[0])]
-        if not keep_class:
-            parts = parts + [other[c, i, j] for c in range(library.shape[0])]
+        if pick.shape[1] > 2 * TYPES * library.shape[0]:
+            parts = parts + [other[c, i, j] for c in range(other.shape[0])]
         table = jnp.concatenate(parts, axis=0)
         high = table.astype(jnp.bfloat16).astype(jnp.float32)
         both = jnp.concatenate([high, table - high], axis=0).astype(jnp.bfloat16)
-        mixing[ij] = jnp.dot(pick, both, preferred_element_type=jnp.float32)
+        mixing[ij] = jnp.dot(pick[...], both, preferred_element_type=jnp.float32)
 
     def mix(from_ref):
         for c in range(rows // 16):
@@ -245,17 +258,17 @@
                             acc[2 * level] = acc[2 * level] + value * value
                         if level == 1:
                             acc[0] = acc[0] + v[0] * v[0]
+    line = jnp.zeros((1, 128), jnp.float32)
+    slot = lax.broadcasted_iota(jnp.int32, (1, 128), 1)
     for k in range(6):
-        moments[k : k + 1, :] = jnp.sum(acc[k], axis=0, keepdims=True)
-    moments[6:8, :] = jnp.zeros((2, 128), jnp.float32)
+        sums = jnp.sum(jnp.sum(acc[k], axis=0, keepdims=True), axis=1, keepdims=True)
+        line = jnp.where(slot == k, sums, line)
+    moments[...] = jnp.broadcast_to(line[None], moments.shape)
 
 
 def combine_kernel(parts, v0, v1, v2, v3, step_out, residual_out):
-    total = parts[0]
-    for k in range(1, parts.shape[0]):
-        total = total + parts[k]
-    sums = jnp.sum(total, axis=1, keepdims=True)
-    nu = [sums[k : k + 1, :] for k in range(6)]
+    total = jnp.sum(parts[...], axis=0)
+    nu = [total[:, k : k + 1] for k in range(6)]
 
     def gram(a, b):
         result = None
@@ -292,16 +305,17 @@
             residual_out[c, x] = residual[0] * a + residual[1] * b + residual[2] * d + residual[3] * v3[c, x]
 
 
-def call(body, outs, ins, scratch=(), name=None):
+def call(body, outs, ins, scratch=(), last=False, raw=False):
     vmem = pl.BlockSpec(memory_space=pltpu.VMEM)
+    shape = jax.ShapeDtypeStruct if last else pltpu.VMEM
     return pl.pallas_call(
         body,
-        name=name,
-        out_shape=tuple(jax.ShapeDtypeStruct(s, d) for s, d in outs),
-        in_specs=[vmem] * len(ins),
+        out_shape=tuple(shape(s, d) for s, d in outs),
+        in_specs=[pl.BlockSpec(memory_space=pltpu.HBM) if raw else vmem] * len(ins),
         out_specs=tuple(vmem for _ in outs),
         scratch_shapes=list(scratch),
-    )(*ins)
+        compiler_params=pltpu.CompilerParams(vmem_limit_bytes=GRANT),
+    )(*(pltpu.with_memory_space_constraint(x, pltpu.HBM if raw else pltpu.VMEM) for x in ins))
 
 
 def ladder(axis):
@@ -312,19 +326,23 @@
 
 def from_both(low_face, high_face, axis):
     forward, backward = ladder(axis)
-    return lax.ppermute(high_face, axis, forward), lax.ppermute(low_face, axis, backward)
-
-
-def per_device(source, contrast, point_field, point_class, cell_kind, inverse_blocks):
+    up = lax.ppermute(high_face, axis, forward)
+    down = lax.ppermute(low_face, axis, backward)
+    return up, down
+
+
+def whole_step(source, contrast, point_field, point_class, cell_kind, inverse_blocks):
     f32, bf16 = jnp.float32, jnp.bfloat16
     rows = contrast.shape[0]
     counts = tuple(lax.axis_size(a) for a in AXES)
     nx, ny, nz = counts
+    devices = nx * ny * nz
     slabs = source.shape[1]
     gx = lax.axis_index("gx")
-    dense = nx * ny * nz <= DENSE
+    dense = devices <= DENSE
     pair = nx == 2
     library = inverse_blocks.transpose(0, 2, 3, 1, 4)
+    field = (source.shape, f32)
     if pair:
         swap = [(0, 1), (1, 0)]
         other = lax.ppermute(library, "gx", swap)
@@ -333,47 +351,44 @@
         xlow = jnp.where(gx == 1, face, 0.0)
         xhigh = jnp.where(gx == 0, face, 0.0)
     else:
-        library = lax.all_gather(library, "gx", axis=0, tiled=True)
-        other = library
+        other = lax.all_gather(library, "gx", axis=0, tiled=True)
         xlow, xhigh = from_both(source[:, :3], source[:, slabs - 3 :], "gx")
-    hartley, spectrum, columns = call(
-        spectrum_kernel,
-        [((VOX, VOX), bf16), ((3 * rows, VOX), f32), ((rows, 8), f32)],
-        (contrast, point_field),
-        [pltpu.VMEM((3 * rows, VOX), bf16)],
-        name="spectrum",
+    count = TYPES * nx
+    hartley, spectrum, columns, pick, contrast, source, library = call(
+        functools.partial(spectrum_kernel, pair, count),
+        [((VOX, VOX), bf16), ((3 * rows, VOX), f32), ((rows, 8), f32), ((rows, 2 * count), bf16),
+         (contrast.shape, bf16), field, (library.shape, f32)],
+        (contrast, point_field, point_class.reshape(1, rows), cell_kind.reshape(1, rows), source, library),
+        [pltpu.VMEM((3 * rows, VOX), bf16), pltpu.VMEM((3, rows), bf16), pltpu.VMEM((1, rows), jnp.int32),
+         pltpu.VMEM((1, rows), jnp.int32), pltpu.SemaphoreType.DMA((6,))],
+        raw=True,
     )
     longer = jnp.concatenate([xlow, source, xhigh], axis=1)
     ylow, yhigh = from_both(longer[:, :, :4], longer[:, :, 4:], "gy")
     tiles, bundle = call(
-        functools.partial(solve_kernel, not pair),
+        solve_kernel,
         [((4, 8, 128), f32), ((nx * ny if dense else 1, nz, 8, 128), f32)],
-        (contrast, columns, spectrum, hartley, point_class.reshape(1, rows), cell_kind.reshape(1, rows),
-         library, other, source),
+        (contrast, columns, spectrum, hartley, pick, library if pair else other, other, source),
         [pltpu.VMEM((9, rows, VOX), f32), pltpu.VMEM((3 * rows, VOX), bf16), pltpu.VMEM((3 * rows, VOX), f32)],
-        name="solve",
     )
     if dense:
-        got = lax.all_to_all(bundle.reshape(nx * ny * nz, 8, 128), AXES, 0, 0).reshape(nx, ny, nz, 8, 128)
+        got = lax.all_to_all(bundle.reshape(devices, 8, 128), AXES, 0, 0).reshape(nx, ny, nz, 8, 128)
     else:
         below, above = from_both(bundle[0], bundle[0], "gx")
         trio = jnp.stack([below, bundle[0], above], axis=1)
         trio = jnp.broadcast_to(trio[None], (ny,) + trio.shape).reshape(ny * nz, 3, 8, 128)
         got = lax.all_to_all(trio, ("gy", "gz"), 0, 0).reshape(ny, nz, 3, 8, 128).transpose(2, 0, 1, 3, 4)
-    field = (source.shape, f32)
     v0, v1, v2, v3, moments = call(
         functools.partial(moment_kernel, dense, counts),
-        [field, field, field, field, ((8, 128), f32)],
+        [field, field, field, field, ((devices if dense else 1, 1, 128), f32)],
         (tiles, got, source, xlow, xhigh, ylow, yhigh),
         [pltpu.VMEM((3, slabs + 6, 4, 8, 128), f32) for _ in range(3)],
-        name="moments",
     )
     if dense:
-        parts = jnp.broadcast_to(moments[None], (nx * ny * nz, 8, 128))
-        parts = lax.all_to_all(parts, AXES, 0, 0)
+        parts = lax.all_to_all(moments, AXES, 0, 0)
     else:
-        parts = lax.psum(moments, AXES)[None]
-    return call(combine_kernel, [field, field], (parts, v0, v1, v2, v3), name="combine")
+        parts = lax.psum(moments, AXES)
+    return call(combine_kernel, [field, field], (parts, v0, v1, v2, v3), last=True)
 
 
 def solution(mesh):
@@ -386,7 +401,7 @@
         P("gx", None, None, None, None),
     )
     return jax.shard_map(
-        per_device,
+        whole_step,
         mesh=mesh,
         in_specs=placed,
         out_specs=(P(None, "gx", "gy", "gz"), P(None, "gx", "gy", "gz")),

time: 48.3 us -> 39.9 us (0.83)
  Pallas kernels: 11.2 us -> 5.73 us
  local copies, waits for them, and re-layouts: 2.93 us -> 0.03 us
  waiting for transfers between devices: 5.78 us -> 7.81 us
  blocking collectives: 12.7 us -> 11.6 us
  starting transfers between devices: 13.6 us -> 12.9 us
    pallas_call x4, Pallas kernels: 11.2 us -> 5.73 us  [call(): pl.pallas_call(body, out_shape=tuple((shape(s, d) for s, d in outs)), in_...]
    unnamed x16 -> x2, local copies, waits for them, and re-layouts: 2.22 us -> 0.01 us
    ppermute x4, waiting for transfers between devices: 5.77 us -> 7.8 us  [the longest x1 4.3 us: from_both(): down = lax.ppermute(low_face, axis, backward)]
    all_to_all x1, blocking collectives: 12.7 us -> 11.6 us  [whole_step(): parts = lax.all_to_all(moments, AXES, 0, 0)]
    all_to_all x1, starting transfers between devices: 5.63 us -> 4.92 us  [whole_step(): lax.all_to_all(bundle.reshape(devices, 8, 128), AXES, 0, 0)]
    broadcast_in_dim x1 -> x0, local copies, waits for them, and re-layouts: 0.68 us -> none  [per_device(): parts = jnp.broadcast_to(moments[None], (nx * ny * nz, 8, 128))]
  transfers between devices with their start and end apart: 5 -> 5, of which waited for: 3 -> 4; matrix products, arithmetic and copies ran while one was open for 0% -> 0% of each run, Pallas kernels for 5% -> 4%
where the time goes in v2:
time: 39.9 us; the launch traced here: 39.7 us
  starting transfers between devices  12.9 us (32%)
  blocking collectives  11.6 us (29%)
  waiting for transfers between devices  7.81 us (20%)
  Pallas kernels  5.73 us (14%)
  other arithmetic  0.85 us (2%)
  between operations  0.7 us (2%)
    all_to_all x1, blocking collectives, whole_step(): parts = lax.all_to_all(moments, AXES, 0, 0)  11.6 us
    pallas_call x4, Pallas kernels, call(): pl.pallas_call(body, out_shape=tuple((shape(s, d) for s, d in outs)), in_...  5.73 us
    all_to_all x1, starting transfers between devices, whole_step(): lax.all_to_all(bundle.reshape(devices, 8, 128), AXES, 0, 0)  4.92 us
    ppermute x1, waiting for transfers between devices, from_both(): down = lax.ppermute(low_face, axis, backward)  4.3 us
    ppermute x1, starting transfers between devices, from_both(): up = lax.ppermute(high_face, axis, forward)  3.68 us
    ppermute x1, starting transfers between devices, whole_step(): face = lax.ppermute(face, 'gx', swap)  2.97 us
    ppermute x1, waiting for transfers between devices, whole_step(): other = lax.ppermute(library, 'gx', swap)  2.39 us
    ppermute x1, starting transfers between devices, from_both(): down = lax.ppermute(low_face, axis, backward)  1.29 us
  transfers between devices with their start and end apart: 5, of which 4 were waited for; matrix products, arithmetic and copies ran while one was open for 0% of the time, Pallas kernels for 4%

profile of v2, /device:TPU:0, one launch (start us, length us, event | category | flops | bytes accessed | tf_op | source)
XLA Modules:
  0.0 39.7 jit_solution(16739817927305241658)
XLA Ops:
  0.6 0.0 copy-start
  0.6 0.8 %slice_select_fusion = f32[3,3,8,128]{3,2,1,0:T(8,128)S(1)} fusion(f32[3,8,8,128]{3,2,1,0:T(8,128)} %source_in.1, pred[]{:T(512)S(6)} %eq.8), kind=kLoop, calls=%fused_computation.1 | loop fusion | flops 9216 | bytes 110593 | tf_op jit(solution)/shard_map/jit(_where)/select_n | solution.py:349
  1.5 3.0 %collective-permute-start.1 = (f32[3,3,8,128]{3,2,1,0:T(8,128)S(1)}, f32[3,3,8,128]{3,2,1,0:T(8,128)S(1)}, u32[]{:S(2)}, u32[]{:S(2)}) collective-permute-start(f32[3,3,8,128]{3,2,1,0:T(8,128)S(1)} %slice_select_fusion), channel_id=1, source_target_pairs={{0,16},{16,0},{1,17},{17,1},{2,18},{18,2},{3,19},{19,3},{4,20},{20... | collective-permute-start | bytes 110600 | tf_op jit(solution)/shard_map/ppermute | solution.py:350
  4.4 0.0 copy-done
  4.4 0.1 collective-permute-start
  4.5 1.5 %shard_map.77 = (bf16[512,512]{1,0:T(8,128)(2,1)S(1)}, f32[384,512]{1,0:T(8,128)S(1)}, f32[128,8]{1,0:T(8,128)S(1)}, bf16[128,16]{1,0:T(8,128)(2,1)S(1)}, bf16[1...) custom-call(bf16[128,1536]{1,0:T(8,128)(2,1)} %contrast_in.1, ...), custom_call_target="tpu_custom_call" | custom-call | tf_op jit(solution)/shard_map/pallas_call | solution.py:311
  6.0 0.3 collective-permute-done.1
  6.4 2.4 %collective-permute-done.other = f32[1,3,3,4,512]{4,3,2,1,0:T(4,128)S(1)} collective-permute-done((f32[1,3,3,4,512]{4,3,2,1,0:T(4,128)S(1)}, f32[1,3,3,4,512]{4,3,2,1,0:T(4,128)S(1)}, u32[]{:S(2)}, u32[]{:S(2)}) %collective-permute-start) | collective-permute-done | bytes 73760 | tf_op jit(solution)/shard_map/ppermute | solution.py:348
  8.8 2.3 %shard_map.78 = (f32[4,8,128]{2,1,0:T(8,128)S(1)}, f32[8,4,8,128]{3,2,1,0:T(8,128)}) custom-call(bf16[128,1536]{1,0:T(8,128)(2,1)S(1)} %get-tuple-element.16.contrast, f32[128,8]{1,0:T(8,128)S(1)} %get-tuple-element.17.columns, f32[384,512]{1,0:T(8,128)S(1)} %get-tuple-element.18.spectrum, bf16[512,512]{1,0:T(8,128)(2,1)S(1)} %get-tuple-element.19.hartley, ...), custom_call_target="tpu_custom_call" | custom-call | tf_op jit(solution)/shard_map/pallas_call | solution.py:311
  11.1 4.9 %all-to-all-start = ((f32[32,8,128]{2,1,0:T(8,128)}), f32[32,8,128]{2,1,0:T(8,128)S(1)}, u32[]{:S(2)}, u32[]{:S(2)}) async-start(f32[32,8,128]{2,1,0:T(8,128)} %bitcast.3), calls=%async_computation | async-start | bytes 262144 | tf_op jit(solution)/shard_map/all_to_all | solution.py:375
  16.1 3.7 %collective-permute-start.2 = (f32[3,14,4,128]{3,2,1,0:T(4,128)S(1)}, f32[3,14,4,128]{3,2,1,0:T(4,128)S(1)}, u32[]{:S(2)}, u32[]{:S(2)}) collective-permute-start(f32[3,14,4,128]{3,2,1,0:T(4,128)S(1)} %get-tuple-element.31), channel_id=1, source_target_pairs={{0,4},{4,8},{8,12},{1,5},{5,9},{9,13},{2,6},{6,10},{10,14},{3,7},{... | collective-permute-start | bytes 258056 | tf_op jit(solution)/shard_map/ppermute | solution.py:329
  19.8 1.3 %collective-permute-start.3 = (f32[3,14,4,128]{3,2,1,0:T(4,128)S(1)}, f32[3,14,4,128]{3,2,1,0:T(4,128)S(1)}, u32[]{:S(2)}, u32[]{:S(2)}) collective-permute-start(f32[3,14,4,128]{3,2,1,0:T(4,128)S(1)} %get-tuple-element.30), channel_id=1, source_target_pairs={{4,0},{8,4},{12,8},{5,1},{9,5},{13,9},{6,2},{10,6},{14,10},{7,3},{... | collective-permute-start | bytes 258056 | tf_op jit(solution)/shard_map/ppermute | solution.py:330
  21.1 0.8 %collective-permute-done.2.ylow = f32[3,14,4,128]{3,2,1,0:T(4,128)S(1)} collective-permute-done((f32[3,14,4,128]{3,2,1,0:T(4,128)S(1)}, f32[3,14,4,128]{3,2,1,0:T(4,128)S(1)}, u32[]{:S(2)}, u32[]{:S(2)}) %collective-permute-start.2) | collective-permute-done | bytes 86048 | tf_op jit(solution)/shard_map/ppermute | solution.py:329
  21.8 4.3 %collective-permute-done.3.yhigh = f32[3,14,4,128]{3,2,1,0:T(4,128)S(1)} collective-permute-done((f32[3,14,4,128]{3,2,1,0:T(4,128)S(1)}, f32[3,14,4,128]{3,2,1,0:T(4,128)S(1)}, u32[]{:S(2)}, u32[]{:S(2)}) %collective-permute-start.3) | collective-permute-done | bytes 86048 | tf_op jit(solution)/shard_map/ppermute | solution.py:330
  26.1 0.0 all-to-all-done
  26.1 1.0 %shard_map.79 = (f32[3,8,8,128]{3,2,1,0:T(8,128)S(1)}, f32[3,8,8,128]{3,2,1,0:T(8,128)S(1)}, f32[3,8,8,128]{3,2,1,0:T(8,128)S(1)}, f32[3,8,8,128]{3,2,1,0:T(8,128)S(1)}, f32[32,1,128]{2,1,0:T(1,128)S(1)}) custom-call(f32[4,8,128]{2,1,0:T(8,128)S(1)} %get-tuple-element.23.tiles, f32[2,4,4,8,128]{4,3,2,1,0:T(8,128)S(1)} %bitcast.5, ...), custom_call_target="tpu_custom_call" | custom-call | tf_op jit(solution)/shard_map/pallas_call | solution.py:311
  27.2 11.6 %all_to_all.10.parts = f32[32,1,128]{2,1,0:T(1,128)S(1)} all-to-all(f32[32,1,128]{2,1,0:T(1,128)S(1)} %get-tuple-element.25), channel_id=1, replica_groups=mesh['gx'=2,'gy'=4,'gz'=4] {'gx','gy','gz'}, dimensions={0} | all-to-all | bytes 32768 | tf_op jit(solution)/shard_map/all_to_all | solution.py:388
  38.8 0.9 %shard_map.80 = (f32[3,8,8,128]{3,2,1,0:T(8,128)}, f32[3,8,8,128]{3,2,1,0:T(8,128)}) custom-call(f32[32,1,128]{2,1,0:T(1,128)S(1)} %all_to_all.10.parts, f32[3,8,8,128]{3,2,1,0:T(8,128)S(1)} %get-tuple-element.26.v0, f32[3,8,8,128]{3,2,1,0:T(8,128)S(1)} %get-tuple-element.27.v1, f32[3,8,8,128]{3,2,1,0:T(8,128)S(1)} %get-tuple-element.28.v2, ...), custom_call_target="tpu_custom_call" | custom-call | tf_op jit(solution)/shard_map/pallas_call | solution.py:311
  (3 shorter events, 0.1 us)
Async XLA Ops:
  0.6 3.8 %copy-start = (f32[1,4,3,3,512]{4,1,3,2,0:T(4,128)S(1)}, f32[1,4,3,3,512]{4,1,3,2,0:T(4,128)}, u32[]{:S(2)}) copy-start(f32[1,4,3,3,512]{4,1,3,2,0:T(4,128)} %param.11) | copy-start | bytes 221188
  1.5 4.9 %collective-permute-start.1 = (f32[3,3,8,128]{3,2,1,0:T(8,128)S(1)}, f32[3,3,8,128]{3,2,1,0:T(8,128)S(1)}, u32[]{:S(2)}, u32[]{:S(2)}) collective-permute-start(f32[3,3,8,128]{3,2,1,0:T(8,128)S(1)} %slice_select_fusion), channel_id=1, source_target_pairs={{0,16},{16,0},{1,17},{17,1},{2,18},{18,2},{3,19},{19,3},{4,20},{20... | collective-permute-start | bytes 110600 | tf_op jit(solution)/shard_map/ppermute | solution.py:350
  4.4 4.4 %collective-permute-start = (f32[1,3,3,4,512]{4,3,2,1,0:T(4,128)S(1)}, f32[1,3,3,4,512]{4,3,2,1,0:T(4,128)S(1)}, u32[]{:S(2)}, u32[]{:S(2)}) collective-permute-start(f32[1,3,3,4,512]{4,3,2,1,0:T(4,128)S(1)} %bitcast.7), channel_id=1, source_target_pairs={{0,16},{16,0},{1,17},{17,1},{2,18},{18,2},{3,19},{19,3},{4,20},{20... | collective-permute-start | bytes 221192 | tf_op jit(solution)/shard_map/ppermute | solution.py:348
  11.1 15.0 %all-to-all-start = ((f32[32,8,128]{2,1,0:T(8,128)}), f32[32,8,128]{2,1,0:T(8,128)S(1)}, u32[]{:S(2)}, u32[]{:S(2)}) async-start(f32[32,8,128]{2,1,0:T(8,128)} %bitcast.3), calls=%async_computation | async-start | bytes 262144 | tf_op jit(solution)/shard_map/all_to_all | solution.py:375
  16.1 5.8 %collective-permute-start.2 = (f32[3,14,4,128]{3,2,1,0:T(4,128)S(1)}, f32[3,14,4,128]{3,2,1,0:T(4,128)S(1)}, u32[]{:S(2)}, u32[]{:S(2)}) collective-permute-start(f32[3,14,4,128]{3,2,1,0:T(4,128)S(1)} %get-tuple-element.31), channel_id=1, source_target_pairs={{0,4},{4,8},{8,12},{1,5},{5,9},{9,13},{2,6},{6,10},{10,14},{3,7},{... | collective-permute-start | bytes 258056 | tf_op jit(solution)/shard_map/ppermute | solution.py:329
  19.8 6.4 %collective-permute-start.3 = (f32[3,14,4,128]{3,2,1,0:T(4,128)S(1)}, f32[3,14,4,128]{3,2,1,0:T(4,128)S(1)}, u32[]{:S(2)}, u32[]{:S(2)}) collective-permute-start(f32[3,14,4,128]{3,2,1,0:T(4,128)S(1)} %get-tuple-element.30), channel_id=1, source_target_pairs={{4,0},{8,4},{12,8},{5,1},{9,5},{13,9},{6,2},{10,6},{14,10},{7,3},{... | collective-permute-start | bytes 258056 | tf_op jit(solution)/shard_map/ppermute | solution.py:330

commit v3 on v2

--- a/solution.py
+++ b/solution.py
@@ -27,9 +27,13 @@
 
 
 def spectrum_kernel(pair, count, contrast_in, field_in, class_in, kind_in, source_in, library_in,
-                    hartley, spectrum, columns, pick, contrast, source, library, polar, field, classes, kinds, sems):
+                    hartley, spectrum, columns, pick, contrast, source, library, face,
+                    polar, field, classes, kinds, plain_source, sems):
     rows = contrast.shape[0]
-    moves = [(field_in, field), (class_in, classes), (kind_in, kinds), (contrast_in, contrast), (source_in, source)]
+    slabs = source.shape[1]
+    gx = lax.axis_index("gx")
+    moves = [(field_in, field), (class_in, classes), (kind_in, kinds), (contrast_in, contrast),
+             (source_in, plain_source)]
     if pair:
         moves.append((library_in, library))
     moves = [pltpu.make_async_copy(a, b, sems.at[k]) for k, (a, b) in enumerate(moves)]
@@ -53,7 +57,7 @@
     fields = field[...].astype(jnp.float32)
     fields = jnp.concatenate([fields, jnp.zeros((5, rows), jnp.float32)], axis=0)
     columns[...] = fields.T
-    keys = jnp.where(classes[...] == lax.axis_index("gx"), 0, 1) if pair else classes[...]
+    keys = jnp.where(classes[...] == gx, 0, 1) if pair else classes[...]
     keys = keys * TYPES + kinds[...]
     named = (lax.broadcasted_iota(jnp.int32, (count, rows), 0) == keys).astype(jnp.float32)
     named = jnp.concatenate([named, named], axis=0)
@@ -66,6 +70,13 @@
     spectrum[...] = jnp.dot(polar[...], hartley[...], preferred_element_type=jnp.float32)
     for move in moves[4:]:
         move.wait()
+    for p in range(slabs):
+        x = jnp.where(gx == 0, p, slabs - 1 - p) if pair else p
+        for c in range(3):
+            value = plain_source[c, x]
+            source[c, p] = value
+            if p >= slabs - 3:
+                face[c, slabs - 1 - p] = value
 
 
 def solve_kernel(contrast, columns, spectrum, hartley, pick, library, other, source, tiles, bundle,
@@ -147,12 +158,15 @@
             bundle[x, d] = tile
 
 
-def moment_kernel(dense, counts, tiles, got, source, xlow, xhigh, ylow, yhigh, v0, v1, v2, v3, moments, w0, w1, w2):
+def moment_kernel(dense, counts, tiles, got, source, xlow, xhigh, ya, yb, v0, v1, v2, v3, moments, w0, w1, w2):
     slabs = source.shape[1]
     gx, gy, gz = where_am_i()
     nx, ny, nz = counts
+    pair = nx == 2
+    base = 0 if pair else 3
     row = lax.broadcasted_iota(jnp.int32, (8, 128), 0)
     lane = lax.broadcasted_iota(jnp.int32, (8, 128), 1)
+    even = gy % 2 == 0
     has_xl, has_xh = gx > 0, gx < nx - 1
     has_yl, has_yh = gy > 0, gy < ny - 1
     has_zl, has_zh = gz > 0, gz < nz - 1
@@ -162,7 +176,9 @@
     masks = (None, mask_y, mask_z, mask_y * mask_z)
     yl, yh = jnp.maximum(gy - 1, 0), jnp.minimum(gy + 1, ny - 1)
     zl, zh = jnp.maximum(gz - 1, 0), jnp.minimum(gz + 1, nz - 1)
-    if dense:
+    if pair:
+        regions = (None, gx, 1 - gx)
+    elif dense:
         regions = (jnp.maximum(gx - 1, 0), gx, jnp.minimum(gx + 1, nx - 1))
     else:
         regions = (0, 1, 2)
@@ -180,7 +196,8 @@
 
     diag = {}
     flux = {}
-    for r in range(3):
+    edges = {1: None, 2: None} if pair else {0: one(has_xl), 1: None, 2: one(has_xh)}
+    for r in edges:
         x = regions[r]
         rowtile = jnp.where(upper, got[x, yh, gz], got[x, yl, gz])
         flux[r, 1] = [unfold(rowtile, t) for t in range(3)]
@@ -196,18 +213,21 @@
         corner_high = jnp.where(upper, got[x, yh, zh], got[x, yl, zh])
         diag[r, 2] = pull(side_low, side_high, 3 * slabs)
         diag[r, 3] = pull(corner_low, corner_high, 3 * slabs)
-        edge_x = None if r == 1 else one(has_xl if r == 0 else has_xh)
+        edge_x = edges[r]
         for c in range(3):
-            for k in range(3 if r != 1 else slabs):
-                at = k if r == 0 else (3 + k if r == 1 else 3 + slabs + k)
+            for k in range(slabs if r == 1 else 3):
+                at = k if r == 0 else (base + k if r == 1 else base + slabs + k)
                 out = (3 - k) if r == 0 else (0 if r == 1 else k + 1)
-                s = c * slabs + (slabs - 3 + k if r == 0 else k)
+                s = slabs - 3 + k if r == 0 else (slabs - 1 - k if pair and r == 2 else k)
+                s = c * slabs + s
                 value = (source if r == 1 else (xlow if r == 0 else xhigh))[c, k] - flux[r, 0][c]
                 w0[c, at, 0] = value if edge_x is None else value * edge_x
                 if r == 1:
                     v0[c, k] = value
                 if out <= 2:
-                    halo = jnp.concatenate([yhigh[c, at], ylow[c, at]], axis=0) - flux[r, 1][c]
+                    a, b = ya[c, at], yb[c, at]
+                    halo = jnp.concatenate([jnp.where(even, a, b), jnp.where(even, b, a)], axis=0)
+                    halo = halo - flux[r, 1][c]
                     w0[c, at, 1] = halo * (mask_y if edge_x is None else mask_y * edge_x)
                     value = pull(side_low, side_high, s)
                     w0[c, at, 2] = value * (mask_z if edge_x is None else mask_z * edge_x)
@@ -226,9 +246,9 @@
         src, dst = levels[level - 1], levels[level]
         reach = 3 - level
         for c in range(3):
-            for at in range(3 - reach, 3 + slabs + reach):
-                out = max(3 - at, at - slabs - 2, 0)
-                r = 0 if at < 3 else (1 if at < 3 + slabs else 2)
+            for at in range(max(base - reach, 0), base + slabs + reach):
+                out = max(base - at, at - base - slabs + 1, 0)
+                r = 0 if at < base else (1 if at < base + slabs else 2)
                 depth = reach - out
                 want = (0,) if depth == 0 else ((0, 1, 2) if depth == 1 else (0, 1, 2, 3))
                 have = (0, 1, 2) if depth == 0 else (0, 1, 2, 3)
@@ -237,13 +257,15 @@
                 right = {t: pltpu.roll(v[t], 1, 1) for t in have if t in (0, 2) or depth > 0}
                 down = {t: pltpu.roll(v[t], 7, 0) for t in have if t in (0, 1) or depth > 0}
                 over = {t: pltpu.roll(v[t], 1, 0) for t in have if t in (0, 1) or depth > 0}
-                edge_x = None if r == 1 else one(has_xl if r == 0 else has_xh)
+                edge_x = edges[r]
                 for t in want:
                     zp = jnp.where(last_lane, left[t ^ 2], left[t])
                     zm = jnp.where(first_lane, right[t ^ 2], right[t])
                     yp = jnp.where(last_row, down[t ^ 1], down[t])
                     ym = jnp.where(first_row, over[t ^ 1], over[t])
-                    beside = (src[c, at - 1, t] + src[c, at + 1, t]) + (zp + zm) + (yp + ym)
+                    beside = src[c, at + 1, t] + (zp + zm) + (yp + ym)
+                    if at > 0:
+                        beside = beside + src[c, at - 1, t]
                     value = diag[r, t] * v[t] - beside
                     if masks[t] is not None:
                         value = value * masks[t]
@@ -252,7 +274,7 @@
                     if dst is not None:
                         dst[c, at, t] = value
                     if t == 0 and r == 1:
-                        results[level][c, at - 3] = value
+                        results[level][c, at - base] = value
                         acc[2 * level - 1] = acc[2 * level - 1] + v[0] * value
                         if level < 3:
                             acc[2 * level] = acc[2 * level] + value * value
@@ -266,7 +288,7 @@
     moments[...] = jnp.broadcast_to(line[None], moments.shape)
 
 
-def combine_kernel(parts, v0, v1, v2, v3, step_out, residual_out):
+def combine_kernel(pair, parts, v0, v1, v2, v3, step_out, residual_out):
     total = jnp.sum(parts[...], axis=0)
     nu = [total[:, k : k + 1] for k in range(6)]
 
@@ -301,8 +323,9 @@
     for c in range(v0.shape[0]):
         for x in range(v0.shape[1]):
             a, b, d = v0[c, x], v1[c, x], v2[c, x]
-            step_out[c, x] = newton[0] * a + newton[1] * b + newton[2] * d
-            residual_out[c, x] = residual[0] * a + residual[1] * b + residual[2] * d + residual[3] * v3[c, x]
+            to = jnp.where(lax.axis_index("gx") == 0, x, v0.shape[1] - 1 - x) if pair else x
+            step_out[c, to] = newton[0] * a + newton[1] * b + newton[2] * d
+            residual_out[c, to] = residual[0] * a + residual[1] * b + residual[2] * d + residual[3] * v3[c, x]
 
 
 def call(body, outs, ins, scratch=(), last=False, raw=False):
@@ -324,6 +347,11 @@
     return forward, [(b, a) for a, b in forward]
 
 
+def pairs_from(first, count):
+    couples = [(i, i + 1) for i in range(first, count - 1, 2)]
+    return couples + [(b, a) for a, b in couples]
+
+
 def from_both(low_face, high_face, axis):
     forward, backward = ladder(axis)
     up = lax.ppermute(high_face, axis, forward)
@@ -338,7 +366,6 @@
     nx, ny, nz = counts
     devices = nx * ny * nz
     slabs = source.shape[1]
-    gx = lax.axis_index("gx")
     dense = devices <= DENSE
     pair = nx == 2
     library = inverse_blocks.transpose(0, 2, 3, 1, 4)
@@ -346,25 +373,29 @@
     if pair:
         swap = [(0, 1), (1, 0)]
         other = lax.ppermute(library, "gx", swap)
-        face = jnp.where(gx == 0, source[:, slabs - 3 :], source[:, :3])
-        face = lax.ppermute(face, "gx", swap)
-        xlow = jnp.where(gx == 1, face, 0.0)
-        xhigh = jnp.where(gx == 0, face, 0.0)
     else:
         other = lax.all_gather(library, "gx", axis=0, tiled=True)
-        xlow, xhigh = from_both(source[:, :3], source[:, slabs - 3 :], "gx")
     count = TYPES * nx
-    hartley, spectrum, columns, pick, contrast, source, library = call(
+    hartley, spectrum, columns, pick, contrast, source, library, face = call(
         functools.partial(spectrum_kernel, pair, count),
         [((VOX, VOX), bf16), ((3 * rows, VOX), f32), ((rows, 8), f32), ((rows, 2 * count), bf16),
-         (contrast.shape, bf16), field, (library.shape, f32)],
+         (contrast.shape, bf16), field, (library.shape, f32), ((3, 3, 8, 128), f32)],
         (contrast, point_field, point_class.reshape(1, rows), cell_kind.reshape(1, rows), source, library),
         [pltpu.VMEM((3 * rows, VOX), bf16), pltpu.VMEM((3, rows), bf16), pltpu.VMEM((1, rows), jnp.int32),
-         pltpu.VMEM((1, rows), jnp.int32), pltpu.SemaphoreType.DMA((6,))],
+         pltpu.VMEM((1, rows), jnp.int32), pltpu.VMEM(*field), pltpu.SemaphoreType.DMA((6,))],
         raw=True,
     )
-    longer = jnp.concatenate([xlow, source, xhigh], axis=1)
-    ylow, yhigh = from_both(longer[:, :, :4], longer[:, :, 4:], "gy")
+    if pair:
+        face = lax.ppermute(face, "gx", swap)
+        xlow = xhigh = face
+        longer = jnp.concatenate([source, face[:, :2]], axis=1)
+    else:
+        xlow, xhigh = from_both(source[:, :3], source[:, slabs - 3 :], "gx")
+        longer = jnp.concatenate([xlow, source, xhigh], axis=1)
+    even = lax.axis_index("gy") % 2 == 0
+    low_rows, high_rows = longer[:, :, :4], longer[:, :, 4:]
+    ya = lax.ppermute(jnp.where(even, high_rows, low_rows), "gy", pairs_from(0, ny))
+    yb = lax.ppermute(jnp.where(even, low_rows, high_rows), "gy", pairs_from(1, ny))
     tiles, bundle = call(
         solve_kernel,
         [((4, 8, 128), f32), ((nx * ny if dense else 1, nz, 8, 128), f32)],
@@ -381,14 +412,14 @@
     v0, v1, v2, v3, moments = call(
         functools.partial(moment_kernel, dense, counts),
         [field, field, field, field, ((devices if dense else 1, 1, 128), f32)],
-        (tiles, got, source, xlow, xhigh, ylow, yhigh),
-        [pltpu.VMEM((3, slabs + 6, 4, 8, 128), f32) for _ in range(3)],
+        (tiles, got, source, xlow, xhigh, ya, yb),
+        [pltpu.VMEM((3, slabs + (3 if pair else 6), 4, 8, 128), f32) for _ in range(3)],
     )
     if dense:
         parts = lax.all_to_all(moments, AXES, 0, 0)
     else:
         parts = lax.psum(moments, AXES)
-    return call(combine_kernel, [field, field], (parts, v0, v1, v2, v3), last=True)
+    return call(functools.partial(combine_kernel, pair), [field, field], (parts, v0, v1, v2, v3), last=True)
 
 
 def solution(mesh):

time: 39.9 us -> 40.7 us (1.020)
  blocking collectives: 11.6 us -> 15.3 us
  waiting for transfers between devices: 7.81 us -> 5.12 us
  starting transfers between devices: 12.9 us -> 13.8 us
  other arithmetic: 0.85 us -> 0.02 us
    all_to_all x1, blocking collectives: 11.6 us -> 15.3 us  [whole_step(): parts = lax.all_to_all(moments, AXES, 0, 0)]
    ppermute x2, waiting for transfers between devices: 5.08 us -> 1.75 us  [the longest x1 1.75 us: whole_step(): lax.ppermute(jnp.where(even, high_rows, low_rows), 'gy', pairs_from(0, ny))]
    ppermute x1, starting transfers between devices: 0.07 us -> 3.03 us  [whole_step(): other = lax.ppermute(library, 'gx', swap)]
    ppermute x2, starting transfers between devices: 4.97 us -> 2.53 us  [the longest x1 1.88 us: whole_step(): lax.ppermute(jnp.where(even, high_rows, low_rows), 'gy', pairs_from(0, ny))]
    ppermute x1, waiting for transfers between devices: 0.34 us -> 2.37 us  [whole_step(): face = lax.ppermute(face, 'gx', swap)]
    all_to_all x1, starting transfers between devices: 4.92 us -> 6.38 us  [whole_step(): lax.all_to_all(bundle.reshape(devices, 8, 128), AXES, 0, 0)]
    ppermute x1, waiting for transfers between devices: 2.39 us -> 1.01 us  [whole_step(): other = lax.ppermute(library, 'gx', swap)]
    ppermute x1, starting transfers between devices: 2.97 us -> 1.83 us  [whole_step(): face = lax.ppermute(face, 'gx', swap)]
  transfers between devices with their start and end apart: 5 -> 5, of which waited for: 4 -> 3; matrix products, arithmetic and copies ran while one was open for 0% -> 0% of each run, Pallas kernels for 4% -> 4%
where the time goes in v3:
time: 40.7 us; the launch traced here: 40.5 us
  blocking collectives  15.3 us (38%)
  starting transfers between devices  13.8 us (34%)
  Pallas kernels  5.68 us (14%)
  waiting for transfers between devices  5.12 us (13%)
  between operations  0.67 us (2%)
    all_to_all x1, blocking collectives, whole_step(): parts = lax.all_to_all(moments, AXES, 0, 0)  15.3 us
    all_to_all x1, starting transfers between devices, whole_step(): lax.all_to_all(bundle.reshape(devices, 8, 128), AXES, 0, 0)  6.38 us
    pallas_call x4, Pallas kernels, call(): pl.pallas_call(body, out_shape=tuple((shape(s, d) for s, d in outs)), in_...  5.68 us
    ppermute x1, starting transfers between devices, whole_step(): other = lax.ppermute(library, 'gx', swap)  3.03 us
    ppermute x1, waiting for transfers between devices, whole_step(): face = lax.ppermute(face, 'gx', swap)  2.37 us
    ppermute x1, starting transfers between devices, whole_step(): lax.ppermute(jnp.where(even, high_rows, low_rows), 'gy', pairs_from(0, ny))  1.88 us
    ppermute x1, starting transfers between devices, whole_step(): face = lax.ppermute(face, 'gx', swap)  1.83 us
    ppermute x1, waiting for transfers between devices, whole_step(): lax.ppermute(jnp.where(even, high_rows, low_rows), 'gy', pairs_from(0, ny))  1.75 us
  transfers between devices with their start and end apart: 5, of which 3 were waited for; matrix products, arithmetic and copies ran while one was open for 0% of the time, Pallas kernels for 4%

profile of v3, /device:TPU:0, one launch (start us, length us, event | category | flops | bytes accessed | tf_op | source)
XLA Modules:
  0.0 40.5 jit_solution(5356553195156307712)
XLA Ops:
  0.6 3.0 %collective-permute-start = (f32[1,3,3,4,512]{4,3,2,1,0:T(4,128)}, f32[1,3,3,4,512]{4,3,2,1,0:T(4,128)S(1)}, u32[]{:S(2)}, u32[]{:S(2)}) collective-permute-start(f32[1,3,3,4,512]{4,3,2,1,0:T(4,128)} %bitcast.6), channel_id=1, source_target_pairs={{0,16},{16,0},{1,17},{17,1},{2,18},{18,2},{3,19},{19,3},{4,20},{20... | collective-permute-start | bytes 221192 | tf_op jit(solution)/shard_map/ppermute | solution.py:375
  3.7 1.5 %shard_map.77 = (bf16[512,512]{1,0:T(8,128)(2,1)S(1)}, f32[384,512]{1,0:T(8,128)S(1)}, f32[128,8]{1,0:T(8,128)S(1)}, bf16[128,16]{1,0:T(8,128)(2,1)S(1)}, bf16[1...) custom-call(bf16[128,1536]{1,0:T(8,128)(2,1)} %contrast_in.1, ...), custom_call_target="tpu_custom_call" | custom-call | tf_op jit(solution)/shard_map/pallas_call | solution.py:334
  5.2 1.0 %collective-permute-done.other = f32[1,3,3,4,512]{4,3,2,1,0:T(4,128)S(1)} collective-permute-done((f32[1,3,3,4,512]{4,3,2,1,0:T(4,128)}, f32[1,3,3,4,512]{4,3,2,1,0:T(4,128)S(1)}, u32[]{:S(2)}, u32[]{:S(2)}) %collective-permute-start) | collective-permute-done | bytes 73760 | tf_op jit(solution)/shard_map/ppermute | solution.py:375
  6.2 2.3 %shard_map.78 = (f32[4,8,128]{2,1,0:T(8,128)S(1)}, f32[8,4,8,128]{3,2,1,0:T(8,128)}) custom-call(bf16[128,1536]{1,0:T(8,128)(2,1)S(1)} %get-tuple-element.17.contrast, f32[128,8]{1,0:T(8,128)S(1)} %get-tuple-element.18.columns, f32[384,512]{1,0:T(8,128)S(1)} %get-tuple-element.19.spectrum, bf16[512,512]{1,0:T(8,128)(2,1)S(1)} %get-tuple-element.20.hartley, ...), custom_call_target="tpu_custom_call" | custom-call | tf_op jit(solution)/shard_map/pallas_call | solution.py:334
  8.5 6.4 %all-to-all-start = ((f32[32,8,128]{2,1,0:T(8,128)}), f32[32,8,128]{2,1,0:T(8,128)S(1)}, u32[]{:S(2)}, u32[]{:S(2)}) async-start(f32[32,8,128]{2,1,0:T(8,128)} %bitcast.3), calls=%async_computation | async-start | bytes 262144 | tf_op jit(solution)/shard_map/all_to_all | solution.py:406
  14.9 1.8 %collective-permute-start.1 = (f32[3,3,8,128]{3,2,1,0:T(8,128)S(1)}, f32[3,3,8,128]{3,2,1,0:T(8,128)S(1)}, u32[]{:S(2)}, u32[]{:S(2)}) collective-permute-start(f32[3,3,8,128]{3,2,1,0:T(8,128)S(1)} %get-tuple-element.26), channel_id=1, source_target_pairs={{0,16},{16,0},{1,17},{17,1},{2,18},{18,2},{3,19},{19,3},{4,20},{20... | collective-permute-start | bytes 110600 | tf_op jit(solution)/shard_map/ppermute | solution.py:389
  16.7 2.4 %collective-permute-done.1.xlow.xhigh = f32[3,3,8,128]{3,2,1,0:T(8,128)S(1)} collective-permute-done((f32[3,3,8,128]{3,2,1,0:T(8,128)S(1)}, f32[3,3,8,128]{3,2,1,0:T(8,128)S(1)}, u32[]{:S(2)}, u32[]{:S(2)}) %collective-permute-start.1) | collective-permute-done | bytes 36896 | tf_op jit(solution)/shard_map/ppermute | solution.py:389
  19.1 1.9 %collective-permute-start.2 = (f32[3,10,4,128]{3,2,1,0:T(4,128)S(1)}, f32[3,10,4,128]{3,2,1,0:T(4,128)S(1)}, u32[]{:S(2)}, u32[]{:S(2)}) collective-permute-start(f32[3,10,4,128]{3,2,1,0:T(4,128)S(1)} %get-tuple-element.33), channel_id=1, source_target_pairs={{0,4},{8,12},{4,0},{12,8},{1,5},{9,13},{5,1},{13,9},{2,6},{10,14},... | collective-permute-start | bytes 184328 | tf_op jit(solution)/shard_map/ppermute | solution.py:397
  21.0 0.7 %collective-permute-start.3 = (f32[3,10,4,128]{3,2,1,0:T(4,128)S(1)}, f32[3,10,4,128]{3,2,1,0:T(4,128)S(1)}, u32[]{:S(2)}, u32[]{:S(2)}) collective-permute-start(f32[3,10,4,128]{3,2,1,0:T(4,128)S(1)} %get-tuple-element.32), channel_id=1, source_target_pairs={{4,8},{8,4},{5,9},{9,5},{6,10},{10,6},{7,11},{11,7},{20,24},{24,20... | collective-permute-start | bytes 184328 | tf_op jit(solution)/shard_map/ppermute | solution.py:398
  21.7 1.7 %collective-permute-done.2.ya = f32[3,10,4,128]{3,2,1,0:T(4,128)S(1)} collective-permute-done((f32[3,10,4,128]{3,2,1,0:T(4,128)S(1)}, f32[3,10,4,128]{3,2,1,0:T(4,128)S(1)}, u32[]{:S(2)}, u32[]{:S(2)}) %collective-permute-start.2) | collective-permute-done | bytes 61472 | tf_op jit(solution)/shard_map/ppermute | solution.py:397
  23.4 0.0 collective-permute-done.3.yb
  23.4 0.0 all-to-all-done
  23.4 0.9 %shard_map.79 = (f32[3,8,8,128]{3,2,1,0:T(8,128)S(1)}, f32[3,8,8,128]{3,2,1,0:T(8,128)S(1)}, f32[3,8,8,128]{3,2,1,0:T(8,128)S(1)}, f32[3,8,8,128]{3,2,1,0:T(8,128)S(1)}, f32[32,1,128]{2,1,0:T(1,128)S(1)}) custom-call(f32[4,8,128]{2,1,0:T(8,128)S(1)} %get-tuple-element.24.tiles, f32[2,4,4,8,128]{4,3,2,1,0:T(8,128)S(1)} %bitcast.5, ...), custom_call_target="tpu_custom_call" | custom-call | tf_op jit(solution)/shard_map/pallas_call | solution.py:334
  24.3 15.3 %all_to_all.10.parts = f32[32,1,128]{2,1,0:T(1,128)S(1)} all-to-all(f32[32,1,128]{2,1,0:T(1,128)S(1)} %get-tuple-element.27), channel_id=1, replica_groups=mesh['gx'=2,'gy'=4,'gz'=4] {'gx','gy','gz'}, dimensions={0} | all-to-all | bytes 32768 | tf_op jit(solution)/shard_map/all_to_all | solution.py:419
  39.6 0.9 %shard_map.80 = (f32[3,8,8,128]{3,2,1,0:T(8,128)}, f32[3,8,8,128]{3,2,1,0:T(8,128)}) custom-call(f32[32,1,128]{2,1,0:T(1,128)S(1)} %all_to_all.10.parts, f32[3,8,8,128]{3,2,1,0:T(8,128)S(1)} %get-tuple-element.28.v0, f32[3,8,8,128]{3,2,1,0:T(8,128)S(1)} %get-tuple-element.29.v1, f32[3,8,8,128]{3,2,1,0:T(8,128)S(1)} %get-tuple-element.30.v2, ...), custom_call_target="tpu_custom_call" | custom-call | tf_op jit(solution)/shard_map/pallas_call | solution.py:334
  (2 shorter events, 0.0 us)
Async XLA Ops:
  0.6 5.6 %collective-permute-start = (f32[1,3,3,4,512]{4,3,2,1,0:T(4,128)}, f32[1,3,3,4,512]{4,3,2,1,0:T(4,128)S(1)}, u32[]{:S(2)}, u32[]{:S(2)}) collective-permute-start(f32[1,3,3,4,512]{4,3,2,1,0:T(4,128)} %bitcast.6), channel_id=1, source_target_pairs={{0,16},{16,0},{1,17},{17,1},{2,18},{18,2},{3,19},{19,3},{4,20},{20... | collective-permute-start | bytes 221192 | tf_op jit(solution)/shard_map/ppermute | solution.py:375
  8.5 14.9 %all-to-all-start = ((f32[32,8,128]{2,1,0:T(8,128)}), f32[32,8,128]{2,1,0:T(8,128)S(1)}, u32[]{:S(2)}, u32[]{:S(2)}) async-start(f32[32,8,128]{2,1,0:T(8,128)} %bitcast.3), calls=%async_computation | async-start | bytes 262144 | tf_op jit(solution)/shard_map/all_to_all | solution.py:406
  14.9 4.2 %collective-permute-start.1 = (f32[3,3,8,128]{3,2,1,0:T(8,128)S(1)}, f32[3,3,8,128]{3,2,1,0:T(8,128)S(1)}, u32[]{:S(2)}, u32[]{:S(2)}) collective-permute-start(f32[3,3,8,128]{3,2,1,0:T(8,128)S(1)} %get-tuple-element.26), channel_id=1, source_target_pairs={{0,16},{16,0},{1,17},{17,1},{2,18},{18,2},{3,19},{19,3},{4,20},{20... | collective-permute-start | bytes 110600 | tf_op jit(solution)/shard_map/ppermute | solution.py:389
  19.1 4.3 %collective-permute-start.2 = (f32[3,10,4,128]{3,2,1,0:T(4,128)S(1)}, f32[3,10,4,128]{3,2,1,0:T(4,128)S(1)}, u32[]{:S(2)}, u32[]{:S(2)}) collective-permute-start(f32[3,10,4,128]{3,2,1,0:T(4,128)S(1)} %get-tuple-element.33), channel_id=1, source_target_pairs={{0,4},{8,12},{4,0},{12,8},{1,5},{9,13},{5,1},{13,9},{2,6},{10,14},... | collective-permute-start | bytes 184328 | tf_op jit(solution)/shard_map/ppermute | solution.py:397
  21.0 2.4 %collective-permute-start.3 = (f32[3,10,4,128]{3,2,1,0:T(4,128)S(1)}, f32[3,10,4,128]{3,2,1,0:T(4,128)S(1)}, u32[]{:S(2)}, u32[]{:S(2)}) collective-permute-start(f32[3,10,4,128]{3,2,1,0:T(4,128)S(1)} %get-tuple-element.32), channel_id=1, source_target_pairs={{4,8},{8,4},{5,9},{9,5},{6,10},{10,6},{7,11},{11,7},{20,24},{24,20... | collective-permute-start | bytes 184328 | tf_op jit(solution)/shard_map/ppermute | solution.py:398

commit v4 on v3

--- a/solution.py
+++ b/solution.py
@@ -27,7 +27,7 @@
 
 
 def spectrum_kernel(pair, count, contrast_in, field_in, class_in, kind_in, source_in, library_in,
-                    hartley, spectrum, columns, pick, contrast, source, library, face,
+                    hartley, spectrum, columns, pick, contrast, source, library,
                     polar, field, classes, kinds, plain_source, sems):
     rows = contrast.shape[0]
     slabs = source.shape[1]
@@ -75,8 +75,6 @@
         for c in range(3):
             value = plain_source[c, x]
             source[c, p] = value
-            if p >= slabs - 3:
-                face[c, slabs - 1 - p] = value
 
 
 def solve_kernel(contrast, columns, spectrum, hartley, pick, library, other, source, tiles, bundle,
@@ -366,6 +364,7 @@
     nx, ny, nz = counts
     devices = nx * ny * nz
     slabs = source.shape[1]
+    gx = lax.axis_index("gx")
     dense = devices <= DENSE
     pair = nx == 2
     library = inverse_blocks.transpose(0, 2, 3, 1, 4)
@@ -373,20 +372,21 @@
     if pair:
         swap = [(0, 1), (1, 0)]
         other = lax.ppermute(library, "gx", swap)
+        face = jnp.where(gx == 0, source[:, slabs - 3 :][:, ::-1], source[:, :3])
+        face = lax.ppermute(face, "gx", swap)
     else:
         other = lax.all_gather(library, "gx", axis=0, tiled=True)
     count = TYPES * nx
-    hartley, spectrum, columns, pick, contrast, source, library, face = call(
+    hartley, spectrum, columns, pick, contrast, source, library = call(
         functools.partial(spectrum_kernel, pair, count),
         [((VOX, VOX), bf16), ((3 * rows, VOX), f32), ((rows, 8), f32), ((rows, 2 * count), bf16),
-         (contrast.shape, bf16), field, (library.shape, f32), ((3, 3, 8, 128), f32)],
+         (contrast.shape, bf16), field, (library.shape, f32)],
         (contrast, point_field, point_class.reshape(1, rows), cell_kind.reshape(1, rows), source, library),
         [pltpu.VMEM((3 * rows, VOX), bf16), pltpu.VMEM((3, rows), bf16), pltpu.VMEM((1, rows), jnp.int32),
          pltpu.VMEM((1, rows), jnp.int32), pltpu.VMEM(*field), pltpu.SemaphoreType.DMA((6,))],
         raw=True,
     )
     if pair:
-        face = lax.ppermute(face, "gx", swap)
         xlow = xhigh = face
         longer = jnp.concatenate([source, face[:, :2]], axis=1)
     else:
@@ -394,8 +394,8 @@
         longer = jnp.concatenate([xlow, source, xhigh], axis=1)
     even = lax.axis_index("gy") % 2 == 0
     low_rows, high_rows = longer[:, :, :4], longer[:, :, 4:]
+    yb = lax.ppermute(jnp.where(even, low_rows, high_rows), "gy", pairs_from(1, ny))
     ya = lax.ppermute(jnp.where(even, high_rows, low_rows), "gy", pairs_from(0, ny))
-    yb = lax.ppermute(jnp.where(even, low_rows, high_rows), "gy", pairs_from(1, ny))
     tiles, bundle = call(
         solve_kernel,
         [((4, 8, 128), f32), ((nx * ny if dense else 1, nz, 8, 128), f32)],

time: 40.7 us -> 40.8 us (level)
  no operation moved by 1% of the time
where the time goes in v4:
time: 40.8 us; the launch traced here: 40.5 us
  blocking collectives  15.2 us (37%)
  starting transfers between devices  13.8 us (34%)
  Pallas kernels  5.69 us (14%)
  waiting for transfers between devices  5.08 us (12%)
  between operations  0.69 us (2%)
    all_to_all x1, blocking collectives, whole_step(): parts = lax.all_to_all(moments, AXES, 0, 0)  15.2 us
    all_to_all x1, starting transfers between devices, whole_step(): lax.all_to_all(bundle.reshape(devices, 8, 128), AXES, 0, 0)  6.38 us
    pallas_call x4, Pallas kernels, call(): pl.pallas_call(body, out_shape=tuple((shape(s, d) for s, d in outs)), in_...  5.69 us
    ppermute x1, starting transfers between devices, whole_step(): other = lax.ppermute(library, 'gx', swap)  3.03 us
    ppermute x1, waiting for transfers between devices, whole_step(): face = lax.ppermute(face, 'gx', swap)  2.37 us
    ppermute x1, starting transfers between devices, whole_step(): lax.ppermute(jnp.where(even, high_rows, low_rows), 'gy', pairs_from(0, ny))  1.92 us
    ppermute x1, starting transfers between devices, whole_step(): face = lax.ppermute(face, 'gx', swap)  1.83 us
    ppermute x1, waiting for transfers between devices, whole_step(): lax.ppermute(jnp.where(even, high_rows, low_rows), 'gy', pairs_from(0, ny))  1.7 us
  transfers between devices with their start and end apart: 5, of which 3 were waited for; matrix products, arithmetic and copies ran while one was open for 0% of the time, Pallas kernels for 4%

profile of v4, /device:TPU:0, one launch (start us, length us, event | category | flops | bytes accessed | tf_op | source)
XLA Modules:
  0.0 40.5 jit_solution(11789868317228626223)
XLA Ops:
  0.6 3.0 %collective-permute-start = (f32[1,3,3,4,512]{4,3,2,1,0:T(4,128)}, f32[1,3,3,4,512]{4,3,2,1,0:T(4,128)S(1)}, u32[]{:S(2)}, u32[]{:S(2)}) collective-permute-start(f32[1,3,3,4,512]{4,3,2,1,0:T(4,128)} %bitcast.6), channel_id=1, source_target_pairs={{0,16},{16,0},{1,17},{17,1},{2,18},{18,2},{3,19},{19,3},{4,20},{20... | collective-permute-start | bytes 221192 | tf_op jit(solution)/shard_map/ppermute | solution.py:374
  3.7 1.5 %shard_map.77 = (bf16[512,512]{1,0:T(8,128)(2,1)S(1)}, f32[384,512]{1,0:T(8,128)S(1)}, f32[128,8]{1,0:T(8,128)S(1)}, bf16[128,16]{1,0:T(8,128)(2,1)S(1)}, bf16[1...) custom-call(bf16[128,1536]{1,0:T(8,128)(2,1)} %contrast_in.1, ...), custom_call_target="tpu_custom_call" | custom-call | tf_op jit(solution)/shard_map/pallas_call | solution.py:332
  5.2 1.0 %collective-permute-done.other = f32[1,3,3,4,512]{4,3,2,1,0:T(4,128)S(1)} collective-permute-done((f32[1,3,3,4,512]{4,3,2,1,0:T(4,128)}, f32[1,3,3,4,512]{4,3,2,1,0:T(4,128)S(1)}, u32[]{:S(2)}, u32[]{:S(2)}) %collective-permute-start) | collective-permute-done | bytes 73760 | tf_op jit(solution)/shard_map/ppermute | solution.py:374
  6.2 2.3 %shard_map.78 = (f32[4,8,128]{2,1,0:T(8,128)S(1)}, f32[8,4,8,128]{3,2,1,0:T(8,128)}) custom-call(bf16[128,1536]{1,0:T(8,128)(2,1)S(1)} %get-tuple-element.16.contrast, f32[128,8]{1,0:T(8,128)S(1)} %get-tuple-element.17.columns, f32[384,512]{1,0:T(8,128)S(1)} %get-tuple-element.18.spectrum, bf16[512,512]{1,0:T(8,128)(2,1)S(1)} %get-tuple-element.19.hartley, ...), custom_call_target="tpu_custom_call" | custom-call | tf_op jit(solution)/shard_map/pallas_call | solution.py:332
  8.5 0.0 copy-start
  8.5 0.0 slice-start
  8.5 6.4 %all-to-all-start = ((f32[32,8,128]{2,1,0:T(8,128)}), f32[32,8,128]{2,1,0:T(8,128)S(1)}, u32[]{:S(2)}, u32[]{:S(2)}) async-start(f32[32,8,128]{2,1,0:T(8,128)} %bitcast.3), calls=%async_computation | async-start | bytes 262144 | tf_op jit(solution)/shard_map/all_to_all | solution.py:406
  14.9 0.0 copy-done
  14.9 0.0 slice-done
  15.0 1.8 %collective-permute-start.1 = (f32[3,3,8,128]{3,2,1,0:T(8,128)S(1)}, f32[3,3,8,128]{3,2,1,0:T(8,128)S(1)}, u32[]{:S(2)}, u32[]{:S(2)}) collective-permute-start(f32[3,3,8,128]{3,2,1,0:T(8,128)S(1)} %slice_select_fusion), channel_id=1, source_target_pairs={{0,16},{16,0},{1,17},{17,1},{2,18},{18,2},{3,19},{19,3},{4,20},{20... | collective-permute-start | bytes 110600 | tf_op jit(solution)/shard_map/ppermute | solution.py:376
  16.8 2.4 %collective-permute-done.1.xlow.xhigh = f32[3,3,8,128]{3,2,1,0:T(8,128)S(1)} collective-permute-done((f32[3,3,8,128]{3,2,1,0:T(8,128)S(1)}, f32[3,3,8,128]{3,2,1,0:T(8,128)S(1)}, u32[]{:S(2)}, u32[]{:S(2)}) %collective-permute-start.1) | collective-permute-done | bytes 36896 | tf_op jit(solution)/shard_map/ppermute | solution.py:376
  19.2 1.9 %collective-permute-start.2 = (f32[3,10,4,128]{3,2,1,0:T(4,128)S(1)}, f32[3,10,4,128]{3,2,1,0:T(4,128)S(1)}, u32[]{:S(2)}, u32[]{:S(2)}) collective-permute-start(f32[3,10,4,128]{3,2,1,0:T(4,128)S(1)} %get-tuple-element.31), channel_id=1, source_target_pairs={{0,4},{8,12},{4,0},{12,8},{1,5},{9,13},{5,1},{13,9},{2,6},{10,14},... | collective-permute-start | bytes 184328 | tf_op jit(solution)/shard_map/ppermute | solution.py:398
  21.1 0.7 %collective-permute-start.3 = (f32[3,10,4,128]{3,2,1,0:T(4,128)S(1)}, f32[3,10,4,128]{3,2,1,0:T(4,128)S(1)}, u32[]{:S(2)}, u32[]{:S(2)}) collective-permute-start(f32[3,10,4,128]{3,2,1,0:T(4,128)S(1)} %get-tuple-element.30), channel_id=1, source_target_pairs={{4,8},{8,4},{5,9},{9,5},{6,10},{10,6},{7,11},{11,7},{20,24},{24,20... | collective-permute-start | bytes 184328 | tf_op jit(solution)/shard_map/ppermute | solution.py:397
  21.8 1.7 %collective-permute-done.2.ya = f32[3,10,4,128]{3,2,1,0:T(4,128)S(1)} collective-permute-done((f32[3,10,4,128]{3,2,1,0:T(4,128)S(1)}, f32[3,10,4,128]{3,2,1,0:T(4,128)S(1)}, u32[]{:S(2)}, u32[]{:S(2)}) %collective-permute-start.2) | collective-permute-done | bytes 61472 | tf_op jit(solution)/shard_map/ppermute | solution.py:398
  23.5 0.0 collective-permute-done.3.yb
  23.5 0.0 all-to-all-done
  23.5 0.9 %shard_map.79 = (f32[3,8,8,128]{3,2,1,0:T(8,128)S(1)}, f32[3,8,8,128]{3,2,1,0:T(8,128)S(1)}, f32[3,8,8,128]{3,2,1,0:T(8,128)S(1)}, f32[3,8,8,128]{3,2,1,0:T(8,128)S(1)}, f32[32,1,128]{2,1,0:T(1,128)S(1)}) custom-call(f32[4,8,128]{2,1,0:T(8,128)S(1)} %get-tuple-element.23.tiles, f32[2,4,4,8,128]{4,3,2,1,0:T(8,128)S(1)} %bitcast.5, ...), custom_call_target="tpu_custom_call" | custom-call | tf_op jit(solution)/shard_map/pallas_call | solution.py:332
  24.4 15.2 %all_to_all.10.parts = f32[32,1,128]{2,1,0:T(1,128)S(1)} all-to-all(f32[32,1,128]{2,1,0:T(1,128)S(1)} %get-tuple-element.25), channel_id=1, replica_groups=mesh['gx'=2,'gy'=4,'gz'=4] {'gx','gy','gz'}, dimensions={0} | all-to-all | bytes 32768 | tf_op jit(solution)/shard_map/all_to_all | solution.py:419
  39.6 0.9 %shard_map.80 = (f32[3,8,8,128]{3,2,1,0:T(8,128)}, f32[3,8,8,128]{3,2,1,0:T(8,128)}) custom-call(f32[32,1,128]{2,1,0:T(1,128)S(1)} %all_to_all.10.parts, f32[3,8,8,128]{3,2,1,0:T(8,128)S(1)} %get-tuple-element.26.v0, f32[3,8,8,128]{3,2,1,0:T(8,128)S(1)} %get-tuple-element.27.v1, f32[3,8,8,128]{3,2,1,0:T(8,128)S(1)} %get-tuple-element.28.v2, ...), custom_call_target="tpu_custom_call" | custom-call | tf_op jit(solution)/shard_map/pallas_call | solution.py:332
  (3 shorter events, 0.0 us)
Async XLA Ops:
  0.6 5.6 %collective-permute-start = (f32[1,3,3,4,512]{4,3,2,1,0:T(4,128)}, f32[1,3,3,4,512]{4,3,2,1,0:T(4,128)S(1)}, u32[]{:S(2)}, u32[]{:S(2)}) collective-permute-start(f32[1,3,3,4,512]{4,3,2,1,0:T(4,128)} %bitcast.6), channel_id=1, source_target_pairs={{0,16},{16,0},{1,17},{17,1},{2,18},{18,2},{3,19},{19,3},{4,20},{20... | collective-permute-start | bytes 221192 | tf_op jit(solution)/shard_map/ppermute | solution.py:374
  8.5 6.4 %copy-start = (f32[3,8,8,128]{3,2,1,0:T(8,128)S(1)}, f32[3,8,8,128]{3,2,1,0:T(8,128)}, u32[]{:S(2)}) copy-start(f32[3,8,8,128]{3,2,1,0:T(8,128)} %source_in.1) | copy-start | bytes 294916
  8.5 6.4 %slice-start = ((f32[3,8,8,128]{3,2,1,0:T(8,128)}), f32[3,3,8,128]{3,2,1,0:T(8,128)S(1)}, s32[]{:S(2)}) async-start(f32[3,8,8,128]{3,2,1,0:T(8,128)} %source_in.1), calls=%async_computation.2 | async-start | bytes 73728 | tf_op jit(solution)/shard_map/slice | solution.py:375
  8.5 14.9 %all-to-all-start = ((f32[32,8,128]{2,1,0:T(8,128)}), f32[32,8,128]{2,1,0:T(8,128)S(1)}, u32[]{:S(2)}, u32[]{:S(2)}) async-start(f32[32,8,128]{2,1,0:T(8,128)} %bitcast.3), calls=%async_computation | async-start | bytes 262144 | tf_op jit(solution)/shard_map/all_to_all | solution.py:406
  15.0 4.2 %collective-permute-start.1 = (f32[3,3,8,128]{3,2,1,0:T(8,128)S(1)}, f32[3,3,8,128]{3,2,1,0:T(8,128)S(1)}, u32[]{:S(2)}, u32[]{:S(2)}) collective-permute-start(f32[3,3,8,128]{3,2,1,0:T(8,128)S(1)} %slice_select_fusion), channel_id=1, source_target_pairs={{0,16},{16,0},{1,17},{17,1},{2,18},{18,2},{3,19},{19,3},{4,20},{20... | collective-permute-start | bytes 110600 | tf_op jit(solution)/shard_map/ppermute | solution.py:376
  19.2 4.3 %collective-permute-start.2 = (f32[3,10,4,128]{3,2,1,0:T(4,128)S(1)}, f32[3,10,4,128]{3,2,1,0:T(4,128)S(1)}, u32[]{:S(2)}, u32[]{:S(2)}) collective-permute-start(f32[3,10,4,128]{3,2,1,0:T(4,128)S(1)} %get-tuple-element.31), channel_id=1, source_target_pairs={{0,4},{8,12},{4,0},{12,8},{1,5},{9,13},{5,1},{13,9},{2,6},{10,14},... | collective-permute-start | bytes 184328 | tf_op jit(solution)/shard_map/ppermute | solution.py:398
  21.1 2.4 %collective-permute-start.3 = (f32[3,10,4,128]{3,2,1,0:T(4,128)S(1)}, f32[3,10,4,128]{3,2,1,0:T(4,128)S(1)}, u32[]{:S(2)}, u32[]{:S(2)}) collective-permute-start(f32[3,10,4,128]{3,2,1,0:T(4,128)S(1)} %get-tuple-element.30), channel_id=1, source_target_pairs={{4,8},{8,4},{5,9},{9,5},{6,10},{10,6},{7,11},{11,7},{20,24},{24,20... | collective-permute-start | bytes 184328 | tf_op jit(solution)/shard_map/ppermute | solution.py:397

commit v5 on v4

--- a/solution.py
+++ b/solution.py
@@ -27,7 +27,7 @@
 
 
 def spectrum_kernel(pair, count, contrast_in, field_in, class_in, kind_in, source_in, library_in,
-                    hartley, spectrum, columns, pick, contrast, source, library,
+                    hartley, spectrum, columns, pick, contrast, source, library, send_a, send_b,
                     polar, field, classes, kinds, plain_source, sems):
     rows = contrast.shape[0]
     slabs = source.shape[1]
@@ -70,11 +70,14 @@
     spectrum[...] = jnp.dot(polar[...], hartley[...], preferred_element_type=jnp.float32)
     for move in moves[4:]:
         move.wait()
+    even = lax.axis_index("gy") % 2 == 0
     for p in range(slabs):
         x = jnp.where(gx == 0, p, slabs - 1 - p) if pair else p
         for c in range(3):
             value = plain_source[c, x]
             source[c, p] = value
+            send_a[c, p] = jnp.where(even, value[4:], value[:4])
+            send_b[c, p] = jnp.where(even, value[:4], value[4:])
 
 
 def solve_kernel(contrast, columns, spectrum, hartley, pick, library, other, source, tiles, bundle,
@@ -156,7 +159,7 @@
             bundle[x, d] = tile
 
 
-def moment_kernel(dense, counts, tiles, got, source, xlow, xhigh, ya, yb, v0, v1, v2, v3, moments, w0, w1, w2):
+def moment_kernel(dense, counts, tiles, got, source, ytile, xlow, xhigh, v0, v1, v2, v3, moments, w0, w1, w2):
     slabs = source.shape[1]
     gx, gy, gz = where_am_i()
     nx, ny, nz = counts
@@ -164,7 +167,6 @@
     base = 0 if pair else 3
     row = lax.broadcasted_iota(jnp.int32, (8, 128), 0)
     lane = lax.broadcasted_iota(jnp.int32, (8, 128), 1)
-    even = gy % 2 == 0
     has_xl, has_xh = gx > 0, gx < nx - 1
     has_yl, has_yh = gy > 0, gy < ny - 1
     has_zl, has_zh = gz > 0, gz < nz - 1
@@ -214,18 +216,17 @@
         edge_x = edges[r]
         for c in range(3):
             for k in range(slabs if r == 1 else 3):
-                at = k if r == 0 else (base + k if r == 1 else base + slabs + k)
-                out = (3 - k) if r == 0 else (0 if r == 1 else k + 1)
-                s = slabs - 3 + k if r == 0 else (slabs - 1 - k if pair and r == 2 else k)
+                at = base - 1 - k if r == 0 else (base + k if r == 1 else base + slabs + k)
+                out = 0 if r == 1 else k + 1
+                s = k if r == 1 or (r == 2 and not pair) else slabs - 1 - k
                 s = c * slabs + s
-                value = (source if r == 1 else (xlow if r == 0 else xhigh))[c, k] - flux[r, 0][c]
+                beyond = xlow if r == 0 else xhigh
+                value = (source if r == 1 else beyond)[c, k] - flux[r, 0][c]
                 w0[c, at, 0] = value if edge_x is None else value * edge_x
                 if r == 1:
                     v0[c, k] = value
                 if out <= 2:
-                    a, b = ya[c, at], yb[c, at]
-                    halo = jnp.concatenate([jnp.where(even, a, b), jnp.where(even, b, a)], axis=0)
-                    halo = halo - flux[r, 1][c]
+                    halo = (ytile[c, k] if r == 1 else beyond[c, 3 + k]) - flux[r, 1][c]
                     w0[c, at, 1] = halo * (mask_y if edge_x is None else mask_y * edge_x)
                     value = pull(side_low, side_high, s)
                     w0[c, at, 2] = value * (mask_z if edge_x is None else mask_z * edge_x)
@@ -364,7 +365,6 @@
     nx, ny, nz = counts
     devices = nx * ny * nz
     slabs = source.shape[1]
-    gx = lax.axis_index("gx")
     dense = devices <= DENSE
     pair = nx == 2
     library = inverse_blocks.transpose(0, 2, 3, 1, 4)
@@ -372,30 +372,20 @@
     if pair:
         swap = [(0, 1), (1, 0)]
         other = lax.ppermute(library, "gx", swap)
-        face = jnp.where(gx == 0, source[:, slabs - 3 :][:, ::-1], source[:, :3])
-        face = lax.ppermute(face, "gx", swap)
     else:
         other = lax.all_gather(library, "gx", axis=0, tiled=True)
     count = TYPES * nx
-    hartley, spectrum, columns, pick, contrast, source, library = call(
+    hartley, spectrum, columns, pick, contrast, source, library, send_a, send_b = call(
         functools.partial(spectrum_kernel, pair, count),
         [((VOX, VOX), bf16), ((3 * rows, VOX), f32), ((rows, 8), f32), ((rows, 2 * count), bf16),
-         (contrast.shape, bf16), field, (library.shape, f32)],
+         (contrast.shape, bf16), field, (library.shape, f32), ((3, slabs, 4, 128), f32), ((3, slabs, 4, 128), f32)],
         (contrast, point_field, point_class.reshape(1, rows), cell_kind.reshape(1, rows), source, library),
         [pltpu.VMEM((3 * rows, VOX), bf16), pltpu.VMEM((3, rows), bf16), pltpu.VMEM((1, rows), jnp.int32),
          pltpu.VMEM((1, rows), jnp.int32), pltpu.VMEM(*field), pltpu.SemaphoreType.DMA((6,))],
         raw=True,
     )
-    if pair:
-        xlow = xhigh = face
-        longer = jnp.concatenate([source, face[:, :2]], axis=1)
-    else:
-        xlow, xhigh = from_both(source[:, :3], source[:, slabs - 3 :], "gx")
-        longer = jnp.concatenate([xlow, source, xhigh], axis=1)
-    even = lax.axis_index("gy") % 2 == 0
-    low_rows, high_rows = longer[:, :, :4], longer[:, :, 4:]
-    yb = lax.ppermute(jnp.where(even, low_rows, high_rows), "gy", pairs_from(1, ny))
-    ya = lax.ppermute(jnp.where(even, high_rows, low_rows), "gy", pairs_from(0, ny))
+    yb = lax.ppermute(send_b, "gy", pairs_from(1, ny))
+    ya = lax.ppermute(send_a, "gy", pairs_from(0, ny))
     tiles, bundle = call(
         solve_kernel,
         [((4, 8, 128), f32), ((nx * ny if dense else 1, nz, 8, 128), f32)],
@@ -409,10 +399,17 @@
         trio = jnp.stack([below, bundle[0], above], axis=1)
         trio = jnp.broadcast_to(trio[None], (ny,) + trio.shape).reshape(ny * nz, 3, 8, 128)
         got = lax.all_to_all(trio, ("gy", "gz"), 0, 0).reshape(ny, nz, 3, 8, 128).transpose(2, 0, 1, 3, 4)
+    even = lax.axis_index("gy") % 2 == 0
+    ytile = jnp.concatenate([jnp.where(even, ya, yb), jnp.where(even, yb, ya)], axis=2)
+    high = jnp.concatenate([source[:, : slabs - 4 : -1], ytile[:, : slabs - 3 : -1]], axis=1)
+    if pair:
+        xlow = xhigh = lax.ppermute(high, "gx", swap)
+    else:
+        xlow, xhigh = from_both(jnp.concatenate([source[:, :3], ytile[:, :2]], axis=1), high, "gx")
     v0, v1, v2, v3, moments = call(
         functools.partial(moment_kernel, dense, counts),
         [field, field, field, field, ((devices if dense else 1, 1, 128), f32)],
-        (tiles, got, source, xlow, xhigh, ya, yb),
+        (tiles, got, source, ytile, xlow, xhigh),
         [pltpu.VMEM((3, slabs + (3 if pair else 6), 4, 8, 128), f32) for _ in range(3)],
     )
     if dense:

time: 40.8 us -> 38.8 us (0.951)
  blocking collectives: 15.2 us -> 9.12 us
  waiting for transfers between devices: 5.08 us -> 9.11 us
    all_to_all x1, blocking collectives: 15.2 us -> 9.12 us  [whole_step(): parts = lax.all_to_all(moments, AXES, 0, 0)]
    all_to_all x1, waiting for transfers between devices: 0.01 us -> 3.35 us  [whole_step(): lax.all_to_all(bundle.reshape(devices, 8, 128), AXES, 0, 0)]
    ppermute x1, waiting for transfers between devices: 1.01 us -> 2.81 us  [whole_step(): other = lax.ppermute(library, 'gx', swap)]
    ppermute x1, starting transfers between devices: 3.03 us -> 1.56 us  [whole_step(): other = lax.ppermute(library, 'gx', swap)]
    ppermute x3, starting transfers between devices: 4.41 us -> 5.6 us  [the longest x1 3.12 us: whole_step(): ya = lax.ppermute(send_a, 'gy', pairs_from(0, ny))]
    ppermute x3, waiting for transfers between devices: 4.07 us -> 2.95 us  [the longest x1 2.95 us: whole_step(): xlow = xhigh = lax.ppermute(high, 'gx', swap)]
  transfers between devices with their start and end apart: 5 -> 5, of which waited for: 3 -> 3; matrix products, arithmetic and copies ran while one was open for 0% -> 0% of each run, Pallas kernels for 4% -> 0%
where the time goes in v5:
time: 38.8 us; the launch traced here: 38.6 us
  starting transfers between devices  13.8 us (36%)
  blocking collectives  9.12 us (24%)
  waiting for transfers between devices  9.11 us (23%)
  Pallas kernels  5.72 us (15%)
  between operations  0.73 us (2%)
    all_to_all x1, blocking collectives, whole_step(): parts = lax.all_to_all(moments, AXES, 0, 0)  9.12 us
    all_to_all x1, starting transfers between devices, whole_step(): lax.all_to_all(bundle.reshape(devices, 8, 128), AXES, 0, 0)  6.65 us
    pallas_call x4, Pallas kernels, call(): pl.pallas_call(body, out_shape=tuple((shape(s, d) for s, d in outs)), in_...  5.72 us
    all_to_all x1, waiting for transfers between devices, whole_step(): lax.all_to_all(bundle.reshape(devices, 8, 128), AXES, 0, 0)  3.35 us
    ppermute x1, starting transfers between devices, whole_step(): ya = lax.ppermute(send_a, 'gy', pairs_from(0, ny))  3.12 us
    ppermute x1, waiting for transfers between devices, whole_step(): xlow = xhigh = lax.ppermute(high, 'gx', swap)  2.95 us
    ppermute x1, waiting for transfers between devices, whole_step(): other = lax.ppermute(library, 'gx', swap)  2.81 us
    ppermute x1, starting transfers between devices, whole_step(): xlow = xhigh = lax.ppermute(high, 'gx', swap)  1.83 us
  transfers between devices with their start and end apart: 5, of which 3 were waited for; matrix products, arithmetic and copies ran while one was open for 0% of the time, Pallas kernels for 0%

profile of v5, /device:TPU:0, one launch (start us, length us, event | category | flops | bytes accessed | tf_op | source)
XLA Modules:
  0.0 38.6 jit_solution(15733484989044094651)
XLA Ops:
  0.6 0.0 copy-start
  0.6 1.6 %shard_map.77 = (bf16[512,512]{1,0:T(8,128)(2,1)S(1)}, f32[384,512]{1,0:T(8,128)S(1)}, f32[128,8]{1,0:T(8,128)S(1)}, bf16[128,16]{1,0:T(8,128)(2,1)S(1)}, bf16[1...) custom-call(bf16[128,1536]{1,0:T(8,128)(2,1)} %contrast_in.1, ...), custom_call_target="tpu_custom_call" | custom-call | tf_op jit(solution)/shard_map/pallas_call | solution.py:333
  2.2 3.1 %collective-permute-start.1 = (f32[3,8,4,128]{3,2,1,0:T(4,128)S(1)}, f32[3,8,4,128]{3,2,1,0:T(4,128)S(1)}, u32[]{:S(2)}, u32[]{:S(2)}) collective-permute-start(f32[3,8,4,128]{3,2,1,0:T(4,128)S(1)} %get-tuple-element.27), channel_id=1, source_target_pairs={{0,4},{8,12},{4,0},{12,8},{1,5},{9,13},{5,1},{13,9},{2,6},{10,14},... | collective-permute-start | bytes 147464 | tf_op jit(solution)/shard_map/ppermute | solution.py:388
  5.3 0.7 %collective-permute-start.2 = (f32[3,8,4,128]{3,2,1,0:T(4,128)S(1)}, f32[3,8,4,128]{3,2,1,0:T(4,128)S(1)}, u32[]{:S(2)}, u32[]{:S(2)}) collective-permute-start(f32[3,8,4,128]{3,2,1,0:T(4,128)S(1)} %get-tuple-element.28), channel_id=1, source_target_pairs={{4,8},{8,4},{5,9},{9,5},{6,10},{10,6},{7,11},{11,7},{20,24},{24,20... | collective-permute-start | bytes 147464 | tf_op jit(solution)/shard_map/ppermute | solution.py:387
  6.0 0.0 copy-done
  6.0 1.6 %collective-permute-start = (f32[1,3,3,4,512]{4,3,2,1,0:T(4,128)S(1)}, f32[1,3,3,4,512]{4,3,2,1,0:T(4,128)S(1)}, u32[]{:S(2)}, u32[]{:S(2)}) collective-permute-start(f32[1,3,3,4,512]{4,3,2,1,0:T(4,128)S(1)} %bitcast.15), channel_id=1, source_target_pairs={{0,16},{16,0},{1,17},{17,1},{2,18},{18,2},{3,19},{19,3},{4,20},{20... | collective-permute-start | bytes 221192 | tf_op jit(solution)/shard_map/ppermute | solution.py:374
  7.6 0.0 collective-permute-done.1
  7.6 0.0 collective-permute-done.2
  7.6 2.8 %collective-permute-done.other = f32[1,3,3,4,512]{4,3,2,1,0:T(4,128)S(1)} collective-permute-done((f32[1,3,3,4,512]{4,3,2,1,0:T(4,128)S(1)}, f32[1,3,3,4,512]{4,3,2,1,0:T(4,128)S(1)}, u32[]{:S(2)}, u32[]{:S(2)}) %collective-permute-start) | collective-permute-done | bytes 73760 | tf_op jit(solution)/shard_map/ppermute | solution.py:374
  10.4 2.3 %shard_map.78 = (f32[4,8,128]{2,1,0:T(8,128)S(1)}, f32[8,4,8,128]{3,2,1,0:T(8,128)}) custom-call(bf16[128,1536]{1,0:T(8,128)(2,1)S(1)} %get-tuple-element.18.contrast, f32[128,8]{1,0:T(8,128)S(1)} %get-tuple-element.19.columns, f32[384,512]{1,0:T(8,128)S(1)} %get-tuple-element.20.spectrum, bf16[512,512]{1,0:T(8,128)(2,1)S(1)} %get-tuple-element.21.hartley, ...), custom_call_target="tpu_custom_call" | custom-call | tf_op jit(solution)/shard_map/pallas_call | solution.py:333
  12.8 6.6 %all-to-all-start = ((f32[32,8,128]{2,1,0:T(8,128)}), f32[32,8,128]{2,1,0:T(8,128)S(1)}, u32[]{:S(2)}, u32[]{:S(2)}) async-start(f32[32,8,128]{2,1,0:T(8,128)} %bitcast.3), calls=%async_computation | async-start | bytes 262144 | tf_op jit(solution)/shard_map/all_to_all | solution.py:396
  19.5 1.8 %collective-permute-start.3 = (f32[3,5,8,128]{3,2,1,0:T(8,128)S(1)}, f32[3,5,8,128]{3,2,1,0:T(8,128)S(1)}, u32[]{:S(2)}, u32[]{:S(2)}) collective-permute-start(f32[3,5,8,128]{3,2,1,0:T(8,128)S(1)} %pad_maximum_fusion.1), channel_id=1, source_target_pairs={{0,16},{16,0},{1,17},{17,1},{2,18},{18,2},{3,19},{19,3},{4,20},{20... | collective-permute-start | bytes 184328 | tf_op jit(solution)/shard_map/ppermute | solution.py:406
  21.3 2.9 %collective-permute-done.3.xlow.xhigh = f32[3,5,8,128]{3,2,1,0:T(8,128)S(1)} collective-permute-done((f32[3,5,8,128]{3,2,1,0:T(8,128)S(1)}, f32[3,5,8,128]{3,2,1,0:T(8,128)S(1)}, u32[]{:S(2)}, u32[]{:S(2)}) %collective-permute-start.3) | collective-permute-done | bytes 61472 | tf_op jit(solution)/shard_map/ppermute | solution.py:406
  24.3 3.4 %all-to-all-done = f32[32,8,128]{2,1,0:T(8,128)S(1)} async-done(((f32[32,8,128]{2,1,0:T(8,128)}), f32[32,8,128]{2,1,0:T(8,128)S(1)}, u32[]{:S(2)}, u32[]{:S(2)}) %all-to-all-start) | async-done | bytes 131104 | tf_op jit(solution)/shard_map/all_to_all | solution.py:396
  27.6 0.9 %shard_map.79 = (f32[3,8,8,128]{3,2,1,0:T(8,128)S(1)}, f32[3,8,8,128]{3,2,1,0:T(8,128)S(1)}, f32[3,8,8,128]{3,2,1,0:T(8,128)S(1)}, f32[3,8,8,128]{3,2,1,0:T(8,128)S(1)}, f32[32,1,128]{2,1,0:T(1,128)S(1)}) custom-call(f32[4,8,128]{2,1,0:T(8,128)S(1)} %get-tuple-element.25.tiles, f32[2,4,4,8,128]{4,3,2,1,0:T(8,128)S(1)} %bitcast.9, ...), custom_call_target="tpu_custom_call" | custom-call | tf_op jit(solution)/shard_map/pallas_call | solution.py:333
  28.5 9.1 %all_to_all.10.parts = f32[32,1,128]{2,1,0:T(1,128)S(1)} all-to-all(f32[32,1,128]{2,1,0:T(1,128)S(1)} %get-tuple-element.29), channel_id=1, replica_groups=mesh['gx'=2,'gy'=4,'gz'=4] {'gx','gy','gz'}, dimensions={0} | all-to-all | bytes 32768 | tf_op jit(solution)/shard_map/all_to_all | solution.py:416
  37.6 0.9 %shard_map.80 = (f32[3,8,8,128]{3,2,1,0:T(8,128)}, f32[3,8,8,128]{3,2,1,0:T(8,128)}) custom-call(f32[32,1,128]{2,1,0:T(1,128)S(1)} %all_to_all.10.parts, f32[3,8,8,128]{3,2,1,0:T(8,128)S(1)} %get-tuple-element.30.v0, f32[3,8,8,128]{3,2,1,0:T(8,128)S(1)} %get-tuple-element.31.v1, f32[3,8,8,128]{3,2,1,0:T(8,128)S(1)} %get-tuple-element.32.v2, ...), custom_call_target="tpu_custom_call" | custom-call | tf_op jit(solution)/shard_map/pallas_call | solution.py:333
  (7 shorter events, 0.1 us)
Async XLA Ops:
  0.6 5.4 %copy-start = (f32[1,4,3,3,512]{4,1,3,2,0:T(4,128)S(1)}, f32[1,4,3,3,512]{4,1,3,2,0:T(4,128)}, u32[]{:S(2)}) copy-start(f32[1,4,3,3,512]{4,1,3,2,0:T(4,128)} %param.11) | copy-start | bytes 221188
  2.2 5.4 %collective-permute-start.1 = (f32[3,8,4,128]{3,2,1,0:T(4,128)S(1)}, f32[3,8,4,128]{3,2,1,0:T(4,128)S(1)}, u32[]{:S(2)}, u32[]{:S(2)}) collective-permute-start(f32[3,8,4,128]{3,2,1,0:T(4,128)S(1)} %get-tuple-element.27), channel_id=1, source_target_pairs={{0,4},{8,12},{4,0},{12,8},{1,5},{9,13},{5,1},{13,9},{2,6},{10,14},... | collective-permute-start | bytes 147464 | tf_op jit(solution)/shard_map/ppermute | solution.py:388
  5.3 2.2 %collective-permute-start.2 = (f32[3,8,4,128]{3,2,1,0:T(4,128)S(1)}, f32[3,8,4,128]{3,2,1,0:T(4,128)S(1)}, u32[]{:S(2)}, u32[]{:S(2)}) collective-permute-start(f32[3,8,4,128]{3,2,1,0:T(4,128)S(1)} %get-tuple-element.28), channel_id=1, source_target_pairs={{4,8},{8,4},{5,9},{9,5},{6,10},{10,6},{7,11},{11,7},{20,24},{24,20... | collective-permute-start | bytes 147464 | tf_op jit(solution)/shard_map/ppermute | solution.py:387
  6.0 4.4 %collective-permute-start = (f32[1,3,3,4,512]{4,3,2,1,0:T(4,128)S(1)}, f32[1,3,3,4,512]{4,3,2,1,0:T(4,128)S(1)}, u32[]{:S(2)}, u32[]{:S(2)}) collective-permute-start(f32[1,3,3,4,512]{4,3,2,1,0:T(4,128)S(1)} %bitcast.15), channel_id=1, source_target_pairs={{0,16},{16,0},{1,17},{17,1},{2,18},{18,2},{3,19},{19,3},{4,20},{20... | collective-permute-start | bytes 221192 | tf_op jit(solution)/shard_map/ppermute | solution.py:374
  12.8 14.9 %all-to-all-start = ((f32[32,8,128]{2,1,0:T(8,128)}), f32[32,8,128]{2,1,0:T(8,128)S(1)}, u32[]{:S(2)}, u32[]{:S(2)}) async-start(f32[32,8,128]{2,1,0:T(8,128)} %bitcast.3), calls=%async_computation | async-start | bytes 262144 | tf_op jit(solution)/shard_map/all_to_all | solution.py:396
  19.5 4.8 %collective-permute-start.3 = (f32[3,5,8,128]{3,2,1,0:T(8,128)S(1)}, f32[3,5,8,128]{3,2,1,0:T(8,128)S(1)}, u32[]{:S(2)}, u32[]{:S(2)}) collective-permute-start(f32[3,5,8,128]{3,2,1,0:T(8,128)S(1)} %pad_maximum_fusion.1), channel_id=1, source_target_pairs={{0,16},{16,0},{1,17},{17,1},{2,18},{18,2},{3,19},{19,3},{4,20},{20... | collective-permute-start | bytes 184328 | tf_op jit(solution)/shard_map/ppermute | solution.py:406

commit v6 on v5

--- a/solution.py
+++ b/solution.py
@@ -27,8 +27,8 @@
 
 
 def spectrum_kernel(pair, count, contrast_in, field_in, class_in, kind_in, source_in, library_in,
-                    hartley, spectrum, columns, pick, contrast, source, library, send_a, send_b,
-                    polar, field, classes, kinds, plain_source, sems):
+                    hartley, spectrum, columns, pick, weights, source, library, send_a, send_b,
+                    polar, field, classes, kinds, plain_source, contrast, sems):
     rows = contrast.shape[0]
     slabs = source.shape[1]
     gx = lax.axis_index("gx")
@@ -66,6 +66,7 @@
     for j in range(3):
         e = columns[:, j : j + 1]
         m = contrast[:, j * VOX : (j + 1) * VOX].astype(jnp.float32)
+        weights[:, j * VOX : (j + 1) * VOX] = m
         polar[j * rows : (j + 1) * rows, :] = (m * e).astype(jnp.bfloat16)
     spectrum[...] = jnp.dot(polar[...], hartley[...], preferred_element_type=jnp.float32)
     for move in moves[4:]:
@@ -80,9 +81,9 @@
             send_b[c, p] = jnp.where(even, value[:4], value[4:])
 
 
-def solve_kernel(contrast, columns, spectrum, hartley, pick, library, other, source, tiles, bundle,
+def solve_kernel(weights, columns, spectrum, hartley, pick, library, other, source, tiles, bundle,
                  mixing, stacked, product):
-    rows = contrast.shape[0]
+    rows = weights.shape[0]
     zb = rows // 8
     _, _, gz = where_am_i()
     for ij in range(9):
@@ -110,7 +111,7 @@
     for c in range(rows // 16):
         for j in range(3):
             at = slice(j * rows + c * 16, j * rows + (c + 1) * 16)
-            m = contrast[c * 16 : (c + 1) * 16, j * VOX : (j + 1) * VOX].astype(jnp.float32)
+            m = weights[c * 16 : (c + 1) * 16, j * VOX : (j + 1) * VOX]
             local = columns[c * 16 : (c + 1) * 16, j : j + 1] - product[at, :]
             stacked[at, :] = (m * local * (1.0 + kerr_scale * local * local)).astype(jnp.bfloat16)
     product[...] = jnp.dot(stacked[...], hartley[...], preferred_element_type=jnp.float32)
@@ -127,10 +128,11 @@
         stiff = jnp.zeros((16, VOX), jnp.float32)
         for j in range(3):
             at = slice(j * rows + c * 16, j * rows + (c + 1) * 16)
-            m = contrast[c * 16 : (c + 1) * 16, j * VOX : (j + 1) * VOX].astype(jnp.float32)
+            m = weights[c * 16 : (c + 1) * 16, j * VOX : (j + 1) * VOX]
             final = columns[c * 16 : (c + 1) * 16, j : j + 1] - product[at, :]
-            means.append(jnp.sum((1.0 + m) * final, axis=1, keepdims=True) * (1.0 / VOX))
-            stiff = stiff + m * final * final
+            weighted = m * final
+            means.append(jnp.sum(final + weighted, axis=1, keepdims=True) * (1.0 / VOX))
+            stiff = stiff + weighted * final
         means.append(0.5 + jnp.sum(stiff, axis=1, keepdims=True) * (1.0 / (3 * VOX)))
         compact = jnp.zeros((zb, 128), jnp.float32)
         for t in range(4):
@@ -152,6 +154,9 @@
         here = (place >= 3 * s) & (place < 3 * s + 3)
         low = jnp.where(here, pltpu.roll(value, (3 * s) % 128, 1) if s else value, low)
         high = jnp.where(here, pltpu.roll(value, (3 * s + 3) % 128, 1), high)
+    mirrored = jnp.minimum(place + 2 - 2 * (place % 3), 127)
+    low = jnp.take_along_axis(low, mirrored, axis=1)
+    high = jnp.take_along_axis(high, mirrored, axis=1)
     for d in range(bundle.shape[1]):
         zero = jnp.zeros((8, 128), jnp.float32)
         tile = jnp.where(gz == d, compact, jnp.where(gz + 1 == d, high, jnp.where(gz - 1 == d, low, zero)))
@@ -172,7 +177,7 @@
     has_zl, has_zh = gz > 0, gz < nz - 1
     one = lambda flag: jnp.where(flag, 1.0, 0.0)
     mask_y = jnp.where(row < 4, one(has_yh), one(has_yl))
-    mask_z = jnp.where(lane < 64, one(has_zh), one(has_zl))
+    mask_z = jnp.where(lane < 64, one(has_zl), one(has_zh))
     masks = (None, mask_y, mask_z, mask_y * mask_z)
     yl, yh = jnp.maximum(gy - 1, 0), jnp.minimum(gy + 1, ny - 1)
     zl, zh = jnp.maximum(gz - 1, 0), jnp.minimum(gz + 1, nz - 1)
@@ -190,9 +195,20 @@
         return jnp.take_along_axis(tile, spread + t * zb, axis=1)
 
     def pull(low_tile, high_tile, s):
-        a = pltpu.roll(high_tile, (-3 * s) % 128, 1) if s else high_tile
-        b = pltpu.roll(low_tile, (125 - 3 * s) % 128, 1)
+        a = pltpu.roll(low_tile, (-3 * s) % 128, 1) if s else low_tile
+        b = pltpu.roll(high_tile, (125 - 3 * s) % 128, 1)
         return jnp.where(lane < 64, a, b)
+
+    def put(ref, c, at, t, value):
+        if t & 1:
+            ref[c, at, t >> 1, 0:8, :] = value
+            ref[c, at, t >> 1, 16:24, :] = value
+        else:
+            ref[c, at, t >> 1, 8:16, :] = value
+
+    def take(ref, c, at, t, shift=0):
+        start = (8, 9, 7)[shift] if not t & 1 else (0, 1, 15)[shift]
+        return ref[c, at, t >> 1, start : start + 8, :]
 
     diag = {}
     flux = {}
@@ -222,21 +238,20 @@
                 s = c * slabs + s
                 beyond = xlow if r == 0 else xhigh
                 value = (source if r == 1 else beyond)[c, k] - flux[r, 0][c]
-                w0[c, at, 0] = value if edge_x is None else value * edge_x
+                put(w0, c, at, 0, value if edge_x is None else value * edge_x)
                 if r == 1:
                     v0[c, k] = value
                 if out <= 2:
                     halo = (ytile[c, k] if r == 1 else beyond[c, 3 + k]) - flux[r, 1][c]
-                    w0[c, at, 1] = halo * (mask_y if edge_x is None else mask_y * edge_x)
+                    put(w0, c, at, 1, halo * (mask_y if edge_x is None else mask_y * edge_x))
                     value = pull(side_low, side_high, s)
-                    w0[c, at, 2] = value * (mask_z if edge_x is None else mask_z * edge_x)
+                    put(w0, c, at, 2, value * (mask_z if edge_x is None else mask_z * edge_x))
                 if out <= 1:
                     value = pull(corner_low, corner_high, s)
-                    w0[c, at, 3] = value * (masks[3] if edge_x is None else masks[3] * edge_x)
+                    put(w0, c, at, 3, value * (masks[3] if edge_x is None else masks[3] * edge_x))
     for key in diag:
         diag[key] = diag[key] + (6.0 - SHIFT)
 
-    first_row, last_row = row == 0, row == 7
     first_lane, last_lane = lane == 0, lane == 127
     acc = [jnp.zeros((8, 128), jnp.float32) for _ in range(6)]
     levels = (w0, w1, w2, None)
@@ -250,35 +265,28 @@
                 r = 0 if at < base else (1 if at < base + slabs else 2)
                 depth = reach - out
                 want = (0,) if depth == 0 else ((0, 1, 2) if depth == 1 else (0, 1, 2, 3))
-                have = (0, 1, 2) if depth == 0 else (0, 1, 2, 3)
-                v = {t: src[c, at, t] for t in have}
-                left = {t: pltpu.roll(v[t], 127, 1) for t in have if t in (0, 2) or depth > 0}
-                right = {t: pltpu.roll(v[t], 1, 1) for t in have if t in (0, 2) or depth > 0}
-                down = {t: pltpu.roll(v[t], 7, 0) for t in have if t in (0, 1) or depth > 0}
-                over = {t: pltpu.roll(v[t], 1, 0) for t in have if t in (0, 1) or depth > 0}
                 edge_x = edges[r]
                 for t in want:
-                    zp = jnp.where(last_lane, left[t ^ 2], left[t])
-                    zm = jnp.where(first_lane, right[t ^ 2], right[t])
-                    yp = jnp.where(last_row, down[t ^ 1], down[t])
-                    ym = jnp.where(first_row, over[t ^ 1], over[t])
-                    beside = src[c, at + 1, t] + (zp + zm) + (yp + ym)
+                    here, across = take(src, c, at, t), take(src, c, at, t ^ 2)
+                    zm = jnp.where(first_lane, across, pltpu.roll(here, 1, 1))
+                    zp = jnp.where(last_lane, across, pltpu.roll(here, 127, 1))
+                    beside = take(src, c, at + 1, t) + (zp + zm) + (take(src, c, at, t, 1) + take(src, c, at, t, 2))
                     if at > 0:
-                        beside = beside + src[c, at - 1, t]
-                    value = diag[r, t] * v[t] - beside
+                        beside = beside + take(src, c, at - 1, t)
+                    value = diag[r, t] * here - beside
                     if masks[t] is not None:
                         value = value * masks[t]
                     if edge_x is not None:
                         value = value * edge_x
                     if dst is not None:
-                        dst[c, at, t] = value
+                        put(dst, c, at, t, value)
                     if t == 0 and r == 1:
                         results[level][c, at - base] = value
-                        acc[2 * level - 1] = acc[2 * level - 1] + v[0] * value
+                        acc[2 * level - 1] = acc[2 * level - 1] + here * value
                         if level < 3:
                             acc[2 * level] = acc[2 * level] + value * value
                         if level == 1:
-                            acc[0] = acc[0] + v[0] * v[0]
+                            acc[0] = acc[0] + here * here
     line = jnp.zeros((1, 128), jnp.float32)
     slot = lax.broadcasted_iota(jnp.int32, (1, 128), 1)
     for k in range(6):
@@ -375,13 +383,13 @@
     else:
         other = lax.all_gather(library, "gx", axis=0, tiled=True)
     count = TYPES * nx
-    hartley, spectrum, columns, pick, contrast, source, library, send_a, send_b = call(
+    hartley, spectrum, columns, pick, weights, source, library, send_a, send_b = call(
         functools.partial(spectrum_kernel, pair, count),
         [((VOX, VOX), bf16), ((3 * rows, VOX), f32), ((rows, 8), f32), ((rows, 2 * count), bf16),
-         (contrast.shape, bf16), field, (library.shape, f32), ((3, slabs, 4, 128), f32), ((3, slabs, 4, 128), f32)],
+         (contrast.shape, f32), field, (library.shape, f32), ((3, slabs, 4, 128), f32), ((3, slabs, 4, 128), f32)],
         (contrast, point_field, point_class.reshape(1, rows), cell_kind.reshape(1, rows), source, library),
         [pltpu.VMEM((3 * rows, VOX), bf16), pltpu.VMEM((3, rows), bf16), pltpu.VMEM((1, rows), jnp.int32),
-         pltpu.VMEM((1, rows), jnp.int32), pltpu.VMEM(*field), pltpu.SemaphoreType.DMA((6,))],
+         pltpu.VMEM((1, rows), jnp.int32), pltpu.VMEM(*field), pltpu.VMEM(contrast.shape, bf16), pltpu.SemaphoreType.DMA((6,))],
         raw=True,
     )
     yb = lax.ppermute(send_b, "gy", pairs_from(1, ny))
@@ -389,7 +397,7 @@
     tiles, bundle = call(
         solve_kernel,
         [((4, 8, 128), f32), ((nx * ny if dense else 1, nz, 8, 128), f32)],
-        (contrast, columns, spectrum, hartley, pick, library if pair else other, other, source),
+        (weights, columns, spectrum, hartley, pick, library if pair else other, other, source),
         [pltpu.VMEM((9, rows, VOX), f32), pltpu.VMEM((3 * rows, VOX), bf16), pltpu.VMEM((3 * rows, VOX), f32)],
     )
     if dense:
@@ -410,7 +418,7 @@
         functools.partial(moment_kernel, dense, counts),
         [field, field, field, field, ((devices if dense else 1, 1, 128), f32)],
         (tiles, got, source, ytile, xlow, xhigh),
-        [pltpu.VMEM((3, slabs + (3 if pair else 6), 4, 8, 128), f32) for _ in range(3)],
+        [pltpu.VMEM((3, slabs + (3 if pair else 6), 2, 24, 128), f32) for _ in range(3)],
     )
     if dense:
         parts = lax.all_to_all(moments, AXES, 0, 0)

time: 38.8 us -> 38.7 us (level)
  no operation moved by 1% of the time
where the time goes in v6:
time: 38.7 us; the launch traced here: 38.5 us
  starting transfers between devices  13.8 us (36%)
  blocking collectives  9.12 us (24%)
  waiting for transfers between devices  9.11 us (24%)
  Pallas kernels  5.61 us (14%)
  between operations  0.73 us (2%)
    all_to_all x1, blocking collectives, whole_step(): parts = lax.all_to_all(moments, AXES, 0, 0)  9.12 us
    all_to_all x1, starting transfers between devices, whole_step(): lax.all_to_all(bundle.reshape(devices, 8, 128), AXES, 0, 0)  6.65 us
    pallas_call x4, Pallas kernels, call(): pl.pallas_call(body, out_shape=tuple((shape(s, d) for s, d in outs)), in_...  5.61 us
    all_to_all x1, waiting for transfers between devices, whole_step(): lax.all_to_all(bundle.reshape(devices, 8, 128), AXES, 0, 0)  3.35 us
    ppermute x1, starting transfers between devices, whole_step(): ya = lax.ppermute(send_a, 'gy', pairs_from(0, ny))  3.12 us
    ppermute x1, waiting for transfers between devices, whole_step(): xlow = xhigh = lax.ppermute(high, 'gx', swap)  2.95 us
    ppermute x1, waiting for transfers between devices, whole_step(): other = lax.ppermute(library, 'gx', swap)  2.81 us
    ppermute x1, starting transfers between devices, whole_step(): xlow = xhigh = lax.ppermute(high, 'gx', swap)  1.83 us
  transfers between devices with their start and end apart: 5, of which 3 were waited for; matrix products, arithmetic and copies ran while one was open for 0% of the time, Pallas kernels for 0%

profile of v6, /device:TPU:0, one launch (start us, length us, event | category | flops | bytes accessed | tf_op | source)
XLA Modules:
  0.0 38.5 jit_solution(14845654497111804845)
XLA Ops:
  0.6 0.0 copy-start
  0.6 1.6 %shard_map.77 = (bf16[512,512]{1,0:T(8,128)(2,1)S(1)}, f32[384,512]{1,0:T(8,128)S(1)}, f32[128,8]{1,0:T(8,128)S(1)}, bf16[128,16]{1,0:T(8,128)(2,1)S(1)}, f32[12...) custom-call(bf16[128,1536]{1,0:T(8,128)(2,1)} %contrast_in.1, ...), custom_call_target="tpu_custom_call" | custom-call | tf_op jit(solution)/shard_map/pallas_call | solution.py:341
  2.2 3.1 %collective-permute-start.1 = (f32[3,8,4,128]{3,2,1,0:T(4,128)S(1)}, f32[3,8,4,128]{3,2,1,0:T(4,128)S(1)}, u32[]{:S(2)}, u32[]{:S(2)}) collective-permute-start(f32[3,8,4,128]{3,2,1,0:T(4,128)S(1)} %get-tuple-element.27), channel_id=1, source_target_pairs={{0,4},{8,12},{4,0},{12,8},{1,5},{9,13},{5,1},{13,9},{2,6},{10,14},... | collective-permute-start | bytes 147464 | tf_op jit(solution)/shard_map/ppermute | solution.py:396
  5.3 0.7 %collective-permute-start.2 = (f32[3,8,4,128]{3,2,1,0:T(4,128)S(1)}, f32[3,8,4,128]{3,2,1,0:T(4,128)S(1)}, u32[]{:S(2)}, u32[]{:S(2)}) collective-permute-start(f32[3,8,4,128]{3,2,1,0:T(4,128)S(1)} %get-tuple-element.28), channel_id=1, source_target_pairs={{4,8},{8,4},{5,9},{9,5},{6,10},{10,6},{7,11},{11,7},{20,24},{24,20... | collective-permute-start | bytes 147464 | tf_op jit(solution)/shard_map/ppermute | solution.py:395
  6.0 0.0 copy-done
  6.0 1.6 %collective-permute-start = (f32[1,3,3,4,512]{4,3,2,1,0:T(4,128)S(1)}, f32[1,3,3,4,512]{4,3,2,1,0:T(4,128)S(1)}, u32[]{:S(2)}, u32[]{:S(2)}) collective-permute-start(f32[1,3,3,4,512]{4,3,2,1,0:T(4,128)S(1)} %bitcast.15), channel_id=1, source_target_pairs={{0,16},{16,0},{1,17},{17,1},{2,18},{18,2},{3,19},{19,3},{4,20},{20... | collective-permute-start | bytes 221192 | tf_op jit(solution)/shard_map/ppermute | solution.py:382
  7.6 0.0 collective-permute-done.1
  7.6 0.0 collective-permute-done.2
  7.6 2.8 %collective-permute-done.other = f32[1,3,3,4,512]{4,3,2,1,0:T(4,128)S(1)} collective-permute-done((f32[1,3,3,4,512]{4,3,2,1,0:T(4,128)S(1)}, f32[1,3,3,4,512]{4,3,2,1,0:T(4,128)S(1)}, u32[]{:S(2)}, u32[]{:S(2)}) %collective-permute-start) | collective-permute-done | bytes 73760 | tf_op jit(solution)/shard_map/ppermute | solution.py:382
  10.4 2.3 %shard_map.78 = (f32[4,8,128]{2,1,0:T(8,128)S(1)}, f32[8,4,8,128]{3,2,1,0:T(8,128)}) custom-call(f32[128,1536]{1,0:T(8,128)S(1)} %get-tuple-element.18.weights, f32[128,8]{1,0:T(8,128)S(1)} %get-tuple-element.19.columns, f32[384,512]{1,0:T(8,128)S(1)} %get-tuple-element.20.spectrum, bf16[512,512]{1,0:T(8,128)(2,1)S(1)} %get-tuple-element.21.hartley, ...), custom_call_target="tpu_custom_call" | custom-call | tf_op jit(solution)/shard_map/pallas_call | solution.py:341
  12.8 6.7 %all-to-all-start = ((f32[32,8,128]{2,1,0:T(8,128)}), f32[32,8,128]{2,1,0:T(8,128)S(1)}, u32[]{:S(2)}, u32[]{:S(2)}) async-start(f32[32,8,128]{2,1,0:T(8,128)} %bitcast.3), calls=%async_computation | async-start | bytes 262144 | tf_op jit(solution)/shard_map/all_to_all | solution.py:404
  19.5 1.8 %collective-permute-start.3 = (f32[3,5,8,128]{3,2,1,0:T(8,128)S(1)}, f32[3,5,8,128]{3,2,1,0:T(8,128)S(1)}, u32[]{:S(2)}, u32[]{:S(2)}) collective-permute-start(f32[3,5,8,128]{3,2,1,0:T(8,128)S(1)} %pad_maximum_fusion.1), channel_id=1, source_target_pairs={{0,16},{16,0},{1,17},{17,1},{2,18},{18,2},{3,19},{19,3},{4,20},{20... | collective-permute-start | bytes 184328 | tf_op jit(solution)/shard_map/ppermute | solution.py:414
  21.3 2.9 %collective-permute-done.3.xlow.xhigh = f32[3,5,8,128]{3,2,1,0:T(8,128)S(1)} collective-permute-done((f32[3,5,8,128]{3,2,1,0:T(8,128)S(1)}, f32[3,5,8,128]{3,2,1,0:T(8,128)S(1)}, u32[]{:S(2)}, u32[]{:S(2)}) %collective-permute-start.3) | collective-permute-done | bytes 61472 | tf_op jit(solution)/shard_map/ppermute | solution.py:414
  24.3 3.4 %all-to-all-done = f32[32,8,128]{2,1,0:T(8,128)S(1)} async-done(((f32[32,8,128]{2,1,0:T(8,128)}), f32[32,8,128]{2,1,0:T(8,128)S(1)}, u32[]{:S(2)}, u32[]{:S(2)}) %all-to-all-start) | async-done | bytes 131104 | tf_op jit(solution)/shard_map/all_to_all | solution.py:404
  27.6 0.8 %shard_map.79 = (f32[3,8,8,128]{3,2,1,0:T(8,128)S(1)}, f32[3,8,8,128]{3,2,1,0:T(8,128)S(1)}, f32[3,8,8,128]{3,2,1,0:T(8,128)S(1)}, f32[3,8,8,128]{3,2,1,0:T(8,128)S(1)}, f32[32,1,128]{2,1,0:T(1,128)S(1)}) custom-call(f32[4,8,128]{2,1,0:T(8,128)S(1)} %get-tuple-element.25.tiles, f32[2,4,4,8,128]{4,3,2,1,0:T(8,128)S(1)} %bitcast.9, ...), custom_call_target="tpu_custom_call" | custom-call | tf_op jit(solution)/shard_map/pallas_call | solution.py:341
  28.4 9.1 %all_to_all.10.parts = f32[32,1,128]{2,1,0:T(1,128)S(1)} all-to-all(f32[32,1,128]{2,1,0:T(1,128)S(1)} %get-tuple-element.29), channel_id=1, replica_groups=mesh['gx'=2,'gy'=4,'gz'=4] {'gx','gy','gz'}, dimensions={0} | all-to-all | bytes 32768 | tf_op jit(solution)/shard_map/all_to_all | solution.py:424
  37.5 0.9 %shard_map.80 = (f32[3,8,8,128]{3,2,1,0:T(8,128)}, f32[3,8,8,128]{3,2,1,0:T(8,128)}) custom-call(f32[32,1,128]{2,1,0:T(1,128)S(1)} %all_to_all.10.parts, f32[3,8,8,128]{3,2,1,0:T(8,128)S(1)} %get-tuple-element.30.v0, f32[3,8,8,128]{3,2,1,0:T(8,128)S(1)} %get-tuple-element.31.v1, f32[3,8,8,128]{3,2,1,0:T(8,128)S(1)} %get-tuple-element.32.v2, ...), custom_call_target="tpu_custom_call" | custom-call | tf_op jit(solution)/shard_map/pallas_call | solution.py:341
  (7 shorter events, 0.1 us)
Async XLA Ops:
  0.6 5.4 %copy-start = (f32[1,4,3,3,512]{4,1,3,2,0:T(4,128)S(1)}, f32[1,4,3,3,512]{4,1,3,2,0:T(4,128)}, u32[]{:S(2)}) copy-start(f32[1,4,3,3,512]{4,1,3,2,0:T(4,128)} %param.11) | copy-start | bytes 221188
  2.2 5.4 %collective-permute-start.1 = (f32[3,8,4,128]{3,2,1,0:T(4,128)S(1)}, f32[3,8,4,128]{3,2,1,0:T(4,128)S(1)}, u32[]{:S(2)}, u32[]{:S(2)}) collective-permute-start(f32[3,8,4,128]{3,2,1,0:T(4,128)S(1)} %get-tuple-element.27), channel_id=1, source_target_pairs={{0,4},{8,12},{4,0},{12,8},{1,5},{9,13},{5,1},{13,9},{2,6},{10,14},... | collective-permute-start | bytes 147464 | tf_op jit(solution)/shard_map/ppermute | solution.py:396
  5.3 2.3 %collective-permute-start.2 = (f32[3,8,4,128]{3,2,1,0:T(4,128)S(1)}, f32[3,8,4,128]{3,2,1,0:T(4,128)S(1)}, u32[]{:S(2)}, u32[]{:S(2)}) collective-permute-start(f32[3,8,4,128]{3,2,1,0:T(4,128)S(1)} %get-tuple-element.28), channel_id=1, source_target_pairs={{4,8},{8,4},{5,9},{9,5},{6,10},{10,6},{7,11},{11,7},{20,24},{24,20... | collective-permute-start | bytes 147464 | tf_op jit(solution)/shard_map/ppermute | solution.py:395
  6.0 4.4 %collective-permute-start = (f32[1,3,3,4,512]{4,3,2,1,0:T(4,128)S(1)}, f32[1,3,3,4,512]{4,3,2,1,0:T(4,128)S(1)}, u32[]{:S(2)}, u32[]{:S(2)}) collective-permute-start(f32[1,3,3,4,512]{4,3,2,1,0:T(4,128)S(1)} %bitcast.15), channel_id=1, source_target_pairs={{0,16},{16,0},{1,17},{17,1},{2,18},{18,2},{3,19},{19,3},{4,20},{20... | collective-permute-start | bytes 221192 | tf_op jit(solution)/shard_map/ppermute | solution.py:382
  12.8 14.9 %all-to-all-start = ((f32[32,8,128]{2,1,0:T(8,128)}), f32[32,8,128]{2,1,0:T(8,128)S(1)}, u32[]{:S(2)}, u32[]{:S(2)}) async-start(f32[32,8,128]{2,1,0:T(8,128)} %bitcast.3), calls=%async_computation | async-start | bytes 262144 | tf_op jit(solution)/shard_map/all_to_all | solution.py:404
  19.5 4.8 %collective-permute-start.3 = (f32[3,5,8,128]{3,2,1,0:T(8,128)S(1)}, f32[3,5,8,128]{3,2,1,0:T(8,128)S(1)}, u32[]{:S(2)}, u32[]{:S(2)}) collective-permute-start(f32[3,5,8,128]{3,2,1,0:T(8,128)S(1)} %pad_maximum_fusion.1), channel_id=1, source_target_pairs={{0,16},{16,0},{1,17},{17,1},{2,18},{18,2},{3,19},{19,3},{4,20},{20... | collective-permute-start | bytes 184328 | tf_op jit(solution)/shard_map/ppermute | solution.py:414

commit v7 on v6

--- a/solution.py
+++ b/solution.py
@@ -16,7 +16,6 @@
 ITERS = 3
 AXES = ("gx", "gy", "gz")
 DENSE = 64
-SHIFT = 8.0
 GRANT = 16 * 1024 * 1024
 
 kerr_scale = 0.1
@@ -140,7 +139,10 @@
             tiles[t, c : c + 1, :] = jnp.sum(jnp.where(spread, wide, 0.0), axis=0, keepdims=True)
             compact = compact + jnp.where(packed & (group == t), wide, 0.0)
         product[c : c + 1, 0:128] = jnp.sum(compact, axis=0, keepdims=True)
+        product[c : c + 1, 128:256] = jnp.max(wide, axis=0, keepdims=True)
+        product[c : c + 1, 256:384] = jnp.min(wide, axis=0, keepdims=True)
     compact = product[0:8, 0:128]
+    tallest, lowest = product[0:8, 128:256], product[0:8, 256:384]
 
     place = lax.broadcasted_iota(jnp.int32, (8, 128), 1)
     low = jnp.zeros((8, 128), jnp.float32)
@@ -160,11 +162,12 @@
     for d in range(bundle.shape[1]):
         zero = jnp.zeros((8, 128), jnp.float32)
         tile = jnp.where(gz == d, compact, jnp.where(gz + 1 == d, high, jnp.where(gz - 1 == d, low, zero)))
+        tile = jnp.where(place == 126, tallest, jnp.where(place == 127, lowest, tile))
         for x in range(bundle.shape[0]):
             bundle[x, d] = tile
 
 
-def moment_kernel(dense, counts, tiles, got, source, ytile, xlow, xhigh, v0, v1, v2, v3, moments, w0, w1, w2):
+def moment_kernel(dense, counts, tiles, got, source, ytile, xlow, xhigh, v0, v1, v2, v3, moments, scale, w0, w1, w2):
     slabs = source.shape[1]
     gx, gy, gz = where_am_i()
     nx, ny, nz = counts
@@ -249,8 +252,24 @@
                 if out <= 1:
                     value = pull(corner_low, corner_high, s)
                     put(w0, c, at, 3, value * (masks[3] if edge_x is None else masks[3] * edge_x))
+    peak = floor = None
+    flat = got.shape[0] * got.shape[1] * got.shape[2]
+    for k in range(flat):
+        tile = got[k // (got.shape[1] * got.shape[2]), k // got.shape[2] % got.shape[1], k % got.shape[2]]
+        peak = tile if peak is None else jnp.maximum(peak, tile)
+        floor = tile if floor is None else jnp.minimum(floor, tile)
+    peak = jnp.max(peak, axis=0, keepdims=True)[:, 126:127]
+    floor = jnp.min(floor, axis=0, keepdims=True)[:, 127:128]
+    middle = 0.5 * peak + 0.5 * floor
+    spread_of = 6.0 + (0.5 * peak - 0.5 * floor)
+    slots = lax.broadcasted_iota(jnp.int32, (1, 128), 1)
+    shrink = 1.0 / spread_of
+    scale[...] = jnp.where(slots == 0, (6.0 + middle) * shrink, shrink)
+    shrink = jnp.broadcast_to(shrink, (8, 128))
+    middle = jnp.broadcast_to(middle, (8, 128))
     for key in diag:
-        diag[key] = diag[key] + (6.0 - SHIFT)
+        diag[key] = diag[key] - middle
+    shrunk = [shrink if mask is None else mask * shrink for mask in masks]
 
     first_lane, last_lane = lane == 0, lane == 127
     acc = [jnp.zeros((8, 128), jnp.float32) for _ in range(6)]
@@ -273,9 +292,7 @@
                     beside = take(src, c, at + 1, t) + (zp + zm) + (take(src, c, at, t, 1) + take(src, c, at, t, 2))
                     if at > 0:
                         beside = beside + take(src, c, at - 1, t)
-                    value = diag[r, t] * here - beside
-                    if masks[t] is not None:
-                        value = value * masks[t]
+                    value = (diag[r, t] * here - beside) * shrunk[t]
                     if edge_x is not None:
                         value = value * edge_x
                     if dst is not None:
@@ -295,7 +312,7 @@
     moments[...] = jnp.broadcast_to(line[None], moments.shape)
 
 
-def combine_kernel(pair, parts, v0, v1, v2, v3, step_out, residual_out):
+def combine_kernel(pair, parts, scale, v0, v1, v2, v3, step_out, residual_out):
     total = jnp.sum(parts[...], axis=0)
     nu = [total[:, k : k + 1] for k in range(6)]
 
@@ -311,11 +328,12 @@
         size = max(len(a), len(b))
         return [a[k] if k >= len(b) else (b[k] if k >= len(a) else a[k] + b[k]) for k in range(size)]
 
+    centre, shrink = scale[:, 0:1], scale[:, 1:2]
     unit = jnp.ones((1, 1), jnp.float32)
     direction, residual, newton = [unit], [unit], []
     norm = nu[0]
     for iteration in range(ITERS):
-        image = added([SHIFT * d for d in direction], [0.0 * unit] + direction)
+        image = added([centre * d for d in direction], [0.0 * unit] + direction)
         alpha = norm / gram(direction, image)
         newton = added(newton, [alpha * d for d in direction])
         residual = added(residual, [-alpha * g for g in image])
@@ -325,7 +343,7 @@
             direction = added(residual, [ratio * d for d in direction])
             norm = following
     wide = lambda a: jnp.broadcast_to(a, (8, 128))
-    newton = [wide(a) for a in newton]
+    newton = [wide(a * shrink) for a in newton]
     residual = [wide(a) for a in residual]
     for c in range(v0.shape[0]):
         for x in range(v0.shape[1]):
@@ -407,6 +425,9 @@
         trio = jnp.stack([below, bundle[0], above], axis=1)
         trio = jnp.broadcast_to(trio[None], (ny,) + trio.shape).reshape(ny * nz, 3, 8, 128)
         got = lax.all_to_all(trio, ("gy", "gz"), 0, 0).reshape(ny, nz, 3, 8, 128).transpose(2, 0, 1, 3, 4)
+    if not dense:
+        got = got.at[..., 126].set(lax.pmax(jnp.max(tiles[3]), AXES))
+        got = got.at[..., 127].set(lax.pmin(jnp.min(tiles[3]), AXES))
     even = lax.axis_index("gy") % 2 == 0
     ytile = jnp.concatenate([jnp.where(even, ya, yb), jnp.where(even, yb, ya)], axis=2)
     high = jnp.concatenate([source[:, : slabs - 4 : -1], ytile[:, : slabs - 3 : -1]], axis=1)
@@ -414,9 +435,9 @@
         xlow = xhigh = lax.ppermute(high, "gx", swap)
     else:
         xlow, xhigh = from_both(jnp.concatenate([source[:, :3], ytile[:, :2]], axis=1), high, "gx")
-    v0, v1, v2, v3, moments = call(
+    v0, v1, v2, v3, moments, scale = call(
         functools.partial(moment_kernel, dense, counts),
-        [field, field, field, field, ((devices if dense else 1, 1, 128), f32)],
+        [field, field, field, field, ((devices if dense else 1, 1, 128), f32), ((1, 128), f32)],
         (tiles, got, source, ytile, xlow, xhigh),
         [pltpu.VMEM((3, slabs + (3 if pair else 6), 2, 24, 128), f32) for _ in range(3)],
     )
@@ -424,7 +445,7 @@
         parts = lax.all_to_all(moments, AXES, 0, 0)
     else:
         parts = lax.psum(moments, AXES)
-    return call(functools.partial(combine_kernel, pair), [field, field], (parts, v0, v1, v2, v3), last=True)
+    return call(functools.partial(combine_kernel, pair), [field, field], (parts, scale, v0, v1, v2, v3), last=True)
 
 
 def solution(mesh):

time: 38.7 us -> 38.8 us (level)
  no operation moved by 1% of the time
where the time goes in v7:
time: 38.8 us; the launch traced here: 38.5 us
  starting transfers between devices  13.8 us (36%)
  blocking collectives  9.12 us (24%)
  waiting for transfers between devices  9.11 us (23%)
  Pallas kernels  5.7 us (15%)
  between operations  0.72 us (2%)
    all_to_all x1, blocking collectives, whole_step(): parts = lax.all_to_all(moments, AXES, 0, 0)  9.12 us
    all_to_all x1, starting transfers between devices, whole_step(): lax.all_to_all(bundle.reshape(devices, 8, 128), AXES, 0, 0)  6.65 us
    pallas_call x4, Pallas kernels, call(): pl.pallas_call(body, out_shape=tuple((shape(s, d) for s, d in outs)), in_...  5.7 us
    all_to_all x1, waiting for transfers between devices, whole_step(): lax.all_to_all(bundle.reshape(devices, 8, 128), AXES, 0, 0)  3.35 us
    ppermute x1, starting transfers between devices, whole_step(): ya = lax.ppermute(send_a, 'gy', pairs_from(0, ny))  3.12 us
    ppermute x1, waiting for transfers between devices, whole_step(): xlow = xhigh = lax.ppermute(high, 'gx', swap)  2.95 us
    ppermute x1, waiting for transfers between devices, whole_step(): other = lax.ppermute(library, 'gx', swap)  2.81 us
    ppermute x1, starting transfers between devices, whole_step(): xlow = xhigh = lax.ppermute(high, 'gx', swap)  1.83 us
  transfers between devices with their start and end apart: 5, of which 3 were waited for; matrix products, arithmetic and copies ran while one was open for 0% of the time, Pallas kernels for 0%

profile of v7, /device:TPU:0, one launch (start us, length us, event | category | flops | bytes accessed | tf_op | source)
XLA Modules:
  0.0 38.5 jit_solution(7214129272305130090)
XLA Ops:
  0.6 0.0 copy-start
  0.6 1.6 %shard_map.77 = (bf16[512,512]{1,0:T(8,128)(2,1)S(1)}, f32[384,512]{1,0:T(8,128)S(1)}, f32[128,8]{1,0:T(8,128)S(1)}, bf16[128,16]{1,0:T(8,128)(2,1)S(1)}, f32[12...) custom-call(bf16[128,1536]{1,0:T(8,128)(2,1)} %contrast_in.1, ...), custom_call_target="tpu_custom_call" | custom-call | tf_op jit(solution)/shard_map/pallas_call | solution.py:359
  2.2 3.1 %collective-permute-start.1 = (f32[3,8,4,128]{3,2,1,0:T(4,128)S(1)}, f32[3,8,4,128]{3,2,1,0:T(4,128)S(1)}, u32[]{:S(2)}, u32[]{:S(2)}) collective-permute-start(f32[3,8,4,128]{3,2,1,0:T(4,128)S(1)} %get-tuple-element.28), channel_id=1, source_target_pairs={{0,4},{8,12},{4,0},{12,8},{1,5},{9,13},{5,1},{13,9},{2,6},{10,14},... | collective-permute-start | bytes 147464 | tf_op jit(solution)/shard_map/ppermute | solution.py:414
  5.3 0.7 %collective-permute-start.2 = (f32[3,8,4,128]{3,2,1,0:T(4,128)S(1)}, f32[3,8,4,128]{3,2,1,0:T(4,128)S(1)}, u32[]{:S(2)}, u32[]{:S(2)}) collective-permute-start(f32[3,8,4,128]{3,2,1,0:T(4,128)S(1)} %get-tuple-element.29), channel_id=1, source_target_pairs={{4,8},{8,4},{5,9},{9,5},{6,10},{10,6},{7,11},{11,7},{20,24},{24,20... | collective-permute-start | bytes 147464 | tf_op jit(solution)/shard_map/ppermute | solution.py:413
  6.0 0.0 copy-done
  6.0 1.6 %collective-permute-start = (f32[1,3,3,4,512]{4,3,2,1,0:T(4,128)S(1)}, f32[1,3,3,4,512]{4,3,2,1,0:T(4,128)S(1)}, u32[]{:S(2)}, u32[]{:S(2)}) collective-permute-start(f32[1,3,3,4,512]{4,3,2,1,0:T(4,128)S(1)} %bitcast.15), channel_id=1, source_target_pairs={{0,16},{16,0},{1,17},{17,1},{2,18},{18,2},{3,19},{19,3},{4,20},{20... | collective-permute-start | bytes 221192 | tf_op jit(solution)/shard_map/ppermute | solution.py:400
  7.6 0.0 collective-permute-done.1
  7.6 0.0 collective-permute-done.2
  7.6 2.8 %collective-permute-done.other = f32[1,3,3,4,512]{4,3,2,1,0:T(4,128)S(1)} collective-permute-done((f32[1,3,3,4,512]{4,3,2,1,0:T(4,128)S(1)}, f32[1,3,3,4,512]{4,3,2,1,0:T(4,128)S(1)}, u32[]{:S(2)}, u32[]{:S(2)}) %collective-permute-start) | collective-permute-done | bytes 73760 | tf_op jit(solution)/shard_map/ppermute | solution.py:400
  10.4 2.3 %shard_map.78 = (f32[4,8,128]{2,1,0:T(8,128)S(1)}, f32[8,4,8,128]{3,2,1,0:T(8,128)}) custom-call(f32[128,1536]{1,0:T(8,128)S(1)} %get-tuple-element.19.weights, f32[128,8]{1,0:T(8,128)S(1)} %get-tuple-element.20.columns, f32[384,512]{1,0:T(8,128)S(1)} %get-tuple-element.21.spectrum, bf16[512,512]{1,0:T(8,128)(2,1)S(1)} %get-tuple-element.22.hartley, ...), custom_call_target="tpu_custom_call" | custom-call | tf_op jit(solution)/shard_map/pallas_call | solution.py:359
  12.8 6.7 %all-to-all-start = ((f32[32,8,128]{2,1,0:T(8,128)}), f32[32,8,128]{2,1,0:T(8,128)S(1)}, u32[]{:S(2)}, u32[]{:S(2)}) async-start(f32[32,8,128]{2,1,0:T(8,128)} %bitcast.3), calls=%async_computation | async-start | bytes 262144 | tf_op jit(solution)/shard_map/all_to_all | solution.py:422
  19.5 1.8 %collective-permute-start.3 = (f32[3,5,8,128]{3,2,1,0:T(8,128)S(1)}, f32[3,5,8,128]{3,2,1,0:T(8,128)S(1)}, u32[]{:S(2)}, u32[]{:S(2)}) collective-permute-start(f32[3,5,8,128]{3,2,1,0:T(8,128)S(1)} %pad_maximum_fusion.1), channel_id=1, source_target_pairs={{0,16},{16,0},{1,17},{17,1},{2,18},{18,2},{3,19},{19,3},{4,20},{20... | collective-permute-start | bytes 184328 | tf_op jit(solution)/shard_map/ppermute | solution.py:435
  21.3 2.9 %collective-permute-done.3.xlow.xhigh = f32[3,5,8,128]{3,2,1,0:T(8,128)S(1)} collective-permute-done((f32[3,5,8,128]{3,2,1,0:T(8,128)S(1)}, f32[3,5,8,128]{3,2,1,0:T(8,128)S(1)}, u32[]{:S(2)}, u32[]{:S(2)}) %collective-permute-start.3) | collective-permute-done | bytes 61472 | tf_op jit(solution)/shard_map/ppermute | solution.py:435
  24.3 3.4 %all-to-all-done = f32[32,8,128]{2,1,0:T(8,128)S(1)} async-done(((f32[32,8,128]{2,1,0:T(8,128)}), f32[32,8,128]{2,1,0:T(8,128)S(1)}, u32[]{:S(2)}, u32[]{:S(2)}) %all-to-all-start) | async-done | bytes 131104 | tf_op jit(solution)/shard_map/all_to_all | solution.py:422
  27.6 0.9 %shard_map.79 = (f32[3,8,8,128]{3,2,1,0:T(8,128)S(1)}, f32[3,8,8,128]{3,2,1,0:T(8,128)S(1)}, f32[3,8,8,128]{3,2,1,0:T(8,128)S(1)}, f32[3,8,8,128]{3,2,1,0:T(8,12...) custom-call(f32[4,8,128]{2,1,0:T(8,128)S(1)} %get-tuple-element.26.tiles, f32[2,4,4,8,128]{4,3,2,1,0:T(8,128)S(1)} %bitcast.9, ...), custom_call_target="tpu_custom_call" | custom-call | tf_op jit(solution)/shard_map/pallas_call | solution.py:359
  28.5 9.1 %all_to_all.10.parts = f32[32,1,128]{2,1,0:T(1,128)S(1)} all-to-all(f32[32,1,128]{2,1,0:T(1,128)S(1)} %get-tuple-element.30), channel_id=1, replica_groups=mesh['gx'=2,'gy'=4,'gz'=4] {'gx','gy','gz'}, dimensions={0} | all-to-all | bytes 32768 | tf_op jit(solution)/shard_map/all_to_all | solution.py:445
  37.6 0.9 %shard_map.80 = (f32[3,8,8,128]{3,2,1,0:T(8,128)}, f32[3,8,8,128]{3,2,1,0:T(8,128)}) custom-call(f32[32,1,128]{2,1,0:T(1,128)S(1)} %all_to_all.10.parts, f32[1,128]{1,0:T(1,128)S(1)} %get-tuple-element.31.scale, f32[3,8,8,128]{3,2,1,0:T(8,128)S(1)} %get-tuple-element.32.v0, f32[3,8,8,128]{3,2,1,0:T(8,128)S(1)} %get-tuple-element.33.v1, ...), custom_call_target="tpu_custom_call" | custom-call | tf_op jit(solution)/shard_map/pallas_call | solution.py:359
  (7 shorter events, 0.1 us)
Async XLA Ops:
  0.6 5.4 %copy-start = (f32[1,4,3,3,512]{4,1,3,2,0:T(4,128)S(1)}, f32[1,4,3,3,512]{4,1,3,2,0:T(4,128)}, u32[]{:S(2)}) copy-start(f32[1,4,3,3,512]{4,1,3,2,0:T(4,128)} %param.11) | copy-start | bytes 221188
  2.2 5.4 %collective-permute-start.1 = (f32[3,8,4,128]{3,2,1,0:T(4,128)S(1)}, f32[3,8,4,128]{3,2,1,0:T(4,128)S(1)}, u32[]{:S(2)}, u32[]{:S(2)}) collective-permute-start(f32[3,8,4,128]{3,2,1,0:T(4,128)S(1)} %get-tuple-element.28), channel_id=1, source_target_pairs={{0,4},{8,12},{4,0},{12,8},{1,5},{9,13},{5,1},{13,9},{2,6},{10,14},... | collective-permute-start | bytes 147464 | tf_op jit(solution)/shard_map/ppermute | solution.py:414
  5.3 2.3 %collective-permute-start.2 = (f32[3,8,4,128]{3,2,1,0:T(4,128)S(1)}, f32[3,8,4,128]{3,2,1,0:T(4,128)S(1)}, u32[]{:S(2)}, u32[]{:S(2)}) collective-permute-start(f32[3,8,4,128]{3,2,1,0:T(4,128)S(1)} %get-tuple-element.29), channel_id=1, source_target_pairs={{4,8},{8,4},{5,9},{9,5},{6,10},{10,6},{7,11},{11,7},{20,24},{24,20... | collective-permute-start | bytes 147464 | tf_op jit(solution)/shard_map/ppermute | solution.py:413
  6.0 4.4 %collective-permute-start = (f32[1,3,3,4,512]{4,3,2,1,0:T(4,128)S(1)}, f32[1,3,3,4,512]{4,3,2,1,0:T(4,128)S(1)}, u32[]{:S(2)}, u32[]{:S(2)}) collective-permute-start(f32[1,3,3,4,512]{4,3,2,1,0:T(4,128)S(1)} %bitcast.15), channel_id=1, source_target_pairs={{0,16},{16,0},{1,17},{17,1},{2,18},{18,2},{3,19},{19,3},{4,20},{20... | collective-permute-start | bytes 221192 | tf_op jit(solution)/shard_map/ppermute | solution.py:400
  12.8 14.9 %all-to-all-start = ((f32[32,8,128]{2,1,0:T(8,128)}), f32[32,8,128]{2,1,0:T(8,128)S(1)}, u32[]{:S(2)}, u32[]{:S(2)}) async-start(f32[32,8,128]{2,1,0:T(8,128)} %bitcast.3), calls=%async_computation | async-start | bytes 262144 | tf_op jit(solution)/shard_map/all_to_all | solution.py:422
  19.5 4.8 %collective-permute-start.3 = (f32[3,5,8,128]{3,2,1,0:T(8,128)S(1)}, f32[3,5,8,128]{3,2,1,0:T(8,128)S(1)}, u32[]{:S(2)}, u32[]{:S(2)}) collective-permute-start(f32[3,5,8,128]{3,2,1,0:T(8,128)S(1)} %pad_maximum_fusion.1), channel_id=1, source_target_pairs={{0,16},{16,0},{1,17},{17,1},{2,18},{18,2},{3,19},{19,3},{4,20},{20... | collective-permute-start | bytes 184328 | tf_op jit(solution)/shard_map/ppermute | solution.py:435

commit v8 on v7

--- a/solution.py
+++ b/solution.py
@@ -410,7 +410,14 @@
          pltpu.VMEM((1, rows), jnp.int32), pltpu.VMEM(*field), pltpu.VMEM(contrast.shape, bf16), pltpu.SemaphoreType.DMA((6,))],
         raw=True,
     )
-    yb = lax.ppermute(send_b, "gy", pairs_from(1, ny))
+    couples = []
+    for z in range(nz):
+        mate = z ^ 1 if z ^ 1 < nz else z
+        for i in range(ny):
+            j = i + 1 if i % 2 else i - 1
+            inside = 0 <= j < ny
+            couples.append((i * nz + z, (j * nz + z) if inside else i * nz + mate))
+    yb = lax.ppermute(send_b, ("gy", "gz"), couples)
     ya = lax.ppermute(send_a, "gy", pairs_from(0, ny))
     tiles, bundle = call(
         solve_kernel,

time: 38.8 us -> 36.8 us (0.948)
  starting transfers between devices: 13.8 us -> 11.5 us
    all_to_all x1, starting transfers between devices: 6.65 us -> 5.07 us  [whole_step(): lax.all_to_all(bundle.reshape(devices, 8, 128), AXES, 0, 0)]
    ppermute x1, starting transfers between devices: 0.65 us -> 0.01 us  [whole_step(): yb = lax.ppermute(send_b, ('gy', 'gz'), couples)]
    ppermute x1, waiting for transfers between devices: 0.01 us -> 0.56 us  [whole_step(): ya = lax.ppermute(send_a, 'gy', pairs_from(0, ny))]
  transfers between devices with their start and end apart: 5 -> 5, of which waited for: 3 -> 4; matrix products, arithmetic and copies ran while one was open for 0% -> 0% of each run, Pallas kernels for 0% -> 0%
where the time goes in v8:
time: 36.8 us; the launch traced here: 36.6 us
  starting transfers between devices  11.5 us (31%)
  waiting for transfers between devices  9.46 us (26%)
  blocking collectives  9.12 us (25%)
  Pallas kernels  5.71 us (16%)
  between operations  0.69 us (2%)
    all_to_all x1, blocking collectives, whole_step(): parts = lax.all_to_all(moments, AXES, 0, 0)  9.12 us
    pallas_call x4, Pallas kernels, call(): pl.pallas_call(body, out_shape=tuple((shape(s, d) for s, d in outs)), in_...  5.71 us
    all_to_all x1, starting transfers between devices, whole_step(): lax.all_to_all(bundle.reshape(devices, 8, 128), AXES, 0, 0)  5.07 us
    all_to_all x1, waiting for transfers between devices, whole_step(): lax.all_to_all(bundle.reshape(devices, 8, 128), AXES, 0, 0)  3.35 us
    ppermute x1, starting transfers between devices, whole_step(): ya = lax.ppermute(send_a, 'gy', pairs_from(0, ny))  3.12 us
    ppermute x1, waiting for transfers between devices, whole_step(): xlow = xhigh = lax.ppermute(high, 'gx', swap)  2.95 us
    ppermute x1, waiting for transfers between devices, whole_step(): other = lax.ppermute(library, 'gx', swap)  2.6 us
    ppermute x1, starting transfers between devices, whole_step(): xlow = xhigh = lax.ppermute(high, 'gx', swap)  1.83 us
  transfers between devices with their start and end apart: 5, of which 4 were waited for; matrix products, arithmetic and copies ran while one was open for 0% of the time, Pallas kernels for 0%

profile of v8, /device:TPU:0, one launch (start us, length us, event | category | flops | bytes accessed | tf_op | source)
XLA Modules:
  0.0 36.6 jit_solution(16989039603098464945)
XLA Ops:
  0.6 0.0 copy-start
  0.6 1.6 %shard_map.77 = (bf16[512,512]{1,0:T(8,128)(2,1)S(1)}, f32[384,512]{1,0:T(8,128)S(1)}, f32[128,8]{1,0:T(8,128)S(1)}, bf16[128,16]{1,0:T(8,128)(2,1)S(1)}, f32[12...) custom-call(bf16[128,1536]{1,0:T(8,128)(2,1)} %contrast_in.1, ...), custom_call_target="tpu_custom_call" | custom-call | tf_op jit(solution)/shard_map/pallas_call | solution.py:359
  2.2 3.1 %collective-permute-start.1 = (f32[3,8,4,128]{3,2,1,0:T(4,128)S(1)}, f32[3,8,4,128]{3,2,1,0:T(4,128)S(1)}, u32[]{:S(2)}, u32[]{:S(2)}) collective-permute-start(f32[3,8,4,128]{3,2,1,0:T(4,128)S(1)} %get-tuple-element.28), channel_id=1, source_target_pairs={{0,4},{8,12},{4,0},{12,8},{1,5},{9,13},{5,1},{13,9},{2,6},{10,14},... | collective-permute-start | bytes 147464 | tf_op jit(solution)/shard_map/ppermute | solution.py:421
  5.3 0.0 collective-permute-start.2
  5.3 0.0 copy-done
  5.3 1.5 %collective-permute-start = (f32[1,3,3,4,512]{4,3,2,1,0:T(4,128)S(1)}, f32[1,3,3,4,512]{4,3,2,1,0:T(4,128)S(1)}, u32[]{:S(2)}, u32[]{:S(2)}) collective-permute-start(f32[1,3,3,4,512]{4,3,2,1,0:T(4,128)S(1)} %bitcast.15), channel_id=1, source_target_pairs={{0,16},{16,0},{1,17},{17,1},{2,18},{18,2},{3,19},{19,3},{4,20},{20... | collective-permute-start | bytes 221192 | tf_op jit(solution)/shard_map/ppermute | solution.py:400
  6.9 0.6 %collective-permute-done.1 = f32[3,8,4,128]{3,2,1,0:T(4,128)S(1)} collective-permute-done((f32[3,8,4,128]{3,2,1,0:T(4,128)S(1)}, f32[3,8,4,128]{3,2,1,0:T(4,128)S(1)}, u32[]{:S(2)}, u32[]{:S(2)}) %collective-permute-start.1) | collective-permute-done | bytes 49184 | tf_op jit(solution)/shard_map/ppermute | solution.py:421
  7.4 0.0 collective-permute-done.2
  7.4 2.6 %collective-permute-done.other = f32[1,3,3,4,512]{4,3,2,1,0:T(4,128)S(1)} collective-permute-done((f32[1,3,3,4,512]{4,3,2,1,0:T(4,128)S(1)}, f32[1,3,3,4,512]{4,3,2,1,0:T(4,128)S(1)}, u32[]{:S(2)}, u32[]{:S(2)}) %collective-permute-start) | collective-permute-done | bytes 73760 | tf_op jit(solution)/shard_map/ppermute | solution.py:400
  10.0 2.3 %shard_map.78 = (f32[4,8,128]{2,1,0:T(8,128)S(1)}, f32[8,4,8,128]{3,2,1,0:T(8,128)}) custom-call(f32[128,1536]{1,0:T(8,128)S(1)} %get-tuple-element.19.weights, f32[128,8]{1,0:T(8,128)S(1)} %get-tuple-element.20.columns, f32[384,512]{1,0:T(8,128)S(1)} %get-tuple-element.21.spectrum, bf16[512,512]{1,0:T(8,128)(2,1)S(1)} %get-tuple-element.22.hartley, ...), custom_call_target="tpu_custom_call" | custom-call | tf_op jit(solution)/shard_map/pallas_call | solution.py:359
  12.4 5.1 %all-to-all-start = ((f32[32,8,128]{2,1,0:T(8,128)}), f32[32,8,128]{2,1,0:T(8,128)S(1)}, u32[]{:S(2)}, u32[]{:S(2)}) async-start(f32[32,8,128]{2,1,0:T(8,128)} %bitcast.3), calls=%async_computation | async-start | bytes 262144 | tf_op jit(solution)/shard_map/all_to_all | solution.py:429
  17.5 1.8 %collective-permute-start.3 = (f32[3,5,8,128]{3,2,1,0:T(8,128)S(1)}, f32[3,5,8,128]{3,2,1,0:T(8,128)S(1)}, u32[]{:S(2)}, u32[]{:S(2)}) collective-permute-start(f32[3,5,8,128]{3,2,1,0:T(8,128)S(1)} %pad_maximum_fusion.1), channel_id=1, source_target_pairs={{0,16},{16,0},{1,17},{17,1},{2,18},{18,2},{3,19},{19,3},{4,20},{20... | collective-permute-start | bytes 184328 | tf_op jit(solution)/shard_map/ppermute | solution.py:442
  19.4 2.9 %collective-permute-done.3.xlow.xhigh = f32[3,5,8,128]{3,2,1,0:T(8,128)S(1)} collective-permute-done((f32[3,5,8,128]{3,2,1,0:T(8,128)S(1)}, f32[3,5,8,128]{3,2,1,0:T(8,128)S(1)}, u32[]{:S(2)}, u32[]{:S(2)}) %collective-permute-start.3) | collective-permute-done | bytes 61472 | tf_op jit(solution)/shard_map/ppermute | solution.py:442
  22.3 3.4 %all-to-all-done = f32[32,8,128]{2,1,0:T(8,128)S(1)} async-done(((f32[32,8,128]{2,1,0:T(8,128)}), f32[32,8,128]{2,1,0:T(8,128)S(1)}, u32[]{:S(2)}, u32[]{:S(2)}) %all-to-all-start) | async-done | bytes 131104 | tf_op jit(solution)/shard_map/all_to_all | solution.py:429
  25.7 0.9 %shard_map.79 = (f32[3,8,8,128]{3,2,1,0:T(8,128)S(1)}, f32[3,8,8,128]{3,2,1,0:T(8,128)S(1)}, f32[3,8,8,128]{3,2,1,0:T(8,128)S(1)}, f32[3,8,8,128]{3,2,1,0:T(8,12...) custom-call(f32[4,8,128]{2,1,0:T(8,128)S(1)} %get-tuple-element.26.tiles, f32[2,4,4,8,128]{4,3,2,1,0:T(8,128)S(1)} %bitcast.9, ...), custom_call_target="tpu_custom_call" | custom-call | tf_op jit(solution)/shard_map/pallas_call | solution.py:359
  26.5 9.1 %all_to_all.10.parts = f32[32,1,128]{2,1,0:T(1,128)S(1)} all-to-all(f32[32,1,128]{2,1,0:T(1,128)S(1)} %get-tuple-element.30), channel_id=1, replica_groups=mesh['gx'=2,'gy'=4,'gz'=4] {'gx','gy','gz'}, dimensions={0} | all-to-all | bytes 32768 | tf_op jit(solution)/shard_map/all_to_all | solution.py:452
  35.6 0.9 %shard_map.80 = (f32[3,8,8,128]{3,2,1,0:T(8,128)}, f32[3,8,8,128]{3,2,1,0:T(8,128)}) custom-call(f32[32,1,128]{2,1,0:T(1,128)S(1)} %all_to_all.10.parts, f32[1,128]{1,0:T(1,128)S(1)} %get-tuple-element.31.scale, f32[3,8,8,128]{3,2,1,0:T(8,128)S(1)} %get-tuple-element.32.v0, f32[3,8,8,128]{3,2,1,0:T(8,128)S(1)} %get-tuple-element.33.v1, ...), custom_call_target="tpu_custom_call" | custom-call | tf_op jit(solution)/shard_map/pallas_call | solution.py:359
  (7 shorter events, 0.1 us)
Async XLA Ops:
  0.6 4.7 %copy-start = (f32[1,4,3,3,512]{4,1,3,2,0:T(4,128)S(1)}, f32[1,4,3,3,512]{4,1,3,2,0:T(4,128)}, u32[]{:S(2)}) copy-start(f32[1,4,3,3,512]{4,1,3,2,0:T(4,128)} %param.11) | copy-start | bytes 221188
  2.2 5.2 %collective-permute-start.1 = (f32[3,8,4,128]{3,2,1,0:T(4,128)S(1)}, f32[3,8,4,128]{3,2,1,0:T(4,128)S(1)}, u32[]{:S(2)}, u32[]{:S(2)}) collective-permute-start(f32[3,8,4,128]{3,2,1,0:T(4,128)S(1)} %get-tuple-element.28), channel_id=1, source_target_pairs={{0,4},{8,12},{4,0},{12,8},{1,5},{9,13},{5,1},{13,9},{2,6},{10,14},... | collective-permute-start | bytes 147464 | tf_op jit(solution)/shard_map/ppermute | solution.py:421
  5.3 2.1 %collective-permute-start.2 = (f32[3,8,4,128]{3,2,1,0:T(4,128)S(1)}, f32[3,8,4,128]{3,2,1,0:T(4,128)S(1)}, u32[]{:S(2)}, u32[]{:S(2)}) collective-permute-start(f32[3,8,4,128]{3,2,1,0:T(4,128)S(1)} %get-tuple-element.29), channel_id=1, source_target_pairs={{0,1},{4,8},{8,4},{12,13},{1,0},{5,9},{9,5},{13,12},{2,3},{6,10},{... | collective-permute-start | bytes 147464 | tf_op jit(solution)/shard_map/ppermute | solution.py:420
  5.3 4.7 %collective-permute-start = (f32[1,3,3,4,512]{4,3,2,1,0:T(4,128)S(1)}, f32[1,3,3,4,512]{4,3,2,1,0:T(4,128)S(1)}, u32[]{:S(2)}, u32[]{:S(2)}) collective-permute-start(f32[1,3,3,4,512]{4,3,2,1,0:T(4,128)S(1)} %bitcast.15), channel_id=1, source_target_pairs={{0,16},{16,0},{1,17},{17,1},{2,18},{18,2},{3,19},{19,3},{4,20},{20... | collective-permute-start | bytes 221192 | tf_op jit(solution)/shard_map/ppermute | solution.py:400
  12.4 13.3 %all-to-all-start = ((f32[32,8,128]{2,1,0:T(8,128)}), f32[32,8,128]{2,1,0:T(8,128)S(1)}, u32[]{:S(2)}, u32[]{:S(2)}) async-start(f32[32,8,128]{2,1,0:T(8,128)} %bitcast.3), calls=%async_computation | async-start | bytes 262144 | tf_op jit(solution)/shard_map/all_to_all | solution.py:429
  17.5 4.8 %collective-permute-start.3 = (f32[3,5,8,128]{3,2,1,0:T(8,128)S(1)}, f32[3,5,8,128]{3,2,1,0:T(8,128)S(1)}, u32[]{:S(2)}, u32[]{:S(2)}) collective-permute-start(f32[3,5,8,128]{3,2,1,0:T(8,128)S(1)} %pad_maximum_fusion.1), channel_id=1, source_target_pairs={{0,16},{16,0},{1,17},{17,1},{2,18},{18,2},{3,19},{19,3},{4,20},{20... | collective-permute-start | bytes 184328 | tf_op jit(solution)/shard_map/ppermute | solution.py:442

commit v9 on v8

--- a/solution.py
+++ b/solution.py
@@ -26,7 +26,7 @@
 
 
 def spectrum_kernel(pair, count, contrast_in, field_in, class_in, kind_in, source_in, library_in,
-                    hartley, spectrum, columns, pick, weights, source, library, send_a, send_b,
+                    hartley, spectrum, columns, pick, weights, source, library, send_a, send_b, faces,
                     polar, field, classes, kinds, plain_source, contrast, sems):
     rows = contrast.shape[0]
     slabs = source.shape[1]
@@ -78,9 +78,20 @@
             source[c, p] = value
             send_a[c, p] = jnp.where(even, value[4:], value[:4])
             send_b[c, p] = jnp.where(even, value[:4], value[4:])
-
-
-def solve_kernel(weights, columns, spectrum, hartley, pick, library, other, source, tiles, bundle,
+    place = lax.broadcasted_iota(jnp.int32, (8, 128), 1)
+    low = jnp.zeros((8, 128), jnp.float32)
+    high = jnp.zeros((8, 128), jnp.float32)
+    for s in range(3 * slabs):
+        value = source[s // slabs, s % slabs]
+        here = (place >= 3 * s) & (place < 3 * s + 3)
+        low = jnp.where(here, pltpu.roll(value, (3 * s) % 128, 1) if s else value, low)
+        high = jnp.where(here, pltpu.roll(value, (3 * s + 3) % 128, 1), high)
+    mirrored = jnp.minimum(place + 2 - 2 * (place % 3), 127)
+    faces[0] = jnp.take_along_axis(low, mirrored, axis=1)
+    faces[1] = jnp.take_along_axis(high, mirrored, axis=1)
+
+
+def solve_kernel(slabs, weights, columns, spectrum, hartley, pick, library, other, faces, tiles, bundle,
                  mixing, stacked, product):
     rows = weights.shape[0]
     zb = rows // 8
@@ -145,20 +156,13 @@
     tallest, lowest = product[0:8, 128:256], product[0:8, 256:384]
 
     place = lax.broadcasted_iota(jnp.int32, (8, 128), 1)
-    low = jnp.zeros((8, 128), jnp.float32)
-    high = jnp.zeros((8, 128), jnp.float32)
-    slabs = source.shape[1]
-    for s in range(3 * slabs + 1):
-        if s < 3 * slabs:
-            value = source[s // slabs, s % slabs] - tiles[s // slabs]
-        else:
-            value = tiles[3]
-        here = (place >= 3 * s) & (place < 3 * s + 3)
-        low = jnp.where(here, pltpu.roll(value, (3 * s) % 128, 1) if s else value, low)
-        high = jnp.where(here, pltpu.roll(value, (3 * s + 3) % 128, 1), high)
-    mirrored = jnp.minimum(place + 2 - 2 * (place % 3), 127)
-    low = jnp.take_along_axis(low, mirrored, axis=1)
-    high = jnp.take_along_axis(high, mirrored, axis=1)
+    width = 3 * slabs
+    sides = []
+    for k, at in enumerate((0, 127)):
+        edge = [jnp.broadcast_to(tiles[t][:, at : at + 1], (8, 128)) for t in range(4)]
+        constant = jnp.where(place < width, edge[0], jnp.where(place < 2 * width, edge[1], edge[2]))
+        sides.append(jnp.where(place < 3 * width, faces[k] - constant, edge[3]))
+    low, high = sides
     for d in range(bundle.shape[1]):
         zero = jnp.zeros((8, 128), jnp.float32)
         tile = jnp.where(gz == d, compact, jnp.where(gz + 1 == d, high, jnp.where(gz - 1 == d, low, zero)))
@@ -401,10 +405,11 @@
     else:
         other = lax.all_gather(library, "gx", axis=0, tiled=True)
     count = TYPES * nx
-    hartley, spectrum, columns, pick, weights, source, library, send_a, send_b = call(
+    hartley, spectrum, columns, pick, weights, source, library, send_a, send_b, faces = call(
         functools.partial(spectrum_kernel, pair, count),
         [((VOX, VOX), bf16), ((3 * rows, VOX), f32), ((rows, 8), f32), ((rows, 2 * count), bf16),
-         (contrast.shape, f32), field, (library.shape, f32), ((3, slabs, 4, 128), f32), ((3, slabs, 4, 128), f32)],
+         (contrast.shape, f32), field, (library.shape, f32), ((3, slabs, 4, 128), f32), ((3, slabs, 4, 128), f32),
+         ((2, 8, 128), f32)],
         (contrast, point_field, point_class.reshape(1, rows), cell_kind.reshape(1, rows), source, library),
         [pltpu.VMEM((3 * rows, VOX), bf16), pltpu.VMEM((3, rows), bf16), pltpu.VMEM((1, rows), jnp.int32),
          pltpu.VMEM((1, rows), jnp.int32), pltpu.VMEM(*field), pltpu.VMEM(contrast.shape, bf16), pltpu.SemaphoreType.DMA((6,))],
@@ -420,9 +425,9 @@
     yb = lax.ppermute(send_b, ("gy", "gz"), couples)
     ya = lax.ppermute(send_a, "gy", pairs_from(0, ny))
     tiles, bundle = call(
-        solve_kernel,
+        functools.partial(solve_kernel, slabs),
         [((4, 8, 128), f32), ((nx * ny if dense else 1, nz, 8, 128), f32)],
-        (weights, columns, spectrum, hartley, pick, library if pair else other, other, source),
+        (weights, columns, spectrum, hartley, pick, library if pair else other, other, faces),
         [pltpu.VMEM((9, rows, VOX), f32), pltpu.VMEM((3 * rows, VOX), bf16), pltpu.VMEM((3 * rows, VOX), f32)],
     )
     if dense:

time: 36.8 us -> 36.9 us (level)
  no operation moved by 1% of the time
where the time goes in v9:
time: 36.9 us; the launch traced here: 36.7 us
  starting transfers between devices  11.5 us (31%)
  waiting for transfers between devices  9.46 us (26%)
  blocking collectives  9.12 us (25%)
  Pallas kernels  5.79 us (16%)
  between operations  0.69 us (2%)
    all_to_all x1, blocking collectives, whole_step(): parts = lax.all_to_all(moments, AXES, 0, 0)  9.12 us
    pallas_call x4, Pallas kernels, call(): pl.pallas_call(body, out_shape=tuple((shape(s, d) for s, d in outs)), in_...  5.79 us
    all_to_all x1, starting transfers between devices, whole_step(): lax.all_to_all(bundle.reshape(devices, 8, 128), AXES, 0, 0)  5.08 us
    all_to_all x1, waiting for transfers between devices, whole_step(): lax.all_to_all(bundle.reshape(devices, 8, 128), AXES, 0, 0)  3.35 us
    ppermute x1, starting transfers between devices, whole_step(): ya = lax.ppermute(send_a, 'gy', pairs_from(0, ny))  3.12 us
    ppermute x1, waiting for transfers between devices, whole_step(): xlow = xhigh = lax.ppermute(high, 'gx', swap)  2.95 us
    ppermute x1, waiting for transfers between devices, whole_step(): other = lax.ppermute(library, 'gx', swap)  2.6 us
    ppermute x1, starting transfers between devices, whole_step(): xlow = xhigh = lax.ppermute(high, 'gx', swap)  1.83 us
  transfers between devices with their start and end apart: 5, of which 4 were waited for; matrix products, arithmetic and copies ran while one was open for 0% of the time, Pallas kernels for 0%

profile of v9, /device:TPU:0, one launch (start us, length us, event | category | flops | bytes accessed | tf_op | source)
XLA Modules:
  0.0 36.7 jit_solution(4625084830108147660)
XLA Ops:
  0.6 0.0 copy-start
  0.6 1.7 %shard_map.77 = (bf16[512,512]{1,0:T(8,128)(2,1)S(1)}, f32[384,512]{1,0:T(8,128)S(1)}, f32[128,8]{1,0:T(8,128)S(1)}, bf16[128,16]{1,0:T(8,128)(2,1)S(1)}, f32[12...) custom-call(bf16[128,1536]{1,0:T(8,128)(2,1)} %contrast_in.1, ...), custom_call_target="tpu_custom_call" | custom-call | tf_op jit(solution)/shard_map/pallas_call | solution.py:363
  2.4 3.1 %collective-permute-start.1 = (f32[3,8,4,128]{3,2,1,0:T(4,128)S(1)}, f32[3,8,4,128]{3,2,1,0:T(4,128)S(1)}, u32[]{:S(2)}, u32[]{:S(2)}) collective-permute-start(f32[3,8,4,128]{3,2,1,0:T(4,128)S(1)} %get-tuple-element.30), channel_id=1, source_target_pairs={{0,4},{8,12},{4,0},{12,8},{1,5},{9,13},{5,1},{13,9},{2,6},{10,14},... | collective-permute-start | bytes 147464 | tf_op jit(solution)/shard_map/ppermute | solution.py:426
  5.5 0.0 collective-permute-start.2
  5.5 0.0 copy-done
  5.5 1.5 %collective-permute-start = (f32[1,3,3,4,512]{4,3,2,1,0:T(4,128)S(1)}, f32[1,3,3,4,512]{4,3,2,1,0:T(4,128)S(1)}, u32[]{:S(2)}, u32[]{:S(2)}) collective-permute-start(f32[1,3,3,4,512]{4,3,2,1,0:T(4,128)S(1)} %bitcast.15), channel_id=1, source_target_pairs={{0,16},{16,0},{1,17},{17,1},{2,18},{18,2},{3,19},{19,3},{4,20},{20... | collective-permute-start | bytes 221192 | tf_op jit(solution)/shard_map/ppermute | solution.py:404
  7.0 0.6 %collective-permute-done.1 = f32[3,8,4,128]{3,2,1,0:T(4,128)S(1)} collective-permute-done((f32[3,8,4,128]{3,2,1,0:T(4,128)S(1)}, f32[3,8,4,128]{3,2,1,0:T(4,128)S(1)}, u32[]{:S(2)}, u32[]{:S(2)}) %collective-permute-start.1) | collective-permute-done | bytes 49184 | tf_op jit(solution)/shard_map/ppermute | solution.py:426
  7.6 0.0 collective-permute-done.2
  7.6 2.6 %collective-permute-done.other = f32[1,3,3,4,512]{4,3,2,1,0:T(4,128)S(1)} collective-permute-done((f32[1,3,3,4,512]{4,3,2,1,0:T(4,128)S(1)}, f32[1,3,3,4,512]{4,3,2,1,0:T(4,128)S(1)}, u32[]{:S(2)}, u32[]{:S(2)}) %collective-permute-start) | collective-permute-done | bytes 73760 | tf_op jit(solution)/shard_map/ppermute | solution.py:404
  10.2 2.3 %shard_map.78 = (f32[4,8,128]{2,1,0:T(8,128)S(1)}, f32[8,4,8,128]{3,2,1,0:T(8,128)}) custom-call(f32[128,1536]{1,0:T(8,128)S(1)} %get-tuple-element.20.weights, f32[128,8]{1,0:T(8,128)S(1)} %get-tuple-element.21.columns, f32[384,512]{1,0:T(8,128)S(1)} %get-tuple-element.22.spectrum, bf16[512,512]{1,0:T(8,128)(2,1)S(1)} %get-tuple-element.23.hartley, ...), custom_call_target="tpu_custom_call" | custom-call | tf_op jit(solution)/shard_map/pallas_call | solution.py:363
  12.5 5.1 %all-to-all-start = ((f32[32,8,128]{2,1,0:T(8,128)}), f32[32,8,128]{2,1,0:T(8,128)S(1)}, u32[]{:S(2)}, u32[]{:S(2)}) async-start(f32[32,8,128]{2,1,0:T(8,128)} %bitcast.3), calls=%async_computation | async-start | bytes 262144 | tf_op jit(solution)/shard_map/all_to_all | solution.py:434
  17.6 1.8 %collective-permute-start.3 = (f32[3,5,8,128]{3,2,1,0:T(8,128)S(1)}, f32[3,5,8,128]{3,2,1,0:T(8,128)S(1)}, u32[]{:S(2)}, u32[]{:S(2)}) collective-permute-start(f32[3,5,8,128]{3,2,1,0:T(8,128)S(1)} %pad_maximum_fusion.1), channel_id=1, source_target_pairs={{0,16},{16,0},{1,17},{17,1},{2,18},{18,2},{3,19},{19,3},{4,20},{20... | collective-permute-start | bytes 184328 | tf_op jit(solution)/shard_map/ppermute | solution.py:447
  19.5 2.9 %collective-permute-done.3.xlow.xhigh = f32[3,5,8,128]{3,2,1,0:T(8,128)S(1)} collective-permute-done((f32[3,5,8,128]{3,2,1,0:T(8,128)S(1)}, f32[3,5,8,128]{3,2,1,0:T(8,128)S(1)}, u32[]{:S(2)}, u32[]{:S(2)}) %collective-permute-start.3) | collective-permute-done | bytes 61472 | tf_op jit(solution)/shard_map/ppermute | solution.py:447
  22.4 3.4 %all-to-all-done = f32[32,8,128]{2,1,0:T(8,128)S(1)} async-done(((f32[32,8,128]{2,1,0:T(8,128)}), f32[32,8,128]{2,1,0:T(8,128)S(1)}, u32[]{:S(2)}, u32[]{:S(2)}) %all-to-all-start) | async-done | bytes 131104 | tf_op jit(solution)/shard_map/all_to_all | solution.py:434
  25.8 0.9 %shard_map.79 = (f32[3,8,8,128]{3,2,1,0:T(8,128)S(1)}, f32[3,8,8,128]{3,2,1,0:T(8,128)S(1)}, f32[3,8,8,128]{3,2,1,0:T(8,128)S(1)}, f32[3,8,8,128]{3,2,1,0:T(8,12...) custom-call(f32[4,8,128]{2,1,0:T(8,128)S(1)} %get-tuple-element.27.tiles, f32[2,4,4,8,128]{4,3,2,1,0:T(8,128)S(1)} %bitcast.9, ...), custom_call_target="tpu_custom_call" | custom-call | tf_op jit(solution)/shard_map/pallas_call | solution.py:363
  26.6 9.1 %all_to_all.10.parts = f32[32,1,128]{2,1,0:T(1,128)S(1)} all-to-all(f32[32,1,128]{2,1,0:T(1,128)S(1)} %get-tuple-element.32), channel_id=1, replica_groups=mesh['gx'=2,'gy'=4,'gz'=4] {'gx','gy','gz'}, dimensions={0} | all-to-all | bytes 32768 | tf_op jit(solution)/shard_map/all_to_all | solution.py:457
  35.7 0.9 %shard_map.80 = (f32[3,8,8,128]{3,2,1,0:T(8,128)}, f32[3,8,8,128]{3,2,1,0:T(8,128)}) custom-call(f32[32,1,128]{2,1,0:T(1,128)S(1)} %all_to_all.10.parts, f32[1,128]{1,0:T(1,128)S(1)} %get-tuple-element.33.scale, f32[3,8,8,128]{3,2,1,0:T(8,128)S(1)} %get-tuple-element.34.v0, f32[3,8,8,128]{3,2,1,0:T(8,128)S(1)} %get-tuple-element.35.v1, ...), custom_call_target="tpu_custom_call" | custom-call | tf_op jit(solution)/shard_map/pallas_call | solution.py:363
  (7 shorter events, 0.1 us)
Async XLA Ops:
  0.6 4.9 %copy-start = (f32[1,4,3,3,512]{4,1,3,2,0:T(4,128)S(1)}, f32[1,4,3,3,512]{4,1,3,2,0:T(4,128)}, u32[]{:S(2)}) copy-start(f32[1,4,3,3,512]{4,1,3,2,0:T(4,128)} %param.11) | copy-start | bytes 221188
  2.4 5.2 %collective-permute-start.1 = (f32[3,8,4,128]{3,2,1,0:T(4,128)S(1)}, f32[3,8,4,128]{3,2,1,0:T(4,128)S(1)}, u32[]{:S(2)}, u32[]{:S(2)}) collective-permute-start(f32[3,8,4,128]{3,2,1,0:T(4,128)S(1)} %get-tuple-element.30), channel_id=1, source_target_pairs={{0,4},{8,12},{4,0},{12,8},{1,5},{9,13},{5,1},{13,9},{2,6},{10,14},... | collective-permute-start | bytes 147464 | tf_op jit(solution)/shard_map/ppermute | solution.py:426
  5.5 2.1 %collective-permute-start.2 = (f32[3,8,4,128]{3,2,1,0:T(4,128)S(1)}, f32[3,8,4,128]{3,2,1,0:T(4,128)S(1)}, u32[]{:S(2)}, u32[]{:S(2)}) collective-permute-start(f32[3,8,4,128]{3,2,1,0:T(4,128)S(1)} %get-tuple-element.31), channel_id=1, source_target_pairs={{0,1},{4,8},{8,4},{12,13},{1,0},{5,9},{9,5},{13,12},{2,3},{6,10},{... | collective-permute-start | bytes 147464 | tf_op jit(solution)/shard_map/ppermute | solution.py:425
  5.5 4.7 %collective-permute-start = (f32[1,3,3,4,512]{4,3,2,1,0:T(4,128)S(1)}, f32[1,3,3,4,512]{4,3,2,1,0:T(4,128)S(1)}, u32[]{:S(2)}, u32[]{:S(2)}) collective-permute-start(f32[1,3,3,4,512]{4,3,2,1,0:T(4,128)S(1)} %bitcast.15), channel_id=1, source_target_pairs={{0,16},{16,0},{1,17},{17,1},{2,18},{18,2},{3,19},{19,3},{4,20},{20... | collective-permute-start | bytes 221192 | tf_op jit(solution)/shard_map/ppermute | solution.py:404
  12.5 13.3 %all-to-all-start = ((f32[32,8,128]{2,1,0:T(8,128)}), f32[32,8,128]{2,1,0:T(8,128)S(1)}, u32[]{:S(2)}, u32[]{:S(2)}) async-start(f32[32,8,128]{2,1,0:T(8,128)} %bitcast.3), calls=%async_computation | async-start | bytes 262144 | tf_op jit(solution)/shard_map/all_to_all | solution.py:434
  17.6 4.8 %collective-permute-start.3 = (f32[3,5,8,128]{3,2,1,0:T(8,128)S(1)}, f32[3,5,8,128]{3,2,1,0:T(8,128)S(1)}, u32[]{:S(2)}, u32[]{:S(2)}) collective-permute-start(f32[3,5,8,128]{3,2,1,0:T(8,128)S(1)} %pad_maximum_fusion.1), channel_id=1, source_target_pairs={{0,16},{16,0},{1,17},{17,1},{2,18},{18,2},{3,19},{19,3},{4,20},{20... | collective-permute-start | bytes 184328 | tf_op jit(solution)/shard_map/ppermute | solution.py:447
